TPU v7x, 512 devices: a whole 4x4x16 slice. The times are simulated.
512 devices in a mesh: seq: 64 (over y, z), piece: 8 (over x, core).
Axes of the slice: x: 4, y: 4, z: 16, core: 2. Of those that a mesh axis runs over, the one named last changes fastest.
Arguments:
- query: bfloat16 [8192, 2048], P('seq', 'piece'), may hold values from -64 to 64
- key_rows: bfloat16 [8192, 2048], P('seq', 'piece'), may hold values from -64 to 64
- value_matrix_rows: bfloat16 [8192, 2048], P('seq', 'piece'), may hold values from -6 to 6
- grad_out: bfloat16 [8192, 2048], P('seq', 'piece'), may hold values from -6 to 6
- rel_embed: bfloat16 [512, 64], replicated, may hold values from -6 to 6
Outputs:
- grad_query: bfloat16 [8192, 2048], P('seq', 'piece')
- grad_key: bfloat16 [8192, 2048], P('seq', 'piece')
- grad_value: bfloat16 [8192, 2048], P('seq', 'piece')
- grad_embed: float32 [512, 64], replicated
All inputs are finite; a program needn't handle non-finite values.
Results may differ from a plain program's by a relative error of at most 0.0086.
Values may be sent and summed in bfloat16 or wider, within the bound.
No kernel may reach another device: no remote copies, remote signals or barrier semaphores. Data moves between devices by JAX's collectives and lax.ppermute only.
A program may use at most 64 MiB of HBM per device.

v0:
```python
import jax
import jax.numpy as jnp
from jax import lax
from jax.sharding import PartitionSpec as P

HEAD_DIM = 64
BAND_EXTENT = 512


def shifted(value, axis, steps):
    count = lax.axis_size(axis)
    leading, last = (max(0, -steps), min(count, count - steps))
    return lax.ppermute(value, axis, [(source, source + steps) for source in range(leading, last)])


def skew_rel(along):
    head_count, row_tiles, cols = along.shape
    padded = jnp.pad(along, ((0, 0), (0, 0), (0, row_tiles)))
    flat = padded.reshape(head_count, row_tiles * (cols + row_tiles))[
        :, : row_tiles * (cols + row_tiles - 1)
    ]
    return flat.reshape(head_count, row_tiles, cols + row_tiles - 1)[
        :, :, row_tiles : 2 * row_tiles
    ]


def unskew_rel(dscore, cols):
    zeros = jnp.zeros(dscore.shape[:2] + (cols,), dscore.dtype)
    _, pull = jax.vjp(skew_rel, zeros)
    return pull(dscore)[0]


def embed_slice(emb_pad, offset, row_tiles):
    return emb_pad[offset + 1 : offset + 2 * row_tiles + 1][::-1]


def masked_scores(query, keys, slab, offset, present, scale):
    row_tiles = query.shape[0]
    direct = jnp.einsum("thd,shd->hts", query, keys, preferred_element_type=jnp.float32)
    along = jnp.einsum("thd,rd->htr", query, slab, preferred_element_type=jnp.float32)
    score = scale * (direct + skew_rel(along))
    qpos = lax.broadcasted_iota(jnp.int32, (row_tiles, row_tiles), 0)
    kpos = lax.broadcasted_iota(jnp.int32, (row_tiles, row_tiles), 1)
    dist = offset + qpos - kpos
    valid = (dist >= 0) & (dist < BAND_EXTENT) & present
    return jnp.where(valid[None], score, -jnp.inf)


def pair_grads(prob, query, value_tensor, dout, delta, scale):
    prob_b = prob.astype(jnp.bfloat16)
    dprob = jnp.einsum("thd,shd->hts", dout, value_tensor, preferred_element_type=jnp.float32)
    dscore = (prob * (dprob - delta[:, :, None]) * scale).astype(jnp.bfloat16)
    gkey = jnp.einsum("hts,thd->shd", dscore, query, preferred_element_type=jnp.float32)
    gvalue = jnp.einsum("hts,thd->shd", prob_b, dout, preferred_element_type=jnp.float32)
    return (dscore, gkey, gvalue)


def query_terms(dscore, keys, slab, query):
    dalong = unskew_rel(dscore, slab.shape[0])
    gquery = jnp.einsum("hts,shd->thd", dscore, keys, preferred_element_type=jnp.float32)
    gquery = gquery + jnp.einsum("htr,rd->thd", dalong, slab, preferred_element_type=jnp.float32)
    gembed = jnp.einsum("htr,thd->rd", dalong, query, preferred_element_type=jnp.float32)
    return (gquery, gembed)


def local(query, key_rows, value_matrix_rows, grad_out, rel_embed):
    row_tiles = query.shape[0]
    width = query.shape[1]
    head_feature_width = HEAD_DIM
    head_count = width // head_feature_width
    scale = head_feature_width ** (-0.5)
    reach = BAND_EXTENT // row_tiles
    here = lax.axis_index("seq")
    qh = query.reshape(row_tiles, head_count, head_feature_width)
    kh = key_rows.reshape(row_tiles, head_count, head_feature_width)
    vh = value_matrix_rows.reshape(row_tiles, head_count, head_feature_width)
    doh = grad_out.reshape(row_tiles, head_count, head_feature_width)
    emb_pad = jnp.pad(rel_embed, ((row_tiles, row_tiles + 1), (0, 0)))
    slabs = [embed_slice(emb_pad, step * row_tiles, row_tiles) for step in range(reach + 1)]
    windows = [(kh, vh)]
    for step in range(1, reach + 1):
        windows.append(shifted((kh, vh), "seq", step))
    scores = [
        masked_scores(qh, windows[step][0], slabs[step], step * row_tiles, here >= step, scale)
        for step in range(reach + 1)
    ]
    top = scores[0].max(axis=2)
    for score in scores[1:]:
        top = jnp.maximum(top, score.max(axis=2))
    total = jnp.zeros_like(top)
    for score in scores:
        total = total + jnp.exp(score - top[:, :, None]).sum(axis=2)
    lse = top + jnp.log(total)
    probs = [jnp.exp(score - lse[:, :, None]) for score in scores]
    attn_out = jnp.zeros((row_tiles, head_count, head_feature_width), jnp.float32)
    for step in range(reach + 1):
        attn_out = attn_out + jnp.einsum(
            "hts,shd->thd",
            probs[step].astype(jnp.bfloat16),
            windows[step][1],
            preferred_element_type=jnp.float32,
        )
    delta = jnp.sum(doh.astype(jnp.float32) * attn_out, axis=2).T
    grad_q = jnp.zeros((row_tiles, head_count, head_feature_width), jnp.float32)
    emb_grad = jnp.zeros(emb_pad.shape, jnp.float32)
    key_parts = []
    value_parts = []
    for step in range(reach + 1):
        dscore, gkey, gvalue = pair_grads(probs[step], qh, windows[step][1], doh, delta, scale)
        gquery, gembed = query_terms(dscore, windows[step][0], slabs[step], qh)
        grad_q = grad_q + gquery
        offset = step * row_tiles
        emb_grad = emb_grad.at[offset + 1 : offset + 2 * row_tiles + 1].add(gembed[::-1])
        key_parts.append(gkey)
        value_parts.append(gvalue)
    grad_k = key_parts[0]
    grad_v = value_parts[0]
    for step in range(1, reach + 1):
        back_k, back_v = shifted((key_parts[step], value_parts[step]), "seq", -step)
        grad_k = grad_k + back_k
        grad_v = grad_v + back_v
    local_embed = emb_grad[row_tiles : row_tiles + BAND_EXTENT]
    grad_embed = lax.psum(local_embed, ("seq", "piece"))
    grad_query = grad_q.reshape(row_tiles, width).astype(jnp.bfloat16)
    grad_key = grad_k.reshape(row_tiles, width).astype(jnp.bfloat16)
    grad_value = grad_v.reshape(row_tiles, width).astype(jnp.bfloat16)
    return (grad_query, grad_key, grad_value, grad_embed)


def solution(mesh):
    placed = (P("seq", "piece"), P("seq", "piece"), P("seq", "piece"), P("seq", "piece"), P())
    return jax.shard_map(
        local,
        mesh=mesh,
        in_specs=placed,
        out_specs=(P("seq", "piece"), P("seq", "piece"), P("seq", "piece"), P()),
        check_vma=False,
    )
```

profile of v0, /device:TPU:1, one launch (start us, length us, event | category | flops | bytes accessed | tf_op | source)
XLA Modules:
  0.0 609.0 jit_solution(11147221646708670581)
XLA Ops:
  7.2 1.6 copy.73
  8.8 10.4 %collective-permute-start.7 = (bf16[128,4,64]{0,2,1:T(8,128)(2,1)}, bf16[128,4,64]{0,2,1:T(8,128)(2,1)}, u32[]{:S(2)}, u32[]{:S(2)}) collective-permute-start(bf16[128,4,64]{0,2,1:T(8,128)(2,1)} %bitcast.13), channel_id=1, source_target_pairs={{0,32},{8,40},{16,48},{24,56},{32,64},{40,72},{48,80},{56,88},{64,... | collective-permute-start | bytes 196616 | tf_op jit(solution)/shard_map/ppermute | solution.py:13
  19.2 6.9 %collective-permute-start.6 = (bf16[128,4,64]{0,2,1:T(8,128)(2,1)}, bf16[128,4,64]{0,2,1:T(8,128)(2,1)}, u32[]{:S(2)}, u32[]{:S(2)}) collective-permute-start(bf16[128,4,64]{0,2,1:T(8,128)(2,1)} %bitcast.13), channel_id=1, source_target_pairs={{0,24},{8,32},{16,40},{24,48},{32,56},{40,64},{48,72},{56,80},{64,... | collective-permute-start | bytes 196616 | tf_op jit(solution)/shard_map/ppermute | solution.py:13
  26.0 5.2 collective-permute-start.5
  31.2 2.7 collective-permute-start.4
  34.6 2.5 collective-permute-start.1
  39.2 0.8 rev.31
  40.0 0.8 rev.33
  43.3 0.9 reshape.329
  47.1 1.0 copy.138
  50.0 1.7 fusion.115
  51.7 1.0 copy.72
  53.3 1.8 reshape.333
  55.1 0.9 slice-done
  56.0 0.8 copy.134
  57.4 0.9 reshape.337
  59.1 0.9 reshape.335
  60.8 0.9 reshape.331
  61.9 2.7 collective-permute-start.3
  64.6 1.1 fusion.114
  66.2 2.2 collective-permute-start.2
  68.7 2.5 collective-permute-done.2
  71.2 6.6 %collective-permute-start = (bf16[128,4,64]{0,2,1:T(8,128)(2,1)}, bf16[128,4,64]{0,2,1:T(8,128)(2,1)S(1)}, u32[]{:S(2)}, u32[]{:S(2)}) collective-permute-start(bf16[128,4,64]{0,2,1:T(8,128)(2,1)} %bitcast.1), channel_id=1, source_target_pairs={{0,8},{8,16},{16,24},{24,32},{32,40},{40,48},{48,56},{56,64},{64,7... | collective-permute-start | bytes 196616 | tf_op jit(solution)/shard_map/ppermute | solution.py:13
  78.0 1.2 collective-permute-done
  80.9 1.0 fusion.99
  82.0 1.0 convolution_add_fusion.8
  83.2 1.0 fusion.92
  84.2 1.0 fusion.89
  85.3 1.0 fusion.49
  86.3 1.1 fusion.20
  87.4 1.1 fusion.24
  88.5 0.9 convolution_bitcast_fusion.13
  89.5 1.1 fusion.23
  90.6 0.8 convolution_bitcast_fusion.14
  91.5 1.1 fusion.21
  92.6 0.9 convolution_bitcast_fusion.16
  93.7 0.8 reshape.342
  95.6 1.1 fusion.22
  96.9 0.8 reshape.344
  99.0 0.8 reshape.346
  101.0 0.8 reshape.348
  103.1 0.8 reshape.340
  105.1 1.3 collective-permute-start.8
  106.4 1.3 collective-permute-start.15
  107.7 1.3 collective-permute-start.14
  109.0 1.3 collective-permute-start.13
  110.3 1.3 collective-permute-start.12
  112.3 1.0 fusion.29
  113.5 1.0 fusion.27
  115.0 0.7 copy.104
  115.8 0.8 scatter-add.19
  116.7 0.8 scatter-add.20
  117.7 0.8 scatter-add.21
  120.2 3.2 collective-permute-done.15
  123.4 1.3 collective-permute-start.9
  124.7 1.3 collective-permute-start.10
  126.0 1.3 collective-permute-start.11
  127.4 1.2 fusion.47
  128.6 6.1 %collective-permute-done.9 = f32[128,4,64]{0,2,1:T(8,128)S(1)} collective-permute-done((f32[128,4,64]{0,2,1:T(8,128)S(1)}, f32[128,4,64]{0,2,1:T(8,128)S(1)}, u32[]{:S(2)}, u32[]{:S(2)}) %collective-permute-start.9) | collective-permute-done | bytes 131104 | tf_op jit(solution)/shard_map/ppermute | solution.py:13
  134.7 11.8 %collective-permute-done.10 = f32[128,4,64]{0,2,1:T(8,128)S(1)} collective-permute-done((f32[128,4,64]{0,2,1:T(8,128)S(1)}, f32[128,4,64]{0,2,1:T(8,128)S(1)}, u32[]{:S(2)}, u32[]{:S(2)}) %collective-permute-start.10) | collective-permute-done | bytes 131104 | tf_op jit(solution)/shard_map/ppermute | solution.py:13
  146.6 17.2 %collective-permute-done.11 = f32[128,4,64]{0,2,1:T(8,128)S(1)} collective-permute-done((f32[128,4,64]{0,2,1:T(8,128)S(1)}, f32[128,4,64]{0,2,1:T(8,128)S(1)}, u32[]{:S(2)}, u32[]{:S(2)}) %collective-permute-start.11) | collective-permute-done | bytes 131104 | tf_op jit(solution)/shard_map/ppermute | solution.py:13
  163.8 1.1 fusion.48
  166.4 434.2 %all-reduce.19.cloned.1.call-done = f32[512,64]{0,1:T(8,128)} async-done(((f32[512,64]{0,1:T(8,128)}), f32[512,64]{0,1:T(8,128)}) %all-reduce.19.cloned.1.call-update) | async-done | bytes 131088 | tf_op jit(solution)/shard_map/psum | solution.py:123
  600.6 1.6 copy.172
  (164 shorter events, 27.1 us)
Async XLA Ops:
  7.2 26.7 %copy-start.15 = (bf16[128,256]{1,0:T(8,128)(2,1)S(1)}, bf16[128,256]{1,0:T(8,128)(2,1)}, u32[]{:S(2)}) copy-start(bf16[128,256]{1,0:T(8,128)(2,1)} %param.16) | copy-start | bytes 196612
  7.2 593.4 %all-reduce.19.cloned.1.call-start = ((), (), s32[]{:S(2)}) async-start(), calls=%async_computation | async-start | bytes 262144 | tf_op jit(solution)/shard_map/psum | solution.py:123
  8.8 29.5 %copy-start.16 = (bf16[128,256]{1,0:T(8,128)(2,1)S(1)}, bf16[128,256]{1,0:T(8,128)(2,1)}, u32[]{:S(2)}) copy-start(bf16[128,256]{1,0:T(8,128)(2,1)} %param.15) | copy-start | bytes 196612
  8.8 75.4 %collective-permute-start.7 = (bf16[128,4,64]{0,2,1:T(8,128)(2,1)}, bf16[128,4,64]{0,2,1:T(8,128)(2,1)}, u32[]{:S(2)}, u32[]{:S(2)}) collective-permute-start(bf16[128,4,64]{0,2,1:T(8,128)(2,1)} %bitcast.13), channel_id=1, source_target_pairs={{0,32},{8,40},{16,48},{24,56},{32,64},{40,72},{48,80},{56,88},{64,... | collective-permute-start | bytes 196616 | tf_op jit(solution)/shard_map/ppermute | solution.py:13
  19.2 64.0 %collective-permute-start.6 = (bf16[128,4,64]{0,2,1:T(8,128)(2,1)}, bf16[128,4,64]{0,2,1:T(8,128)(2,1)}, u32[]{:S(2)}, u32[]{:S(2)}) collective-permute-start(bf16[128,4,64]{0,2,1:T(8,128)(2,1)} %bitcast.13), channel_id=1, source_target_pairs={{0,24},{8,32},{16,40},{24,48},{32,56},{40,64},{48,72},{56,80},{64,... | collective-permute-start | bytes 196616 | tf_op jit(solution)/shard_map/ppermute | solution.py:13
  26.0 59.2 %collective-permute-start.5 = (bf16[128,4,64]{0,2,1:T(8,128)(2,1)}, bf16[128,4,64]{0,2,1:T(8,128)(2,1)}, u32[]{:S(2)}, u32[]{:S(2)}) collective-permute-start(bf16[128,4,64]{0,2,1:T(8,128)(2,1)} %bitcast.13), channel_id=1, source_target_pairs={{0,16},{8,24},{16,32},{24,40},{32,48},{40,56},{48,64},{56,72},{64,... | collective-permute-start | bytes 196616 | tf_op jit(solution)/shard_map/ppermute | solution.py:13
  31.2 50.7 %collective-permute-start.4 = (bf16[128,4,64]{0,2,1:T(8,128)(2,1)}, bf16[128,4,64]{0,2,1:T(8,128)(2,1)}, u32[]{:S(2)}, u32[]{:S(2)}) collective-permute-start(bf16[128,4,64]{0,2,1:T(8,128)(2,1)} %bitcast.13), channel_id=1, source_target_pairs={{0,8},{8,16},{16,24},{24,32},{32,40},{40,48},{48,56},{56,64},{64,7... | collective-permute-start | bytes 196616 | tf_op jit(solution)/shard_map/ppermute | solution.py:13
  34.6 27.2 %collective-permute-start.1 = (bf16[128,4,64]{0,2,1:T(8,128)(2,1)}, bf16[128,4,64]{0,2,1:T(8,128)(2,1)}, u32[]{:S(2)}, u32[]{:S(2)}) collective-permute-start(bf16[128,4,64]{0,2,1:T(8,128)(2,1)} %bitcast.1), channel_id=1, source_target_pairs={{0,16},{8,24},{16,32},{24,40},{32,48},{40,56},{48,64},{56,72},{64,... | collective-permute-start | bytes 196616 | tf_op jit(solution)/shard_map/ppermute | solution.py:13
  38.3 0.8 copy-start.12
  40.9 3.4 copy-start.4
  41.1 1.1 copy-start.2
  41.3 0.6 copy-start.8
  44.8 0.8 copy-start.6
  46.0 0.8 copy-start.10
  47.1 2.9 copy-start.22
  47.1 2.9 copy-start.19
  48.1 3.6 copy-start
  55.1 0.9 slice-start
  61.7 2.9 copy-start.1
  61.7 2.9 copy-start.20
  61.9 6.5 %copy-start.18 = (pred[128,128]{0,1:T(8,128)(4,1)S(1)}, pred[128,128]{0,1:T(8,128)(4,1)}, u32[]{:S(2)}) copy-start(pred[128,128]{0,1:T(8,128)(4,1)} %fusion.87) | copy-start | bytes 49156
  61.9 4.3 collective-permute-start.3
  65.7 12.0 %copy-start.17 = (pred[128,128]{0,1:T(8,128)(4,1)S(1)}, pred[128,128]{0,1:T(8,128)(4,1)}, u32[]{:S(2)}) copy-start(pred[128,128]{0,1:T(8,128)(4,1)} %fusion.85) | copy-start | bytes 49156
  66.2 4.9 collective-permute-start.2
  71.2 8.0 %collective-permute-start = (bf16[128,4,64]{0,2,1:T(8,128)(2,1)}, bf16[128,4,64]{0,2,1:T(8,128)(2,1)S(1)}, u32[]{:S(2)}, u32[]{:S(2)}) collective-permute-start(bf16[128,4,64]{0,2,1:T(8,128)(2,1)} %bitcast.1), channel_id=1, source_target_pairs={{0,8},{8,16},{16,24},{24,32},{32,40},{40,48},{48,56},{56,64},{64,7... | collective-permute-start | bytes 196616 | tf_op jit(solution)/shard_map/ppermute | solution.py:13
  79.4 0.7 copy-start.21
  94.7 0.8 copy-start.11
  97.9 0.8 copy-start.9
  100.0 0.8 copy-start.7
  102.0 0.8 copy-start.5
  104.2 0.8 copy-start.3
  105.1 23.5 %collective-permute-start.8 = (f32[128,4,64]{0,2,1:T(8,128)}, f32[128,4,64]{0,2,1:T(8,128)}, u32[]{:S(2)}, u32[]{:S(2)}) collective-permute-start(f32[128,4,64]{0,2,1:T(8,128)} %convolution_bitcast_fusion.16), channel_id=1, source_target_pairs={{8,0},{16,8},{24,16},{32,24},{40,32},{48,40},{56,48},{64,56},{72,6... | collective-permute-start | bytes 393224 | tf_op jit(solution)/shard_map/ppermute | solution.py:13
  106.4 17.0 %collective-permute-start.15 = (f32[128,4,64]{0,2,1:T(8,128)S(1)}, f32[128,4,64]{0,2,1:T(8,128)S(1)}, u32[]{:S(2)}, u32[]{:S(2)}) collective-permute-start(f32[128,4,64]{0,2,1:T(8,128)S(1)} %convolution_bitcast_fusion.8), channel_id=1, source_target_pairs={{32,0},{40,8},{48,16},{56,24},{64,32},{72,40},{80,48},{88,56},{96,... | collective-permute-start | bytes 393224 | tf_op jit(solution)/shard_map/ppermute | solution.py:13
  107.7 17.0 %collective-permute-start.14 = (f32[128,4,64]{0,2,1:T(8,128)S(1)}, f32[128,4,64]{0,2,1:T(8,128)}, u32[]{:S(2)}, u32[]{:S(2)}) collective-permute-start(f32[128,4,64]{0,2,1:T(8,128)S(1)} %convolution_bitcast_fusion.9), channel_id=1, source_target_pairs={{24,0},{32,8},{40,16},{48,24},{56,32},{64,40},{72,48},{80,56},{88,... | collective-permute-start | bytes 393224 | tf_op jit(solution)/shard_map/ppermute | solution.py:13
  109.0 17.0 %collective-permute-start.13 = (f32[128,4,64]{0,2,1:T(8,128)S(1)}, f32[128,4,64]{0,2,1:T(8,128)}, u32[]{:S(2)}, u32[]{:S(2)}) collective-permute-start(f32[128,4,64]{0,2,1:T(8,128)S(1)} %convolution_bitcast_fusion.10), channel_id=1, source_target_pairs={{16,0},{24,8},{32,16},{40,24},{48,32},{56,40},{64,48},{72,56},{80,... | collective-permute-start | bytes 393224 | tf_op jit(solution)/shard_map/ppermute | solution.py:13
  110.3 17.0 %collective-permute-start.12 = (f32[128,4,64]{0,2,1:T(8,128)S(1)}, f32[128,4,64]{0,2,1:T(8,128)}, u32[]{:S(2)}, u32[]{:S(2)}) collective-permute-start(f32[128,4,64]{0,2,1:T(8,128)S(1)} %convolution_bitcast_fusion.11), channel_id=1, source_target_pairs={{8,0},{16,8},{24,16},{32,24},{40,32},{48,40},{56,48},{64,56},{72,6... | collective-permute-start | bytes 393224 | tf_op jit(solution)/shard_map/ppermute | solution.py:13
  120.0 4.7 copy-start.14
  120.0 6.0 copy-start.13
  123.4 11.3 %collective-permute-start.9 = (f32[128,4,64]{0,2,1:T(8,128)S(1)}, f32[128,4,64]{0,2,1:T(8,128)S(1)}, u32[]{:S(2)}, u32[]{:S(2)}) collective-permute-start(f32[128,4,64]{0,2,1:T(8,128)S(1)} %convolution_bitcast_fusion.15), channel_id=1, source_target_pairs={{16,0},{24,8},{32,16},{40,24},{48,32},{56,40},{64,48},{72,56},{80,... | collective-permute-start | bytes 393224 | tf_op jit(solution)/shard_map/ppermute | solution.py:13
  124.7 21.8 %collective-permute-start.10 = (f32[128,4,64]{0,2,1:T(8,128)S(1)}, f32[128,4,64]{0,2,1:T(8,128)S(1)}, u32[]{:S(2)}, u32[]{:S(2)}) collective-permute-start(f32[128,4,64]{0,2,1:T(8,128)S(1)} %copy-done.14), channel_id=1, source_target_pairs={{24,0},{32,8},{40,16},{48,24},{56,32},{64,40},{72,48},{80,56},{88,... | collective-permute-start | bytes 393224 | tf_op jit(solution)/shard_map/ppermute | solution.py:13
  126.0 37.7 %collective-permute-start.11 = (f32[128,4,64]{0,2,1:T(8,128)S(1)}, f32[128,4,64]{0,2,1:T(8,128)S(1)}, u32[]{:S(2)}, u32[]{:S(2)}) collective-permute-start(f32[128,4,64]{0,2,1:T(8,128)S(1)} %copy-done.13), channel_id=1, source_target_pairs={{32,0},{40,8},{48,16},{56,24},{64,32},{72,40},{80,48},{88,56},{96,... | collective-permute-start | bytes 393224 | tf_op jit(solution)/shard_map/ppermute | solution.py:13
Sparse Core Ops, SparseCore 0:
  120.1 480.4 all-reduce.18
where the time goes:
time: 611 us; the launch traced here: 609 us
  waiting for transfers between devices  477 us (78%)
  starting transfers between devices  49.4 us (8%)
  local copies, waits for them, and re-layouts  38.8 us (6%)
  matrix products  25.5 us (4%)
  between operations  15.1 us (2%)
    psum x1, waiting for transfers between devices, local(): grad_embed = lax.psum(local_embed, ('seq', 'piece'))  434 us
    ppermute x16, starting transfers between devices, shifted(): lax.ppermute(value, axis, [(source, source + steps) for source in range(l...  49.4 us
    ppermute x16, waiting for transfers between devices, shifted(): lax.ppermute(value, axis, [(source, source + steps) for source in range(l...  42.6 us
    unnamed x84, local copies, waits for them, and re-layouts  20.1 us
  transfers between devices with their start and end apart: 17, of which 8 were waited for; matrix products, arithmetic and copies ran while one was open for 7% of the time, Pallas kernels for 0%

commit v1 on v0

v1 whole, which is shorter than its diff:
```python
import jax
import jax.numpy as jnp
from jax import lax
from jax.experimental import pallas as pl
from jax.experimental.pallas import tpu as pltpu
from jax.sharding import PartitionSpec as P

HEAD_DIM = 64
BAND = 512
TOK = 128
GROUP = 4
ROWS = 256
SPAN = ROWS + BAND
DIMS = (4, 4, 4, 4, 2)
PIECES = 8
OTHERS = 16
F32 = jnp.float32
BF16 = jnp.bfloat16


def call(body, outs, *args, **kw):
    return pl.pallas_call(body, out_shape=[jax.ShapeDtypeStruct(s, d) for s, d in outs], **kw)(*args)


def mm(a, b, dims, precision=None):
    return lax.dot_general(a, b, (dims, ((), ())), precision=precision, preferred_element_type=F32)


NN = ((1,), (0,))
NT = ((1,), (1,))
TN = ((0,), (0,))


def flip_matrix(count, dtype):
    row = lax.broadcasted_iota(jnp.int32, (count, count), 0)
    col = lax.broadcasted_iota(jnp.int32, (count, count), 1)
    return jnp.where(row + col == count - 1, 1.0, 0.0).astype(dtype)


def pack_body(q, k, v, do, emb_t, packed, erev_t):
    for h in range(GROUP):
        cols = slice(h * HEAD_DIM, (h + 1) * HEAD_DIM)
        packed[h] = jnp.concatenate([q[:, cols], do[:, cols], k[:, cols], v[:, cols]], axis=1)
    flip = flip_matrix(TOK, BF16)
    blocks = BAND // TOK
    for b in range(blocks):
        cols = slice(b * TOK, (b + 1) * TOK)
        back = slice((blocks - 1 - b) * TOK, (blocks - b) * TOK)
        erev_t[:, back] = mm(emb_t[:, cols], flip, NN).astype(BF16)


def main_body(flag, own, halo, erev_t, ghalo, gown, gq_out, gemb, kv, gkv):
    scale = HEAD_DIM ** (-0.5)
    kv[:BAND] = halo[...].reshape(BAND, 2 * HEAD_DIM)
    own_all = own[...].reshape(BAND, 4 * HEAD_DIM)
    kv[BAND:] = own_all[:, 2 * HEAD_DIM :]
    emb_t = erev_t[...]
    flip = flip_matrix(ROWS, BF16)
    row = lax.broadcasted_iota(jnp.int32, (ROWS, SPAN), 0)
    col = lax.broadcasted_iota(jnp.int32, (ROWS, SPAN), 1)
    ahead = col - row - 1
    first = jnp.where(flag[0] > 0, 0, BAND)
    gerev = jnp.zeros((BAND, HEAD_DIM), F32)
    parts = []
    for b in range(BAND // ROWS):
        q = own_all[b * ROWS : (b + 1) * ROWS, :HEAD_DIM]
        do = own_all[b * ROWS : (b + 1) * ROWS, HEAD_DIM : 2 * HEAD_DIM]
        k = kv[b * ROWS : b * ROWS + SPAN, :HEAD_DIM]
        v = kv[b * ROWS : b * ROWS + SPAN, HEAD_DIM:]
        along = jnp.concatenate([mm(q, emb_t, NN), jnp.zeros((ROWS, SPAN - BAND), F32)], axis=1)
        along = pltpu.roll(along, 1, 1, stride=1, stride_axis=0)
        valid = (ahead >= 0) & (ahead < BAND) & (col + b * ROWS >= first)
        score = jnp.where(valid, scale * (mm(q, k, NT) + along), -jnp.inf)
        top = jnp.max(score, axis=1, keepdims=True)
        prob = jnp.exp(score - top)
        prob = prob * (1.0 / jnp.sum(prob, axis=1, keepdims=True))
        prob_b = prob.astype(BF16)
        dprob = mm(do, v, NT)
        delta = jnp.sum(prob_b.astype(F32) * dprob, axis=1, keepdims=True)
        dscore = (prob * (dprob - delta) * scale).astype(BF16)
        dalong = pltpu.roll(mm(flip, dscore, NN), SPAN - ROWS, 1, stride=1, stride_axis=0)
        dalong = dalong[:, :BAND].astype(BF16)
        gqe = mm(dalong, emb_t, NT)
        hi = gqe.astype(BF16)
        lo = (gqe - hi.astype(F32)).astype(BF16)
        gq = mm(dscore, k, NN) + mm(flip, hi, NN) + mm(flip, lo, NN)
        gq_out[b * ROWS : (b + 1) * ROWS] = gq
        gerev = gerev + mm(dalong, mm(flip, q, NN).astype(BF16), TN)
        parts.append(jnp.concatenate([mm(dscore, q, TN), mm(prob_b, do, TN)], axis=1))
    gkv[:ROWS] = parts[0][:ROWS]
    gkv[ROWS:SPAN] = parts[0][ROWS:] + parts[1][:BAND]
    gkv[SPAN:] = parts[1][BAND:]
    ghalo[...] = gkv[:BAND].astype(BF16).reshape(GROUP, TOK, 2 * HEAD_DIM)
    gown[...] = gkv[BAND:]
    for p in range(PIECES):
        chunk = gerev[BAND - (p + 1) * 64 : BAND - p * 64]
        gemb[p] = jnp.concatenate([chunk[:32], chunk[32:]], axis=1)


def sum_body(x, out):
    out[...] = jnp.sum(x[...].astype(F32), axis=0)


def out_pack_body(gown, gq, back, emb, out):
    gkv = gown[...].reshape(GROUP, TOK, 2 * HEAD_DIM) + back[...].astype(F32)
    gqs = gq[...].reshape(GROUP, TOK, HEAD_DIM)
    e = jnp.sum(emb[...], axis=0)
    e = jnp.concatenate([e[:, :HEAD_DIM], e[:, HEAD_DIM:]], axis=0)
    hi = e.astype(BF16)
    lo = (e - hi.astype(F32)).astype(BF16)
    hl = jnp.concatenate([hi, lo], axis=0)
    for g in range(GROUP):
        out[g] = jnp.concatenate([gkv[g].astype(BF16), gqs[g].astype(BF16), hl], axis=1)


def unpack_body(x, gq, gk, gv, emb):
    gk[...] = jnp.concatenate([x[h, :, :HEAD_DIM] for h in range(GROUP)], axis=1)
    gv[...] = jnp.concatenate([x[h, :, HEAD_DIM : 2 * HEAD_DIM] for h in range(GROUP)], axis=1)
    gq[...] = jnp.concatenate([x[h, :, 2 * HEAD_DIM : 3 * HEAD_DIM] for h in range(GROUP)], axis=1)
    hl = jnp.sum(x[:, :, 3 * HEAD_DIM :].astype(F32), axis=0)
    e = hl[:64] + hl[64:]
    e = jnp.concatenate([e[:32], e[32:]], axis=1)
    for i in range(emb.shape[0]):
        emb[i] = e


def last_body(x, out):
    e = jnp.sum(x[...].astype(F32), axis=0)
    e = jnp.concatenate([e[:, :HEAD_DIM], e[:, HEAD_DIM:]], axis=0)
    e = mm(flip_matrix(64, F32), e, NN, precision=lax.Precision.HIGHEST)
    e = jnp.concatenate([e[:32], e[32:]], axis=1)
    for i in range(PIECES):
        out[i] = e


def place_body(x, out):
    for p in range(PIECES):
        e = jnp.concatenate([x[p, :, :HEAD_DIM], x[p, :, HEAD_DIM:]], axis=0)
        out[:, p * 64 : (p + 1) * 64] = e.T


def local(query, key_rows, value_matrix_rows, grad_out, rel_embed):
    seq = ("y", "zg", "zi")
    piece = ("x", "core")
    here = lax.axis_index(seq)
    packed, erev_t = call(
        pack_body,
        [((GROUP, TOK, 4 * HEAD_DIM), BF16), ((HEAD_DIM, BAND), BF16)],
        query, key_rows, value_matrix_rows, grad_out, rel_embed.T,
    )
    own = lax.all_to_all(packed, "zi", 0, 0, tiled=True)
    n = lax.axis_size(seq)
    halo = lax.ppermute(own[:, :, 2 * HEAD_DIM :], seq, [(s, s + GROUP) for s in range(n - GROUP)])
    flag = (here >= GROUP).astype(jnp.int32).reshape(1)
    vm = pl.BlockSpec(memory_space=pltpu.VMEM)
    ghalo, gown, gq, gemb = call(
        main_body,
        [
            ((GROUP, TOK, 2 * HEAD_DIM), BF16),
            ((BAND, 2 * HEAD_DIM), F32),
            ((BAND, HEAD_DIM), F32),
            ((PIECES, 32, 128), F32),
        ],
        flag, own, halo, erev_t,
        in_specs=[pl.BlockSpec(memory_space=pltpu.SMEM), vm, vm, vm],
        scratch_shapes=[pltpu.VMEM((2 * BAND, 2 * HEAD_DIM), BF16), pltpu.VMEM((2 * BAND, 2 * HEAD_DIM), F32)],
    )
    back = lax.ppermute(ghalo, seq, [(s, s - GROUP) for s in range(GROUP, n)])
    gemb = lax.all_to_all(gemb, piece, 0, 0, tiled=True)
    (out,) = call(out_pack_body, [((GROUP, TOK, 4 * HEAD_DIM), BF16)], gown, gq, back, gemb)
    out = lax.all_to_all(out, "zi", 0, 0, tiled=True)
    grad_query, grad_key, grad_value, part = call(
        unpack_body,
        [((TOK, GROUP * HEAD_DIM), BF16)] * 3 + [((OTHERS, 32, 128), F32)],
        out,
    )
    part = lax.all_to_all(part, ("y", "zg"), 0, 0, tiled=True)
    (part,) = call(last_body, [((PIECES, 32, 128), F32)], part)
    part = lax.all_to_all(part, piece, 0, 0, tiled=True)
    (grad_embed_t,) = call(place_body, [((HEAD_DIM, BAND), F32)], part)
    return grad_query, grad_key, grad_value, grad_embed_t.T


def solution(mesh):
    fine = jax.sharding.Mesh(mesh.devices.reshape(DIMS), ("y", "zg", "zi", "x", "core"))
    rows = P(("y", "zg", "zi"), ("x", "core"))
    return jax.shard_map(
        local,
        mesh=fine,
        in_specs=(rows, rows, rows, rows, P()),
        out_specs=(rows, rows, rows, P()),
        check_vma=False,
    )
```

time: 611 us -> 125 us (0.20)
  waiting for transfers between devices: 477 us -> 2.77 us
  blocking collectives: 0 us -> 92.7 us
  starting transfers between devices: 49.4 us -> 10.9 us
  local copies, waits for them, and re-layouts: 38.8 us -> 1.33 us
  matrix products: 25.5 us -> 0 us
  Pallas kernels: 0 us -> 15.3 us
  between operations: 15.1 us -> 0.67 us
    psum x1 -> x0, waiting for transfers between devices: 434 us -> none  [local(): grad_embed = lax.psum(local_embed, ('seq', 'piece'))]
    all_to_all x0 -> x5, blocking collectives: none -> 92.7 us  [the longest x1 29.3 us: local(): part = lax.all_to_all(part, ('y', 'zg'), 0, 0, tiled=True)]
    ppermute x16 -> x2, waiting for transfers between devices: 42.6 us -> 2.77 us  [the longest x1 2.77 us: local(): lax.ppermute(own[:, :, 2 * HEAD_DIM:], seq, [(s, s + GROUP) for s in rang...]
    ppermute x16 -> x2, starting transfers between devices: 49.4 us -> 10.9 us  [the longest x1 9.67 us: local(): lax.ppermute(own[:, :, 2 * HEAD_DIM:], seq, [(s, s + GROUP) for s in rang...]
    dot_general x45 -> x0, matrix products: 25.5 us -> none  [the longest x5 5.41 us: pair_grads(): jnp.einsum('thd,shd->hts', dout, value_tensor, preferred_element_type=jnp...]
    unnamed x84 -> x6, local copies, waits for them, and re-layouts: 20.1 us -> 1.31 us
    pallas_call x0 -> x6, Pallas kernels: none -> 15.3 us  [call(): pl.pallas_call(body, out_shape=[jax.ShapeDtypeStruct(s, d) for s, d in ou...]
    reshape x10 -> x0, local copies, waits for them, and re-layouts: 9.41 us -> none  [skew_rel(): flat.reshape(head_count, row_tiles, cols + row_tiles - 1)]
  transfers between devices with their start and end apart: 17 -> 2, of which waited for: 8 -> 1; matrix products, arithmetic and copies ran while one was open for 7% -> 0% of each run, Pallas kernels for 0% -> 0%
where the time goes in v1:
time: 125 us; the launch traced here: 124 us
  blocking collectives  92.7 us (74%)
  Pallas kernels  15.3 us (12%)
  starting transfers between devices  10.9 us (9%)
  waiting for transfers between devices  2.77 us (2%)
  local copies, waits for them, and re-layouts  1.33 us (1%)
    all_to_all x1, blocking collectives, local(): part = lax.all_to_all(part, ('y', 'zg'), 0, 0, tiled=True)  29.3 us
    all_to_all x1, blocking collectives, local(): out = lax.all_to_all(out, 'zi', 0, 0, tiled=True)  23.1 us
    pallas_call x6, Pallas kernels, call(): pl.pallas_call(body, out_shape=[jax.ShapeDtypeStruct(s, d) for s, d in ou...  15.3 us
    all_to_all x1, blocking collectives, local(): part = lax.all_to_all(part, piece, 0, 0, tiled=True)  14.1 us
    all_to_all x1, blocking collectives, local(): gemb = lax.all_to_all(gemb, piece, 0, 0, tiled=True)  13.9 us
    all_to_all x1, blocking collectives, local(): own = lax.all_to_all(packed, 'zi', 0, 0, tiled=True)  12.4 us
    ppermute x1, starting transfers between devices, local(): lax.ppermute(own[:, :, 2 * HEAD_DIM:], seq, [(s, s + GROUP) for s in rang...  9.67 us
    ppermute x1, waiting for transfers between devices, local(): lax.ppermute(own[:, :, 2 * HEAD_DIM:], seq, [(s, s + GROUP) for s in rang...  2.77 us
  transfers between devices with their start and end apart: 2, of which 1 were waited for; matrix products, arithmetic and copies ran while one was open for 0% of the time, Pallas kernels for 0%

profile of v1, /device:TPU:1, one launch (start us, length us, event | category | flops | bytes accessed | tf_op | source)
XLA Modules:
  0.0 123.8 jit_solution(3146366618743461909)
XLA Ops:
  0.6 1.8 %shard_map.84 = (bf16[4,128,256]{2,1,0:T(8,128)(2,1)}, bf16[64,512]{1,0:T(8,128)(2,1)}) custom-call(bf16[128,256]{1,0:T(8,128)(2,1)} %q.1, bf16[128,256]{1,0:T(8,128)(2,1)} %k.1, bf16[128,256]{1,0:T(8,128)(2,1)} %v.1, bf16[128,256]{1,0:T(8,128)(2,1)} %do.1, bf16[64,512]{1,0:T(8,128)(2,1)} %bitcast.4), custom_call_target="tpu_custom_call" | custom-call | tf_op jit(solution)/shard_map/pallas_call | solution.py:22
  2.5 12.4 %all_to_all.25.own = bf16[4,128,256]{2,1,0:T(8,128)(2,1)S(1)} all-to-all(bf16[4,128,256]{2,1,0:T(8,128)(2,1)} %get-tuple-element.14), channel_id=1, replica_groups=mesh['y'=4,'zg'=4,'zi'=4,'x'=4,'core'=2] {'zi'}, dimensions={0} | all-to-all | bytes 524288 | tf_op jit(solution)/shard_map/all_to_all | solution.py:151
  14.9 0.0 copy-start
  14.9 9.7 %collective-permute-start = (bf16[4,128,128]{2,1,0:T(8,128)(2,1)S(1)}, bf16[4,128,128]{2,1,0:T(8,128)(2,1)S(1)}, u32[]{:S(2)}, u32[]{:S(2)}) collective-permute-start(bf16[4,128,128]{2,1,0:T(8,128)(2,1)S(1)} %slice.4), channel_id=1, source_target_pairs={{0,32},{8,40},{16,48},{24,56},{32,64},{40,72},{48,80},{56,88},{64,... | collective-permute-start | bytes 393224 | tf_op jit(solution)/shard_map/ppermute | solution.py:153
  24.6 2.8 %collective-permute-done.halo = bf16[4,128,128]{2,1,0:T(8,128)(2,1)S(1)} collective-permute-done((bf16[4,128,128]{2,1,0:T(8,128)(2,1)S(1)}, bf16[4,128,128]{2,1,0:T(8,128)(2,1)S(1)}, u32[]{:S(2)}, u32[]{:S(2)}) %collective-permute-start) | collective-permute-done | bytes 131104 | tf_op jit(solution)/shard_map/ppermute | solution.py:153
  27.4 0.0 copy-start.1
  27.4 0.0 copy-done
  27.4 0.7 copy-done.1
  28.0 5.7 %shard_map.85 = (bf16[4,128,128]{2,1,0:T(8,128)(2,1)}, f32[512,128]{1,0:T(8,128)}, f32[512,64]{1,0:T(8,128)}, f32[8,32,128]{2,1,0:T(8,128)}) custom-call(s32[1]{0:T(128)} %bitcast.flag, bf16[4,128,256]{2,1,0:T(8,128)(2,1)} %copy-done, bf16[4,128,128]{2,1,0:T(8,128)(2,1)} %copy-done.1, bf16[64,512]{1,0:T(8,128)(2,1)} %get-tuple-element.15.erev_t), custom_call_target="tpu_custom_call" | custom-call | tf_op jit(solution)/shard_map/pallas_call | solution.py:22
  33.7 1.3 %collective-permute-start.1 = (bf16[4,128,128]{2,1,0:T(8,128)(2,1)}, bf16[4,128,128]{2,1,0:T(8,128)(2,1)S(1)}, u32[]{:S(2)}, u32[]{:S(2)}) collective-permute-start(bf16[4,128,128]{2,1,0:T(8,128)(2,1)} %get-tuple-element.18), channel_id=1, source_target_pairs={{32,0},{40,8},{48,16},{56,24},{64,32},{72,40},{80,48},{88,56},{96,... | collective-permute-start | bytes 393224 | tf_op jit(solution)/shard_map/ppermute | solution.py:168
  35.0 13.9 %all_to_all.26.emb = f32[8,32,128]{2,1,0:T(8,128)} all-to-all(f32[8,32,128]{2,1,0:T(8,128)} %get-tuple-element.19), channel_id=1, replica_groups=mesh['y'=4,'zg'=4,'zi'=4,'x'=4,'core'=2] {'x','core'}, dimensions={0} | all-to-all | bytes 262144 | tf_op jit(solution)/shard_map/all_to_all | solution.py:169
  48.9 0.0 collective-permute-done.1.back
  48.9 0.0 copy-start.2
  48.9 0.7 copy-done.2
  49.5 2.0 %shard_map.86 = bf16[4,128,256]{2,1,0:T(8,128)(2,1)} custom-call(f32[512,128]{1,0:T(8,128)} %get-tuple-element.16.gown, f32[512,64]{1,0:T(8,128)} %get-tuple-element.17.gq, bf16[4,128,128]{2,1,0:T(8,128)(2,1)} %copy-done.2, f32[8,32,128]{2,1,0:T(8,128)} %all_to_all.26.emb), custom_call_target="tpu_custom_call" | custom-call | tf_op jit(solution)/shard_map/pallas_call | solution.py:22
  51.5 23.1 %all_to_all.27.x = bf16[4,128,256]{2,1,0:T(8,128)(2,1)} all-to-all(bf16[4,128,256]{2,1,0:T(8,128)(2,1)} %shard_map.86), channel_id=1, replica_groups=mesh['y'=4,'zg'=4,'zi'=4,'x'=4,'core'=2] {'zi'}, dimensions={0} | all-to-all | bytes 524288 | tf_op jit(solution)/shard_map/all_to_all | solution.py:171
  74.5 1.8 %shard_map.87 = (bf16[128,256]{1,0:T(8,128)(2,1)}, bf16[128,256]{1,0:T(8,128)(2,1)}, bf16[128,256]{1,0:T(8,128)(2,1)}, f32[16,32,128]{2,1,0:T(8,128)}) custom-call(bf16[4,128,256]{2,1,0:T(8,128)(2,1)} %all_to_all.27.x), custom_call_target="tpu_custom_call" | custom-call | tf_op jit(solution)/shard_map/pallas_call | solution.py:22
  76.3 29.3 %all_to_all.28.x = f32[16,32,128]{2,1,0:T(8,128)} all-to-all(f32[16,32,128]{2,1,0:T(8,128)} %get-tuple-element.23), channel_id=1, replica_groups=mesh['y'=4,'zg'=4,'zi'=4,'x'=4,'core'=2] {'y','zg'}, dimensions={0} | all-to-all | bytes 524288 | tf_op jit(solution)/shard_map/all_to_all | solution.py:177
  105.7 1.9 %shard_map.88 = f32[8,32,128]{2,1,0:T(8,128)} custom-call(f32[16,32,128]{2,1,0:T(8,128)} %all_to_all.28.x), custom_call_target="tpu_custom_call" | custom-call | tf_op jit(solution)/shard_map/pallas_call | solution.py:22
  107.6 14.1 %all_to_all.29.x = f32[8,32,128]{2,1,0:T(8,128)} all-to-all(f32[8,32,128]{2,1,0:T(8,128)} %shard_map.88), channel_id=1, replica_groups=mesh['y'=4,'zg'=4,'zi'=4,'x'=4,'core'=2] {'x','core'}, dimensions={0} | all-to-all | bytes 262144 | tf_op jit(solution)/shard_map/all_to_all | solution.py:179
  121.7 2.1 %shard_map.89 = f32[64,512]{1,0:T(8,128)} custom-call(f32[8,32,128]{2,1,0:T(8,128)} %all_to_all.29.x), custom_call_target="tpu_custom_call" | custom-call | tf_op jit(solution)/shard_map/pallas_call | solution.py:22
  (1 shorter events, 0.0 us)
Async XLA Ops:
  14.9 12.5 %copy-start = (bf16[4,128,256]{2,1,0:T(8,128)(2,1)}, bf16[4,128,256]{2,1,0:T(8,128)(2,1)S(1)}, u32[]{:S(2)}) copy-start(bf16[4,128,256]{2,1,0:T(8,128)(2,1)S(1)} %all_to_all.25.own) | copy-start | bytes 786436
  14.9 12.5 %collective-permute-start = (bf16[4,128,128]{2,1,0:T(8,128)(2,1)S(1)}, bf16[4,128,128]{2,1,0:T(8,128)(2,1)S(1)}, u32[]{:S(2)}, u32[]{:S(2)}) collective-permute-start(bf16[4,128,128]{2,1,0:T(8,128)(2,1)S(1)} %slice.4), channel_id=1, source_target_pairs={{0,32},{8,40},{16,48},{24,56},{32,64},{40,72},{48,80},{56,88},{64,... | collective-permute-start | bytes 393224 | tf_op jit(solution)/shard_map/ppermute | solution.py:153
  27.4 0.7 copy-start.1
  33.7 15.1 %collective-permute-start.1 = (bf16[4,128,128]{2,1,0:T(8,128)(2,1)}, bf16[4,128,128]{2,1,0:T(8,128)(2,1)S(1)}, u32[]{:S(2)}, u32[]{:S(2)}) collective-permute-start(bf16[4,128,128]{2,1,0:T(8,128)(2,1)} %get-tuple-element.18), channel_id=1, source_target_pairs={{32,0},{40,8},{48,16},{56,24},{64,32},{72,40},{80,48},{88,56},{96,... | collective-permute-start | bytes 393224 | tf_op jit(solution)/shard_map/ppermute | solution.py:168
  48.9 0.7 copy-start.2

commit v2 on v1

v2 whole, which is shorter than its diff:
```python
import jax
import jax.numpy as jnp
from jax import lax
from jax.experimental import pallas as pl
from jax.experimental.pallas import tpu as pltpu
from jax.sharding import PartitionSpec as P


HEAD_DIM = 64
BAND = 512
TOK = 128
GROUP = 4
ROWS = 256
SPAN = ROWS + BAND
DIMS = (4, 4, 4, 4, 2)
BLOCKS = BAND // TOK
F32 = jnp.float32
BF16 = jnp.bfloat16


def call(body, outs, *args, **kw):
    args = [near(a) if a.ndim == 3 else a for a in args]
    shapes = [pltpu.VMEM(s, d) if v else jax.ShapeDtypeStruct(s, d) for s, d, v in outs]
    return pl.pallas_call(body, out_shape=shapes, **kw)(*args)


def near(x):
    return pltpu.with_memory_space_constraint(x, pltpu.VMEM)


def mm(a, b, dims, precision=None):
    return lax.dot_general(a, b, (dims, ((), ())), precision=precision, preferred_element_type=F32)


NN = ((1,), (0,))
NT = ((1,), (1,))
TN = ((0,), (0,))


def span(block):
    return slice(block * TOK, (block + 1) * TOK)


def flip_matrix(count, dtype):
    row = lax.broadcasted_iota(jnp.int32, (count, count), 0)
    col = lax.broadcasted_iota(jnp.int32, (count, count), 1)
    return jnp.where(row + col == count - 1, 1.0, 0.0).astype(dtype)


def pack_kv_body(k, v, packed):
    for h in range(GROUP):
        cols = slice(h * HEAD_DIM, (h + 1) * HEAD_DIM)
        packed[h] = jnp.concatenate([k[:, cols], v[:, cols]], axis=1)


def pack_q_body(q, do, emb_t, packed, erev_t):
    for h in range(GROUP):
        cols = slice(h * HEAD_DIM, (h + 1) * HEAD_DIM)
        packed[h] = jnp.concatenate([q[:, cols], do[:, cols]], axis=1)
    flip = flip_matrix(TOK, BF16)
    for b in range(BLOCKS):
        erev_t[:, span(BLOCKS - 1 - b)] = mm(emb_t[:, span(b)], flip, NN).astype(BF16)


def main_body(flag, qd, own, halo, erev_t, ghalo, gown, gq_out, gemb, kv, gkv):
    scale = HEAD_DIM ** (-0.5)
    kv[:BAND] = halo[...].reshape(BAND, 2 * HEAD_DIM)
    kv[BAND:] = own[...].reshape(BAND, 2 * HEAD_DIM)
    qdo = qd[...].reshape(BAND, 2 * HEAD_DIM)
    emb_t = erev_t[...]
    flip = flip_matrix(ROWS, BF16)
    row = lax.broadcasted_iota(jnp.int32, (ROWS, SPAN), 0)
    col = lax.broadcasted_iota(jnp.int32, (ROWS, SPAN), 1)
    ahead = col - row - 1
    first = jnp.where(flag[0] > 0, 0, BAND)
    gerev_t = jnp.zeros((HEAD_DIM, BAND), F32)
    parts = []
    for b in range(BAND // ROWS):
        q = qdo[b * ROWS : (b + 1) * ROWS, :HEAD_DIM]
        do = qdo[b * ROWS : (b + 1) * ROWS, HEAD_DIM:]
        k = kv[b * ROWS : b * ROWS + SPAN, :HEAD_DIM]
        v = kv[b * ROWS : b * ROWS + SPAN, HEAD_DIM:]
        along = jnp.concatenate([mm(q, emb_t, NN), jnp.zeros((ROWS, SPAN - BAND), F32)], axis=1)
        along = pltpu.roll(along, 1, 1, stride=1, stride_axis=0)
        valid = (ahead >= 0) & (ahead < BAND) & (col + b * ROWS >= first)
        score = jnp.where(valid, scale * (mm(q, k, NT) + along), -jnp.inf)
        top = jnp.max(score, axis=1, keepdims=True)
        prob = jnp.exp(score - top)
        prob = prob * (1.0 / jnp.sum(prob, axis=1, keepdims=True))
        prob_b = prob.astype(BF16)
        dprob = mm(do, v, NT)
        delta = jnp.sum(prob_b.astype(F32) * dprob, axis=1, keepdims=True)
        dscore = (prob * (dprob - delta) * scale).astype(BF16)
        dalong = pltpu.roll(mm(flip, dscore, NN), SPAN - ROWS, 1, stride=1, stride_axis=0)
        dalong = dalong[:, :BAND].astype(BF16)
        gqe = mm(dalong, emb_t, NT)
        hi = gqe.astype(BF16)
        lo = (gqe - hi.astype(F32)).astype(BF16)
        gq = mm(dscore, k, NN) + mm(flip, hi, NN) + mm(flip, lo, NN)
        gq_out[b * ROWS : (b + 1) * ROWS] = gq
        gerev_t = gerev_t + mm(mm(flip, q, NN).astype(BF16), dalong, TN)
        parts.append(jnp.concatenate([mm(dscore, q, TN), mm(prob_b, do, TN)], axis=1))
    gkv[:ROWS] = parts[0][:ROWS]
    gkv[ROWS:SPAN] = parts[0][ROWS:] + parts[1][:BAND]
    gkv[SPAN:] = parts[1][BAND:]
    ghalo[...] = gkv[:BAND].astype(BF16).reshape(GROUP, TOK, 2 * HEAD_DIM)
    gown[...] = gkv[BAND:]
    flip = flip_matrix(TOK, BF16)
    for b in range(BLOCKS):
        block = gerev_t[:, span(BLOCKS - 1 - b)]
        hi = block.astype(BF16)
        lo = (block - hi.astype(F32)).astype(BF16)
        block = mm(hi, flip, NN) + mm(lo, flip, NN)
        for d in range(HEAD_DIM // 8):
            gemb[d * BLOCKS + b] = block[d * 8 : (d + 1) * 8]


def out_pack_body(gown, gq, back, out):
    gkv = gown[...].reshape(GROUP, TOK, 2 * HEAD_DIM) + back[...].astype(F32)
    half = TOK // 2
    for g in range(GROUP):
        rows = gq[g * TOK : (g + 1) * TOK]
        out[g, :TOK] = gkv[g].astype(BF16)
        out[g, TOK:] = jnp.concatenate([rows[:half], rows[half:]], axis=1).astype(BF16)


def unpack_body(x, gq, gk, gv):
    half = TOK // 2
    gk[...] = jnp.concatenate([x[h, :TOK, :HEAD_DIM] for h in range(GROUP)], axis=1)
    gv[...] = jnp.concatenate([x[h, :TOK, HEAD_DIM:] for h in range(GROUP)], axis=1)
    gq[:half] = jnp.concatenate([x[h, TOK:, :HEAD_DIM] for h in range(GROUP)], axis=1)
    gq[half:] = jnp.concatenate([x[h, TOK:, HEAD_DIM:] for h in range(GROUP)], axis=1)


def local(query, key_rows, value_matrix_rows, grad_out, rel_embed):
    seq, line, plane = ("y", "zg", "zi"), ("zg", "zi"), ("y", "x", "core")
    n = lax.axis_size(seq)
    packed = ((GROUP, TOK, 2 * HEAD_DIM), BF16, True)
    (kv,) = call(pack_kv_body, [packed], key_rows, value_matrix_rows)
    kv = exchange(kv, "zi")
    halo = lax.ppermute(kv, seq, [(s, s + GROUP) for s in range(n - GROUP)])
    qd, erev_t = call(pack_q_body, [packed, ((HEAD_DIM, BAND), BF16, True)], query, grad_out, rel_embed.T)
    qd = exchange(qd, "zi")
    flag = (lax.axis_index(seq) >= GROUP).astype(jnp.int32).reshape(1)
    vm = pl.BlockSpec(memory_space=pltpu.VMEM)
    ghalo, gown, gq, gemb = call(
        main_body,
        [
            packed,
            ((BAND, 2 * HEAD_DIM), F32, True),
            ((BAND, HEAD_DIM), F32, True),
            ((lax.axis_size(plane), 8, 128), F32, True),
        ],
        flag, qd, kv, halo, near(erev_t),
        in_specs=[pl.BlockSpec(memory_space=pltpu.SMEM), vm, vm, vm, vm],
        scratch_shapes=[pltpu.VMEM((2 * BAND, 2 * HEAD_DIM), BF16), pltpu.VMEM((2 * BAND, 2 * HEAD_DIM), F32)],
    )
    back = lax.ppermute(ghalo, seq, [(s, s - GROUP) for s in range(GROUP, n)])
    part = jnp.sum(exchange(gemb, plane), axis=0)
    part = jnp.sum(spread(part, line), axis=0)
    whole = spread(part, plane)
    grad_embed_t = whole.reshape(8, BLOCKS, 8, 128).transpose(0, 2, 1, 3).reshape(HEAD_DIM, BAND)
    (out,) = call(out_pack_body, [((GROUP, TOK + TOK // 2, 2 * HEAD_DIM), BF16, True)], near(gown), near(gq), back)
    out = exchange(out, "zi")
    grad_query, grad_key, grad_value = call(unpack_body, [((TOK, GROUP * HEAD_DIM), BF16, False)] * 3, out)
    return grad_query, grad_key, grad_value, grad_embed_t.T


def exchange(x, axes):
    return lax.all_to_all(x, axes, 0, 0, tiled=True)


def spread(x, axes):
    return exchange(jnp.tile(x, (lax.axis_size(axes), 1, 1)), axes)


def solution(mesh):
    fine = jax.sharding.Mesh(mesh.devices.reshape(DIMS), ("y", "zg", "zi", "x", "core"))
    rows = P(("y", "zg", "zi"), ("x", "core"))
    return jax.shard_map(
        local,
        mesh=fine,
        in_specs=(rows, rows, rows, rows, P()),
        out_specs=(rows, rows, rows, P()),
        check_vma=False,
    )
```

time: 125 us -> 110 us (0.88)
  blocking collectives: 92.7 us -> 19.4 us
  starting transfers between devices: 10.9 us -> 50.2 us
  waiting for transfers between devices: 2.77 us -> 27.4 us
  Pallas kernels: 15.3 us -> 8.65 us
    all_to_all x5 -> x1, blocking collectives: 92.7 us -> 19.4 us  [exchange(): return lax.all_to_all(x, axes, 0, 0, tiled=True)]
    all_to_all x0 -> x5, starting transfers between devices: none -> 39.9 us  [exchange(): return lax.all_to_all(x, axes, 0, 0, tiled=True)]
    all_to_all x0 -> x5, waiting for transfers between devices: none -> 22.3 us  [exchange(): return lax.all_to_all(x, axes, 0, 0, tiled=True)]
    pallas_call x6 -> x5, Pallas kernels: 15.3 us -> 8.65 us  [call(): return pl.pallas_call(body, out_shape=shapes, **kw)(*args)]
    ppermute x1, waiting for transfers between devices: 0.01 us -> 3.23 us  [local(): back = lax.ppermute(ghalo, seq, [(s, s - GROUP) for s in range(GROUP, n)])]
    another operation x0 -> x2, local copies, waits for them, and re-layouts: none -> 1.3 us  [spread(): return exchange(jnp.tile(x, (lax.axis_size(axes), 1, 1)), axes)]
  transfers between devices with their start and end apart: 2 -> 7, of which waited for: 1 -> 6; matrix products, arithmetic and copies ran while one was open for 0% -> 1% of each run, Pallas kernels for 0% -> 2%
where the time goes in v2:
time: 110 us; the launch traced here: 108 us
  starting transfers between devices  50.2 us (46%)
  waiting for transfers between devices  27.4 us (25%)
  blocking collectives  19.4 us (18%)
  Pallas kernels  8.65 us (8%)
  local copies, waits for them, and re-layouts  1.96 us (2%)
    all_to_all x5, starting transfers between devices, exchange(): return lax.all_to_all(x, axes, 0, 0, tiled=True)  39.9 us
    all_to_all x5, waiting for transfers between devices, exchange(): return lax.all_to_all(x, axes, 0, 0, tiled=True)  22.3 us
    all_to_all x1, blocking collectives, exchange(): return lax.all_to_all(x, axes, 0, 0, tiled=True)  19.4 us
    ppermute x1, starting transfers between devices, local(): halo = lax.ppermute(kv, seq, [(s, s + GROUP) for s in range(n - GROUP)])  8.98 us
    pallas_call x5, Pallas kernels, call(): return pl.pallas_call(body, out_shape=shapes, **kw)(*args)  8.65 us
    ppermute x1, waiting for transfers between devices, local(): back = lax.ppermute(ghalo, seq, [(s, s - GROUP) for s in range(GROUP, n)])  3.23 us
  transfers between devices with their start and end apart: 7, of which 6 were waited for; matrix products, arithmetic and copies ran while one was open for 1% of the time, Pallas kernels for 2%

profile of v2, /device:TPU:1, one launch (start us, length us, event | category | flops | bytes accessed | tf_op | source)
XLA Modules:
  0.0 108.5 jit_solution(13327941855047706439)
XLA Ops:
  0.6 1.6 %shard_map.85 = bf16[4,128,128]{2,1,0:T(8,128)(2,1)} custom-call(bf16[128,256]{1,0:T(8,128)(2,1)} %k.1, bf16[128,256]{1,0:T(8,128)(2,1)} %v.1), custom_call_target="tpu_custom_call" | custom-call | tf_op jit(solution)/shard_map/pallas_call | solution.py:24
  2.2 6.4 %all-to-all-start.1 = ((bf16[4,128,128]{2,1,0:T(8,128)(2,1)}), bf16[4,128,128]{2,1,0:T(8,128)(2,1)S(1)}, u32[]{:S(2)}, u32[]{:S(2)}) async-start(bf16[4,128,128]{2,1,0:T(8,128)(2,1)} %shard_map.85), calls=%async_computation.1 | async-start | bytes 262144 | tf_op jit(solution)/shard_map/all_to_all | solution.py:170
  8.7 1.7 %shard_map.84 = (bf16[4,128,128]{2,1,0:T(8,128)(2,1)}, bf16[64,512]{1,0:T(8,128)(2,1)S(1)}) custom-call(bf16[128,256]{1,0:T(8,128)(2,1)} %q.1, bf16[128,256]{1,0:T(8,128)(2,1)} %do.1, bf16[64,512]{1,0:T(8,128)(2,1)} %bitcast.10), custom_call_target="tpu_custom_call" | custom-call | tf_op jit(solution)/shard_map/pallas_call | solution.py:24
  10.4 3.1 %all-to-all-done.1.own = bf16[4,128,128]{2,1,0:T(8,128)(2,1)S(1)} async-done(((bf16[4,128,128]{2,1,0:T(8,128)(2,1)}), bf16[4,128,128]{2,1,0:T(8,128)(2,1)S(1)}, u32[]{:S(2)}, u32[]{:S(2)}) %all-to-all-start.1) | async-done | bytes 131104 | tf_op jit(solution)/shard_map/all_to_all | solution.py:170
  13.5 3.3 %all-to-all-start = ((bf16[4,128,128]{2,1,0:T(8,128)(2,1)}), bf16[4,128,128]{2,1,0:T(8,128)(2,1)S(1)}, u32[]{:S(2)}, u32[]{:S(2)}) async-start(bf16[4,128,128]{2,1,0:T(8,128)(2,1)} %get-tuple-element.13), calls=%async_computation | async-start | bytes 262144 | tf_op jit(solution)/shard_map/all_to_all | solution.py:170
  16.8 9.0 %collective-permute-start = (bf16[4,128,128]{2,1,0:T(8,128)(2,1)S(1)}, bf16[4,128,128]{2,1,0:T(8,128)(2,1)S(1)}, u32[]{:S(2)}, u32[]{:S(2)}) collective-permute-start(bf16[4,128,128]{2,1,0:T(8,128)(2,1)S(1)} %all-to-all-done.1.own), channel_id=1, source_target_pairs={{0,32},{8,40},{16,48},{24,56},{32,64},{40,72},{48,80},{56,88},{64,... | collective-permute-start | bytes 393224 | tf_op jit(solution)/shard_map/ppermute | solution.py:141
  25.8 0.0 all-to-all-done.qd
  25.8 1.9 %collective-permute-done.halo = bf16[4,128,128]{2,1,0:T(8,128)(2,1)S(1)} collective-permute-done((bf16[4,128,128]{2,1,0:T(8,128)(2,1)S(1)}, bf16[4,128,128]{2,1,0:T(8,128)(2,1)S(1)}, u32[]{:S(2)}, u32[]{:S(2)}) %collective-permute-start) | collective-permute-done | bytes 131104 | tf_op jit(solution)/shard_map/ppermute | solution.py:141
  27.7 3.8 %shard_map.86 = (bf16[4,128,128]{2,1,0:T(8,128)(2,1)S(1)}, f32[512,128]{1,0:T(8,128)S(1)}, f32[512,64]{1,0:T(8,128)S(1)}, f32[32,8,128]{2,1,0:T(8,128)S(1)}) custom-call(s32[1]{0:T(128)} %bitcast.flag, bf16[4,128,128]{2,1,0:T(8,128)(2,1)S(1)} %all-to-all-done.qd, bf16[4,128,128]{2,1,0:T(8,128)(2,1)S(1)} %all-to-all-done.1.own, ...), custom_call_target="tpu_custom_call" | custom-call | tf_op jit(solution)/shard_map/pallas_call | solution.py:24
  31.5 19.4 %all_to_all.30 = f32[32,8,128]{2,1,0:T(8,128)S(1)} all-to-all(f32[32,8,128]{2,1,0:T(8,128)S(1)} %get-tuple-element.21), channel_id=1, replica_groups=mesh['y'=4,'zg'=4,'zi'=4,'x'=4,'core'=2] {'y','x','core'}, dimensions={0} | all-to-all | bytes 262144 | tf_op jit(solution)/shard_map/all_to_all | solution.py:170
  51.0 0.6 tile.4
  51.6 17.1 %all-to-all-start.4 = ((f32[16,8,128]{2,1,0:T(8,128)}), f32[16,8,128]{2,1,0:T(8,128)S(1)}, u32[]{:S(2)}, u32[]{:S(2)}) async-start(f32[16,8,128]{2,1,0:T(8,128)} %tile.4), calls=%async_computation.4 | async-start | bytes 131072 | tf_op jit(solution)/shard_map/all_to_all | solution.py:170
  68.8 1.3 %collective-permute-start.1 = (bf16[4,128,128]{2,1,0:T(8,128)(2,1)S(1)}, bf16[4,128,128]{2,1,0:T(8,128)(2,1)S(1)}, u32[]{:S(2)}, u32[]{:S(2)}) collective-permute-start(bf16[4,128,128]{2,1,0:T(8,128)(2,1)S(1)} %get-tuple-element.17), channel_id=1, source_target_pairs={{32,0},{40,8},{48,16},{56,24},{64,32},{72,40},{80,48},{88,56},{96,... | collective-permute-start | bytes 393224 | tf_op jit(solution)/shard_map/ppermute | solution.py:158
  70.1 10.3 %all-to-all-done.4 = f32[16,8,128]{2,1,0:T(8,128)S(1)} async-done(((f32[16,8,128]{2,1,0:T(8,128)}), f32[16,8,128]{2,1,0:T(8,128)S(1)}, u32[]{:S(2)}, u32[]{:S(2)}) %all-to-all-start.4) | async-done | bytes 65568 | tf_op jit(solution)/shard_map/all_to_all | solution.py:170
  80.4 0.7 tile.5
  81.0 5.7 %all-to-all-start.5 = ((f32[32,8,128]{2,1,0:T(8,128)}), f32[32,8,128]{2,1,0:T(8,128)S(1)}, u32[]{:S(2)}, u32[]{:S(2)}) async-start(f32[32,8,128]{2,1,0:T(8,128)} %tile.5), calls=%async_computation.5 | async-start | bytes 262144 | tf_op jit(solution)/shard_map/all_to_all | solution.py:170
  86.7 3.2 %collective-permute-done.1.back = bf16[4,128,128]{2,1,0:T(8,128)(2,1)S(1)} collective-permute-done((bf16[4,128,128]{2,1,0:T(8,128)(2,1)S(1)}, bf16[4,128,128]{2,1,0:T(8,128)(2,1)S(1)}, u32[]{:S(2)}, u32[]{:S(2)}) %collective-permute-start.1) | collective-permute-done | bytes 131104 | tf_op jit(solution)/shard_map/ppermute | solution.py:158
  90.0 0.8 shard_map.87
  90.7 3.7 %all-to-all-done.5 = f32[32,8,128]{2,1,0:T(8,128)S(1)} async-done(((f32[32,8,128]{2,1,0:T(8,128)}), f32[32,8,128]{2,1,0:T(8,128)S(1)}, u32[]{:S(2)}, u32[]{:S(2)}) %all-to-all-start.5) | async-done | bytes 131104 | tf_op jit(solution)/shard_map/all_to_all | solution.py:170
  94.5 7.4 %all-to-all-start.2 = ((bf16[4,192,128]{2,1,0:T(8,128)(2,1)}), bf16[4,192,128]{2,1,0:T(8,128)(2,1)S(1)}, u32[]{:S(2)}, u32[]{:S(2)}) async-start(bf16[4,192,128]{2,1,0:T(8,128)(2,1)} %shard_map.87), calls=%async_computation.2 | async-start | bytes 393216 | tf_op jit(solution)/shard_map/all_to_all | solution.py:170
  101.8 5.2 %all-to-all-done.2.x = bf16[4,192,128]{2,1,0:T(8,128)(2,1)S(1)} async-done(((bf16[4,192,128]{2,1,0:T(8,128)(2,1)}), bf16[4,192,128]{2,1,0:T(8,128)(2,1)S(1)}, u32[]{:S(2)}, u32[]{:S(2)}) %all-to-all-start.2) | async-done | bytes 196640 | tf_op jit(solution)/shard_map/all_to_all | solution.py:170
  107.0 0.8 shard_map.88
  107.8 0.7 copy.10
  (2 shorter events, 0.1 us)
Async XLA Ops:
  2.2 11.2 %all-to-all-start.1 = ((bf16[4,128,128]{2,1,0:T(8,128)(2,1)}), bf16[4,128,128]{2,1,0:T(8,128)(2,1)S(1)}, u32[]{:S(2)}, u32[]{:S(2)}) async-start(bf16[4,128,128]{2,1,0:T(8,128)(2,1)} %shard_map.85), calls=%async_computation.1 | async-start | bytes 262144 | tf_op jit(solution)/shard_map/all_to_all | solution.py:170
  13.5 12.3 %all-to-all-start = ((bf16[4,128,128]{2,1,0:T(8,128)(2,1)}), bf16[4,128,128]{2,1,0:T(8,128)(2,1)S(1)}, u32[]{:S(2)}, u32[]{:S(2)}) async-start(bf16[4,128,128]{2,1,0:T(8,128)(2,1)} %get-tuple-element.13), calls=%async_computation | async-start | bytes 262144 | tf_op jit(solution)/shard_map/all_to_all | solution.py:170
  16.8 10.9 %collective-permute-start = (bf16[4,128,128]{2,1,0:T(8,128)(2,1)S(1)}, bf16[4,128,128]{2,1,0:T(8,128)(2,1)S(1)}, u32[]{:S(2)}, u32[]{:S(2)}) collective-permute-start(bf16[4,128,128]{2,1,0:T(8,128)(2,1)S(1)} %all-to-all-done.1.own), channel_id=1, source_target_pairs={{0,32},{8,40},{16,48},{24,56},{32,64},{40,72},{48,80},{56,88},{64,... | collective-permute-start | bytes 393224 | tf_op jit(solution)/shard_map/ppermute | solution.py:141
  51.6 28.7 %all-to-all-start.4 = ((f32[16,8,128]{2,1,0:T(8,128)}), f32[16,8,128]{2,1,0:T(8,128)S(1)}, u32[]{:S(2)}, u32[]{:S(2)}) async-start(f32[16,8,128]{2,1,0:T(8,128)} %tile.4), calls=%async_computation.4 | async-start | bytes 131072 | tf_op jit(solution)/shard_map/all_to_all | solution.py:170
  68.8 21.2 %collective-permute-start.1 = (bf16[4,128,128]{2,1,0:T(8,128)(2,1)S(1)}, bf16[4,128,128]{2,1,0:T(8,128)(2,1)S(1)}, u32[]{:S(2)}, u32[]{:S(2)}) collective-permute-start(bf16[4,128,128]{2,1,0:T(8,128)(2,1)S(1)} %get-tuple-element.17), channel_id=1, source_target_pairs={{32,0},{40,8},{48,16},{56,24},{64,32},{72,40},{80,48},{88,56},{96,... | collective-permute-start | bytes 393224 | tf_op jit(solution)/shard_map/ppermute | solution.py:158
  81.0 13.4 %all-to-all-start.5 = ((f32[32,8,128]{2,1,0:T(8,128)}), f32[32,8,128]{2,1,0:T(8,128)S(1)}, u32[]{:S(2)}, u32[]{:S(2)}) async-start(f32[32,8,128]{2,1,0:T(8,128)} %tile.5), calls=%async_computation.5 | async-start | bytes 262144 | tf_op jit(solution)/shard_map/all_to_all | solution.py:170
  94.5 12.6 %all-to-all-start.2 = ((bf16[4,192,128]{2,1,0:T(8,128)(2,1)}), bf16[4,192,128]{2,1,0:T(8,128)(2,1)S(1)}, u32[]{:S(2)}, u32[]{:S(2)}) async-start(bf16[4,192,128]{2,1,0:T(8,128)(2,1)} %shard_map.87), calls=%async_computation.2 | async-start | bytes 393216 | tf_op jit(solution)/shard_map/all_to_all | solution.py:170

commit v3 on v2

--- a/solution.py
+++ b/solution.py
@@ -21,7 +21,7 @@
 def call(body, outs, *args, **kw):
     args = [near(a) if a.ndim == 3 else a for a in args]
     shapes = [pltpu.VMEM(s, d) if v else jax.ShapeDtypeStruct(s, d) for s, d, v in outs]
-    return pl.pallas_call(body, out_shape=shapes, **kw)(*args)
+    return list(pl.pallas_call(body, out_shape=shapes, **kw)(*args))
 
 
 def near(x):
@@ -115,17 +115,20 @@
             gemb[d * BLOCKS + b] = block[d * 8 : (d + 1) * 8]
 
 
-def out_pack_body(gown, gq, back, out):
-    gkv = gown[...].reshape(GROUP, TOK, 2 * HEAD_DIM) + back[...].astype(F32)
+def out_pack_body(place, gown, gq, back, *outs):
     half = TOK // 2
-    for g in range(GROUP):
-        rows = gq[g * TOK : (g + 1) * TOK]
-        out[g, :TOK] = gkv[g].astype(BF16)
-        out[g, TOK:] = jnp.concatenate([rows[:half], rows[half:]], axis=1).astype(BF16)
+    for m, out in enumerate(outs):
+        g = place[0] ^ m
+        rows = pl.ds(pl.multiple_of(g * TOK, TOK), TOK)
+        out[:TOK] = (gown[rows] + back[g].astype(F32)).astype(BF16)
+        rows = gq[rows]
+        out[TOK:] = jnp.concatenate([rows[:half], rows[half:]], axis=1).astype(BF16)
 
 
-def unpack_body(x, gq, gk, gv):
+def unpack_body(place, x0, x1, x2, x3, gq, gk, gv, x):
     half = TOK // 2
+    for m, part in enumerate((x0, x1, x2, x3)):
+        x[place[0] ^ m] = part[...]
     gk[...] = jnp.concatenate([x[h, :TOK, :HEAD_DIM] for h in range(GROUP)], axis=1)
     gv[...] = jnp.concatenate([x[h, :TOK, HEAD_DIM:] for h in range(GROUP)], axis=1)
     gq[:half] = jnp.concatenate([x[h, TOK:, :HEAD_DIM] for h in range(GROUP)], axis=1)
@@ -160,9 +163,19 @@
     part = jnp.sum(spread(part, line), axis=0)
     whole = spread(part, plane)
     grad_embed_t = whole.reshape(8, BLOCKS, 8, 128).transpose(0, 2, 1, 3).reshape(HEAD_DIM, BAND)
-    (out,) = call(out_pack_body, [((GROUP, TOK + TOK // 2, 2 * HEAD_DIM), BF16, True)], near(gown), near(gq), back)
-    out = exchange(out, "zi")
-    grad_query, grad_key, grad_value = call(unpack_body, [((TOK, GROUP * HEAD_DIM), BF16, False)] * 3, out)
+    place = lax.axis_index("zi").reshape(1)
+    slot = ((TOK + TOK // 2, 2 * HEAD_DIM), BF16, True)
+    sm = pl.BlockSpec(memory_space=pltpu.SMEM)
+    outs = call(out_pack_body, [slot] * GROUP, place, near(gown), near(gq), back, in_specs=[sm, vm, vm, vm])
+    for m in range(1, GROUP):
+        outs[m] = lax.ppermute(outs[m], seq, [(s, s ^ m) for s in range(n)])
+    grad_query, grad_key, grad_value = call(
+        unpack_body,
+        [((TOK, GROUP * HEAD_DIM), BF16, False)] * 3,
+        place, *[near(x) for x in outs],
+        in_specs=[sm] + [vm] * GROUP,
+        scratch_shapes=[pltpu.VMEM((GROUP, TOK + TOK // 2, 2 * HEAD_DIM), BF16)],
+    )
     return grad_query, grad_key, grad_value, grad_embed_t.T
 
 

time: 110 us -> 107 us (0.973)
  waiting for transfers between devices: 27.4 us -> 22.9 us
  starting transfers between devices: 50.2 us -> 52.1 us
    ppermute x0 -> x3, starting transfers between devices: none -> 9.3 us  [local(): outs[m] = lax.ppermute(outs[m], seq, [(s, s ^ m) for s in range(n)])]
    all_to_all x5 -> x4, waiting for transfers between devices: 22.3 us -> 13.4 us  [exchange(): return lax.all_to_all(x, axes, 0, 0, tiled=True)]
    all_to_all x5 -> x4, starting transfers between devices: 39.9 us -> 32.6 us  [exchange(): return lax.all_to_all(x, axes, 0, 0, tiled=True)]
    ppermute x0 -> x3, waiting for transfers between devices: none -> 4.42 us  [local(): outs[m] = lax.ppermute(outs[m], seq, [(s, s ^ m) for s in range(n)])]
  transfers between devices with their start and end apart: 7 -> 9, of which waited for: 6 -> 6; matrix products, arithmetic and copies ran while one was open for 1% -> 1% of each run, Pallas kernels for 2% -> 2%
where the time goes in v3:
time: 107 us; the launch traced here: 105 us
  starting transfers between devices  52.1 us (49%)
  waiting for transfers between devices  22.9 us (21%)
  blocking collectives  19.4 us (18%)
  Pallas kernels  7.99 us (7%)
  local copies, waits for them, and re-layouts  1.96 us (2%)
    all_to_all x4, starting transfers between devices, exchange(): return lax.all_to_all(x, axes, 0, 0, tiled=True)  32.6 us
    all_to_all x1, blocking collectives, exchange(): return lax.all_to_all(x, axes, 0, 0, tiled=True)  19.4 us
    all_to_all x4, waiting for transfers between devices, exchange(): return lax.all_to_all(x, axes, 0, 0, tiled=True)  13.4 us
    ppermute x3, starting transfers between devices, local(): outs[m] = lax.ppermute(outs[m], seq, [(s, s ^ m) for s in range(n)])  9.3 us
    ppermute x1, starting transfers between devices, local(): halo = lax.ppermute(kv, seq, [(s, s + GROUP) for s in range(n - GROUP)])  8.98 us
    pallas_call x5, Pallas kernels, call(): return list(pl.pallas_call(body, out_shape=shapes, **kw)(*args))  7.99 us
    ppermute x3, waiting for transfers between devices, local(): outs[m] = lax.ppermute(outs[m], seq, [(s, s ^ m) for s in range(n)])  4.42 us
    ppermute x1, waiting for transfers between devices, local(): back = lax.ppermute(ghalo, seq, [(s, s - GROUP) for s in range(GROUP, n)])  3.23 us
  transfers between devices with their start and end apart: 9, of which 6 were waited for; matrix products, arithmetic and copies ran while one was open for 1% of the time, Pallas kernels for 2%

profile of v3, /device:TPU:1, one launch (start us, length us, event | category | flops | bytes accessed | tf_op | source)
XLA Modules:
  0.0 105.2 jit_solution(17364134994208150461)
XLA Ops:
  0.6 1.6 %shard_map.85 = bf16[4,128,128]{2,1,0:T(8,128)(2,1)} custom-call(bf16[128,256]{1,0:T(8,128)(2,1)} %k.1, bf16[128,256]{1,0:T(8,128)(2,1)} %v.1), custom_call_target="tpu_custom_call" | custom-call | tf_op jit(solution)/shard_map/pallas_call | solution.py:24
  2.2 6.4 %all-to-all-start.1 = ((bf16[4,128,128]{2,1,0:T(8,128)(2,1)}), bf16[4,128,128]{2,1,0:T(8,128)(2,1)S(1)}, u32[]{:S(2)}, u32[]{:S(2)}) async-start(bf16[4,128,128]{2,1,0:T(8,128)(2,1)} %shard_map.85), calls=%async_computation.1 | async-start | bytes 262144 | tf_op jit(solution)/shard_map/all_to_all | solution.py:183
  8.7 1.7 %shard_map.84 = (bf16[4,128,128]{2,1,0:T(8,128)(2,1)}, bf16[64,512]{1,0:T(8,128)(2,1)S(1)}) custom-call(bf16[128,256]{1,0:T(8,128)(2,1)} %q.1, bf16[128,256]{1,0:T(8,128)(2,1)} %do.1, bf16[64,512]{1,0:T(8,128)(2,1)} %bitcast.11), custom_call_target="tpu_custom_call" | custom-call | tf_op jit(solution)/shard_map/pallas_call | solution.py:24
  10.4 3.1 %all-to-all-done.1.own = bf16[4,128,128]{2,1,0:T(8,128)(2,1)S(1)} async-done(((bf16[4,128,128]{2,1,0:T(8,128)(2,1)}), bf16[4,128,128]{2,1,0:T(8,128)(2,1)S(1)}, u32[]{:S(2)}, u32[]{:S(2)}) %all-to-all-start.1) | async-done | bytes 131104 | tf_op jit(solution)/shard_map/all_to_all | solution.py:183
  13.4 3.3 %all-to-all-start = ((bf16[4,128,128]{2,1,0:T(8,128)(2,1)}), bf16[4,128,128]{2,1,0:T(8,128)(2,1)S(1)}, u32[]{:S(2)}, u32[]{:S(2)}) async-start(bf16[4,128,128]{2,1,0:T(8,128)(2,1)} %get-tuple-element.17), calls=%async_computation | async-start | bytes 262144 | tf_op jit(solution)/shard_map/all_to_all | solution.py:183
  16.8 9.0 %collective-permute-start = (bf16[4,128,128]{2,1,0:T(8,128)(2,1)S(1)}, bf16[4,128,128]{2,1,0:T(8,128)(2,1)S(1)}, u32[]{:S(2)}, u32[]{:S(2)}) collective-permute-start(bf16[4,128,128]{2,1,0:T(8,128)(2,1)S(1)} %all-to-all-done.1.own), channel_id=1, source_target_pairs={{0,32},{8,40},{16,48},{24,56},{32,64},{40,72},{48,80},{56,88},{64,... | collective-permute-start | bytes 393224 | tf_op jit(solution)/shard_map/ppermute | solution.py:144
  25.8 0.0 all-to-all-done.qd
  25.8 1.9 %collective-permute-done.halo = bf16[4,128,128]{2,1,0:T(8,128)(2,1)S(1)} collective-permute-done((bf16[4,128,128]{2,1,0:T(8,128)(2,1)S(1)}, bf16[4,128,128]{2,1,0:T(8,128)(2,1)S(1)}, u32[]{:S(2)}, u32[]{:S(2)}) %collective-permute-start) | collective-permute-done | bytes 131104 | tf_op jit(solution)/shard_map/ppermute | solution.py:144
  27.7 3.8 %shard_map.86 = (bf16[4,128,128]{2,1,0:T(8,128)(2,1)S(1)}, f32[512,128]{1,0:T(8,128)S(1)}, f32[512,64]{1,0:T(8,128)S(1)}, f32[32,8,128]{2,1,0:T(8,128)S(1)}) custom-call(s32[1]{0:T(128)} %bitcast.1.flag, bf16[4,128,128]{2,1,0:T(8,128)(2,1)S(1)} %all-to-all-done.qd, bf16[4,128,128]{2,1,0:T(8,128)(2,1)S(1)} %all-to-all-done.1.own, ...), custom_call_target="tpu_custom_call" | custom-call | tf_op jit(solution)/shard_map/pallas_call | solution.py:24
  31.5 19.4 %all_to_all.25 = f32[32,8,128]{2,1,0:T(8,128)S(1)} all-to-all(f32[32,8,128]{2,1,0:T(8,128)S(1)} %get-tuple-element.29), channel_id=1, replica_groups=mesh['y'=4,'zg'=4,'zi'=4,'x'=4,'core'=2] {'y','x','core'}, dimensions={0} | all-to-all | bytes 262144 | tf_op jit(solution)/shard_map/all_to_all | solution.py:183
  51.0 0.6 tile.4
  51.6 17.1 %all-to-all-start.3 = ((f32[16,8,128]{2,1,0:T(8,128)}), f32[16,8,128]{2,1,0:T(8,128)S(1)}, u32[]{:S(2)}, u32[]{:S(2)}) async-start(f32[16,8,128]{2,1,0:T(8,128)} %tile.4), calls=%async_computation.3 | async-start | bytes 131072 | tf_op jit(solution)/shard_map/all_to_all | solution.py:183
  68.8 1.3 %collective-permute-start.1 = (bf16[4,128,128]{2,1,0:T(8,128)(2,1)S(1)}, bf16[4,128,128]{2,1,0:T(8,128)(2,1)S(1)}, u32[]{:S(2)}, u32[]{:S(2)}) collective-permute-start(bf16[4,128,128]{2,1,0:T(8,128)(2,1)S(1)} %get-tuple-element.21), channel_id=1, source_target_pairs={{32,0},{40,8},{48,16},{56,24},{64,32},{72,40},{80,48},{88,56},{96,... | collective-permute-start | bytes 393224 | tf_op jit(solution)/shard_map/ppermute | solution.py:161
  70.1 10.3 %all-to-all-done.3 = f32[16,8,128]{2,1,0:T(8,128)S(1)} async-done(((f32[16,8,128]{2,1,0:T(8,128)}), f32[16,8,128]{2,1,0:T(8,128)S(1)}, u32[]{:S(2)}, u32[]{:S(2)}) %all-to-all-start.3) | async-done | bytes 65568 | tf_op jit(solution)/shard_map/all_to_all | solution.py:183
  80.4 0.7 tile.5
  81.0 5.7 %all-to-all-start.4 = ((f32[32,8,128]{2,1,0:T(8,128)}), f32[32,8,128]{2,1,0:T(8,128)S(1)}, u32[]{:S(2)}, u32[]{:S(2)}) async-start(f32[32,8,128]{2,1,0:T(8,128)} %tile.5), calls=%async_computation.4 | async-start | bytes 262144 | tf_op jit(solution)/shard_map/all_to_all | solution.py:183
  86.7 3.2 %collective-permute-done.1.back = bf16[4,128,128]{2,1,0:T(8,128)(2,1)S(1)} collective-permute-done((bf16[4,128,128]{2,1,0:T(8,128)(2,1)S(1)}, bf16[4,128,128]{2,1,0:T(8,128)(2,1)S(1)}, u32[]{:S(2)}, u32[]{:S(2)}) %collective-permute-start.1) | collective-permute-done | bytes 131104 | tf_op jit(solution)/shard_map/ppermute | solution.py:161
  90.0 0.1 shard_map.87
  90.1 3.4 %collective-permute-start.2 = (bf16[192,128]{1,0:T(8,128)(2,1)S(1)}, bf16[192,128]{1,0:T(8,128)(2,1)S(1)}, u32[]{:S(2)}, u32[]{:S(2)}) collective-permute-start(bf16[192,128]{1,0:T(8,128)(2,1)S(1)} %get-tuple-element.23), channel_id=1, source_target_pairs={{0,8},{8,0},{16,24},{24,16},{32,40},{40,32},{48,56},{56,48},{64,72... | collective-permute-start | bytes 147464 | tf_op jit(solution)/shard_map/ppermute | solution.py:171
  93.5 3.7 %collective-permute-start.3 = (bf16[192,128]{1,0:T(8,128)(2,1)S(1)}, bf16[192,128]{1,0:T(8,128)(2,1)S(1)}, u32[]{:S(2)}, u32[]{:S(2)}) collective-permute-start(bf16[192,128]{1,0:T(8,128)(2,1)S(1)} %get-tuple-element.24), channel_id=1, source_target_pairs={{0,16},{8,24},{16,0},{24,8},{32,48},{40,56},{48,32},{56,40},{64,80... | collective-permute-start | bytes 147464 | tf_op jit(solution)/shard_map/ppermute | solution.py:171
  97.2 2.2 %collective-permute-start.4 = (bf16[192,128]{1,0:T(8,128)(2,1)S(1)}, bf16[192,128]{1,0:T(8,128)(2,1)S(1)}, u32[]{:S(2)}, u32[]{:S(2)}) collective-permute-start(bf16[192,128]{1,0:T(8,128)(2,1)S(1)} %get-tuple-element.25), channel_id=1, source_target_pairs={{0,24},{8,16},{16,8},{24,0},{32,56},{40,48},{48,40},{56,32},{64,88... | collective-permute-start | bytes 147464 | tf_op jit(solution)/shard_map/ppermute | solution.py:171
  99.4 0.0 collective-permute-done.2.x1
  99.4 0.1 collective-permute-done.3.x2
  99.4 4.4 %collective-permute-done.4.x3 = bf16[192,128]{1,0:T(8,128)(2,1)S(1)} collective-permute-done((bf16[192,128]{1,0:T(8,128)(2,1)S(1)}, bf16[192,128]{1,0:T(8,128)(2,1)S(1)}, u32[]{:S(2)}, u32[]{:S(2)}) %collective-permute-start.4) | collective-permute-done | bytes 49184 | tf_op jit(solution)/shard_map/ppermute | solution.py:171
  103.8 0.8 shard_map.88
  104.6 0.0 all-to-all-done.4
  104.6 0.7 copy.10
  (2 shorter events, 0.1 us)
Async XLA Ops:
  2.2 11.2 %all-to-all-start.1 = ((bf16[4,128,128]{2,1,0:T(8,128)(2,1)}), bf16[4,128,128]{2,1,0:T(8,128)(2,1)S(1)}, u32[]{:S(2)}, u32[]{:S(2)}) async-start(bf16[4,128,128]{2,1,0:T(8,128)(2,1)} %shard_map.85), calls=%async_computation.1 | async-start | bytes 262144 | tf_op jit(solution)/shard_map/all_to_all | solution.py:183
  13.4 12.3 %all-to-all-start = ((bf16[4,128,128]{2,1,0:T(8,128)(2,1)}), bf16[4,128,128]{2,1,0:T(8,128)(2,1)S(1)}, u32[]{:S(2)}, u32[]{:S(2)}) async-start(bf16[4,128,128]{2,1,0:T(8,128)(2,1)} %get-tuple-element.17), calls=%async_computation | async-start | bytes 262144 | tf_op jit(solution)/shard_map/all_to_all | solution.py:183
  16.8 10.9 %collective-permute-start = (bf16[4,128,128]{2,1,0:T(8,128)(2,1)S(1)}, bf16[4,128,128]{2,1,0:T(8,128)(2,1)S(1)}, u32[]{:S(2)}, u32[]{:S(2)}) collective-permute-start(bf16[4,128,128]{2,1,0:T(8,128)(2,1)S(1)} %all-to-all-done.1.own), channel_id=1, source_target_pairs={{0,32},{8,40},{16,48},{24,56},{32,64},{40,72},{48,80},{56,88},{64,... | collective-permute-start | bytes 393224 | tf_op jit(solution)/shard_map/ppermute | solution.py:144
  51.6 28.7 %all-to-all-start.3 = ((f32[16,8,128]{2,1,0:T(8,128)}), f32[16,8,128]{2,1,0:T(8,128)S(1)}, u32[]{:S(2)}, u32[]{:S(2)}) async-start(f32[16,8,128]{2,1,0:T(8,128)} %tile.4), calls=%async_computation.3 | async-start | bytes 131072 | tf_op jit(solution)/shard_map/all_to_all | solution.py:183
  68.8 21.2 %collective-permute-start.1 = (bf16[4,128,128]{2,1,0:T(8,128)(2,1)S(1)}, bf16[4,128,128]{2,1,0:T(8,128)(2,1)S(1)}, u32[]{:S(2)}, u32[]{:S(2)}) collective-permute-start(bf16[4,128,128]{2,1,0:T(8,128)(2,1)S(1)} %get-tuple-element.21), channel_id=1, source_target_pairs={{32,0},{40,8},{48,16},{56,24},{64,32},{72,40},{80,48},{88,56},{96,... | collective-permute-start | bytes 393224 | tf_op jit(solution)/shard_map/ppermute | solution.py:161
  81.0 23.6 %all-to-all-start.4 = ((f32[32,8,128]{2,1,0:T(8,128)}), f32[32,8,128]{2,1,0:T(8,128)S(1)}, u32[]{:S(2)}, u32[]{:S(2)}) async-start(f32[32,8,128]{2,1,0:T(8,128)} %tile.5), calls=%async_computation.4 | async-start | bytes 262144 | tf_op jit(solution)/shard_map/all_to_all | solution.py:183
  90.1 9.3 %collective-permute-start.2 = (bf16[192,128]{1,0:T(8,128)(2,1)S(1)}, bf16[192,128]{1,0:T(8,128)(2,1)S(1)}, u32[]{:S(2)}, u32[]{:S(2)}) collective-permute-start(bf16[192,128]{1,0:T(8,128)(2,1)S(1)} %get-tuple-element.23), channel_id=1, source_target_pairs={{0,8},{8,0},{16,24},{24,16},{32,40},{40,32},{48,56},{56,48},{64,72... | collective-permute-start | bytes 147464 | tf_op jit(solution)/shard_map/ppermute | solution.py:171
  93.5 6.0 %collective-permute-start.3 = (bf16[192,128]{1,0:T(8,128)(2,1)S(1)}, bf16[192,128]{1,0:T(8,128)(2,1)S(1)}, u32[]{:S(2)}, u32[]{:S(2)}) collective-permute-start(bf16[192,128]{1,0:T(8,128)(2,1)S(1)} %get-tuple-element.24), channel_id=1, source_target_pairs={{0,16},{8,24},{16,0},{24,8},{32,48},{40,56},{48,32},{56,40},{64,80... | collective-permute-start | bytes 147464 | tf_op jit(solution)/shard_map/ppermute | solution.py:171
  97.2 6.6 %collective-permute-start.4 = (bf16[192,128]{1,0:T(8,128)(2,1)S(1)}, bf16[192,128]{1,0:T(8,128)(2,1)S(1)}, u32[]{:S(2)}, u32[]{:S(2)}) collective-permute-start(bf16[192,128]{1,0:T(8,128)(2,1)S(1)} %get-tuple-element.25), channel_id=1, source_target_pairs={{0,24},{8,16},{16,8},{24,0},{32,56},{40,48},{48,40},{56,32},{64,88... | collective-permute-start | bytes 147464 | tf_op jit(solution)/shard_map/ppermute | solution.py:171

commit v4 on v2

v4 whole, which is shorter than its diff:
```python
import jax
import jax.numpy as jnp
from jax import lax
from jax.experimental import pallas as pl
from jax.experimental.pallas import tpu as pltpu
from jax.sharding import PartitionSpec as P


HEAD_DIM = 64
BAND = 512
TOK = 128
REACH = BAND // TOK
SPAN = BAND + TOK
PAIR = 2 * HEAD_DIM
PAIRS = 2
ROWS = 2 * TOK
WIDE = PAIRS * PAIR
DIMS = (4, 4, 4, 4, 2)
SCALE = HEAD_DIM ** (-0.5)
F32 = jnp.float32
BF16 = jnp.bfloat16
NN = ((1,), (0,))
NT = ((1,), (1,))
TN = ((0,), (0,))


def call(body, outs, *args, **kw):
    shapes = [pltpu.VMEM(s, d) if v else jax.ShapeDtypeStruct(s, d) for s, d, v in outs]
    return list(pl.pallas_call(body, out_shape=shapes, **kw)(*args))


def near(x):
    return pltpu.with_memory_space_constraint(x, pltpu.VMEM)


def mm(a, b, dims):
    return lax.dot_general(a, b, (dims, ((), ())), preferred_element_type=F32)


def span(block):
    return slice(block * TOK, (block + 1) * TOK)


def flip_matrix(count):
    row = lax.broadcasted_iota(jnp.int32, (count, count), 0)
    col = lax.broadcasted_iota(jnp.int32, (count, count), 1)
    same = row // TOK == col // TOK
    return jnp.where(same & (row % TOK + col % TOK == TOK - 1), 1.0, 0.0).astype(BF16)


def skew(x, shift):
    halves = [pltpu.roll(x[span(b)], shift, 1, stride=1, stride_axis=0) for b in range(2)]
    return jnp.concatenate(halves, axis=0)


def stack_heads(x):
    low = lax.broadcasted_iota(jnp.int32, x.shape, 1) < HEAD_DIM
    zero = jnp.zeros_like(x)
    return jnp.concatenate([jnp.where(low, x, zero), jnp.where(low, zero, x)], axis=0)


def join_heads(x):
    low = lax.broadcasted_iota(jnp.int32, (TOK, PAIR), 1) < HEAD_DIM
    return jnp.where(low, x[:TOK], x[TOK:])


def early_body(q, do, emb_t, qs, dos, erev):
    flip = flip_matrix(TOK)
    for b in range(REACH):
        back = mm(emb_t[:, span(REACH - 1 - b)], flip, NN).astype(BF16)
        erev[:HEAD_DIM, span(b)] = back
        erev[HEAD_DIM:, span(b)] = back
    for p in range(PAIRS):
        lanes = slice(p * PAIR, (p + 1) * PAIR)
        qs[p] = stack_heads(q[:, lanes])
        dos[p] = stack_heads(do[:, lanes])


def main_body(first, qs, dos, erev, kv0, kv1, kv2, kv3, kv4, gq, far, d2, d1, d0, gemb):
    flip = flip_matrix(ROWS)
    row = lax.broadcasted_iota(jnp.int32, (ROWS, SPAN), 0) % TOK
    col = lax.broadcasted_iota(jnp.int32, (ROWS, SPAN), 1)
    ahead = col - row - 1
    valid = (ahead >= 0) & (ahead < BAND) & (col >= first[0])
    total = jnp.zeros((PAIR, BAND), F32)
    for p in range(PAIRS):
        k_lanes = slice(p * PAIR, (p + 1) * PAIR)
        v_lanes = slice(WIDE + p * PAIR, WIDE + (p + 1) * PAIR)
        blocks = (kv4, kv3, kv2, kv1, kv0)
        k = jnp.concatenate([x[:, k_lanes] for x in blocks], axis=0)
        v = jnp.concatenate([x[:, v_lanes] for x in blocks], axis=0)
        q, do = qs[p], dos[p]
        along = jnp.concatenate([mm(q, erev[...], NN), jnp.zeros((ROWS, TOK), F32)], axis=1)
        s = (skew(along, 1) + mm(q, k, NT)) * SCALE
        s = jnp.where(valid, s, -jnp.inf)
        dp = mm(do, v, NT)
        prob = jnp.exp(s - jnp.max(s, axis=1, keepdims=True))
        prob = prob * (1.0 / jnp.sum(prob, axis=1, keepdims=True))
        prob_b = prob.astype(BF16)
        delta = jnp.sum(prob_b.astype(F32) * dp, axis=1, keepdims=True)
        ds = (prob * (dp - delta) * SCALE).astype(BF16)
        dalong = skew(mm(flip, ds, NN), BAND)[:, :BAND].astype(BF16)
        total = total + mm(mm(flip, q, NN).astype(BF16), dalong, TN)
        for part, lanes in ((mm(ds, q, TN), k_lanes), (mm(prob_b, do, TN), v_lanes)):
            far[:TOK, lanes] = part[span(0)].astype(BF16)
            far[TOK:, lanes] = part[span(1)].astype(BF16)
            d2[:, lanes] = part[span(2)]
            d1[:, lanes] = part[span(3)]
            d0[:, lanes] = part[span(4)]
        gqe = mm(dalong, erev[...], NT)
        hi = gqe.astype(BF16)
        lo = (gqe - hi.astype(F32)).astype(BF16)
        g = mm(ds, k, NN) + mm(flip, hi, NN) + mm(flip, lo, NN)
        gq[:, k_lanes] = join_heads(g).astype(BF16)
    total = total[:HEAD_DIM] + total[HEAD_DIM:]
    flip = flip_matrix(TOK)
    for b in range(REACH):
        block = total[:, span(REACH - 1 - b)]
        hi = block.astype(BF16)
        lo = (block - hi.astype(F32)).astype(BF16)
        block = mm(hi, flip, NN) + mm(lo, flip, NN)
        for d in range(HEAD_DIM // 8):
            gemb[d * REACH + b] = block[d * 8 : (d + 1) * 8]


def add_body(far, d2, d1, e2, e1):
    e2[...] = (d2[...] + far[:TOK].astype(F32)).astype(BF16)
    e1[...] = (d1[...] + far[TOK:].astype(F32)).astype(BF16)


def last_body(d0, r2, r1, gk, gv):
    g = (d0[...] + r2[...].astype(F32) + r1[...].astype(F32)).astype(BF16)
    gk[...] = g[:, :WIDE]
    gv[...] = g[:, WIDE:]


def join_body(k, v, out):
    out[:, :WIDE] = k[...]
    out[:, WIDE:] = v[...]


SEQ = ("y", "zg", "zi")


def shift(x, steps):
    n = lax.axis_size(SEQ)
    return lax.ppermute(x, SEQ, [(s, s + steps) for s in range(max(0, -steps), min(n, n - steps))])


def exchange(x, axes):
    return lax.all_to_all(x, axes, 0, 0, tiled=True)


def spread(x, axes):
    return exchange(jnp.tile(x, (lax.axis_size(axes), 1, 1)), axes)


def local(query, key_rows, value_matrix_rows, grad_out, rel_embed):
    line, plane = ("zg", "zi"), ("y", "x", "core")
    block = (TOK, 2 * WIDE)
    (kv0,) = call(join_body, [(block, BF16, True)], key_rows, value_matrix_rows)
    kvs = [kv0]
    for _ in range(1, REACH + 1):
        kvs.append(shift(kvs[-1], 1))
    kvs = [near(x) for x in kvs]
    tall = (PAIRS, ROWS, PAIR)
    qs, dos, erev = call(
        early_body,
        [(tall, BF16, True), (tall, BF16, True), ((PAIR, BAND), BF16, True)],
        query, grad_out, rel_embed.T,
    )
    qs, dos = near(qs), near(dos)
    first = (TOK * jnp.maximum(REACH - lax.axis_index(SEQ), 0)).astype(jnp.int32).reshape(1)
    vm = pl.BlockSpec(memory_space=pltpu.VMEM)
    grad_query, far, d2, d1, d0, gemb = call(
        main_body,
        [((TOK, WIDE), BF16, False), ((2 * TOK, 2 * WIDE), BF16, True)]
        + [(block, F32, True)] * 3
        + [((lax.axis_size(plane), 8, 128), F32, True)],
        first, qs, dos, near(erev), *kvs,
        in_specs=[pl.BlockSpec(memory_space=pltpu.SMEM)] + [vm] * 8,
    )
    part = jnp.sum(exchange(gemb, plane), axis=0)
    part = jnp.sum(spread(part, line), axis=0)
    whole = spread(part, plane)
    grad_embed_t = whole.reshape(8, REACH, 8, 128).transpose(0, 2, 1, 3).reshape(HEAD_DIM, BAND)
    far = shift(far, -2)
    e2, e1 = call(add_body, [(block, BF16, True)] * 2, near(far), near(d2), near(d1))
    e2 = shift(e2, -2)
    e1 = shift(e1, -1)
    grad_key, grad_value = call(last_body, [((TOK, WIDE), BF16, False)] * 2, near(d0), near(e2), near(e1))
    return grad_query, grad_key, grad_value, grad_embed_t.T


def solution(mesh):
    fine = jax.sharding.Mesh(mesh.devices.reshape(DIMS), ("y", "zg", "zi", "x", "core"))
    rows = P(SEQ, ("x", "core"))
    return jax.shard_map(
        local,
        mesh=fine,
        in_specs=(rows, rows, rows, rows, P()),
        out_specs=(rows, rows, rows, P()),
        check_vma=False,
    )
```

time: 110 us -> 97 us (0.88)
  blocking collectives: 19.4 us -> 0 us
  starting transfers between devices: 50.2 us -> 56.4 us
  waiting for transfers between devices: 27.4 us -> 30.3 us
  Pallas kernels: 8.65 us -> 6.91 us
    all_to_all x1 -> x0, blocking collectives: 19.4 us -> none  [exchange(): return lax.all_to_all(x, axes, 0, 0, tiled=True)]
    ppermute x2 -> x7, starting transfers between devices: 10.3 us -> 19.9 us  [shift(): lax.ppermute(x, SEQ, [(s, s + steps) for s in range(max(0, -steps), min(n...]
    ppermute x2 -> x7, waiting for transfers between devices: 5.13 us -> 9.73 us  [shift(): lax.ppermute(x, SEQ, [(s, s + steps) for s in range(max(0, -steps), min(n...]
    all_to_all x5 -> x3, starting transfers between devices: 39.9 us -> 36.5 us  [exchange(): return lax.all_to_all(x, axes, 0, 0, tiled=True)]
    all_to_all x5 -> x3, waiting for transfers between devices: 22.3 us -> 20.6 us  [exchange(): return lax.all_to_all(x, axes, 0, 0, tiled=True)]
    pallas_call x5, Pallas kernels: 8.65 us -> 6.91 us  [call(): return list(pl.pallas_call(body, out_shape=shapes, **kw)(*args))]
  transfers between devices with their start and end apart: 7 -> 10, of which waited for: 6 -> 8; matrix products, arithmetic and copies ran while one was open for 1% -> 1% of each run, Pallas kernels for 2% -> 2%
where the time goes in v4:
time: 97 us; the launch traced here: 96.4 us
  starting transfers between devices  56.4 us (58%)
  waiting for transfers between devices  30.3 us (31%)
  Pallas kernels  6.91 us (7%)
  local copies, waits for them, and re-layouts  1.96 us (2%)
    all_to_all x3, starting transfers between devices, exchange(): return lax.all_to_all(x, axes, 0, 0, tiled=True)  36.5 us
    all_to_all x3, waiting for transfers between devices, exchange(): return lax.all_to_all(x, axes, 0, 0, tiled=True)  20.6 us
    ppermute x7, starting transfers between devices, shift(): lax.ppermute(x, SEQ, [(s, s + steps) for s in range(max(0, -steps), min(n...  19.9 us
    ppermute x7, waiting for transfers between devices, shift(): lax.ppermute(x, SEQ, [(s, s + steps) for s in range(max(0, -steps), min(n...  9.73 us
    pallas_call x5, Pallas kernels, call(): return list(pl.pallas_call(body, out_shape=shapes, **kw)(*args))  6.91 us
  transfers between devices with their start and end apart: 10, of which 8 were waited for; matrix products, arithmetic and copies ran while one was open for 1% of the time, Pallas kernels for 2%

profile of v4, /device:TPU:1, one launch (start us, length us, event | category | flops | bytes accessed | tf_op | source)
XLA Modules:
  0.0 96.4 jit_solution(5344417078963669048)
XLA Ops:
  0.6 0.9 shard_map.85.kv0
  1.5 4.4 %collective-permute-start = (bf16[128,512]{1,0:T(8,128)(2,1)S(1)}, bf16[128,512]{1,0:T(8,128)(2,1)S(1)}, u32[]{:S(2)}, u32[]{:S(2)}) collective-permute-start(bf16[128,512]{1,0:T(8,128)(2,1)S(1)} %shard_map.85.kv0), channel_id=1, source_target_pairs={{0,8},{8,16},{16,24},{24,32},{32,40},{40,48},{48,56},{56,64},{64,7... | collective-permute-start | bytes 393224 | tf_op jit(solution)/shard_map/ppermute | solution.py:147
  5.9 1.9 %collective-permute-done.kv1 = bf16[128,512]{1,0:T(8,128)(2,1)S(1)} collective-permute-done((bf16[128,512]{1,0:T(8,128)(2,1)S(1)}, bf16[128,512]{1,0:T(8,128)(2,1)S(1)}, u32[]{:S(2)}, u32[]{:S(2)}) %collective-permute-start) | collective-permute-done | bytes 131104 | tf_op jit(solution)/shard_map/ppermute | solution.py:147
  7.8 3.8 %collective-permute-start.1 = (bf16[128,512]{1,0:T(8,128)(2,1)S(1)}, bf16[128,512]{1,0:T(8,128)(2,1)S(1)}, u32[]{:S(2)}, u32[]{:S(2)}) collective-permute-start(bf16[128,512]{1,0:T(8,128)(2,1)S(1)} %collective-permute-done.kv1), channel_id=1, source_target_pairs={{0,8},{8,16},{16,24},{24,32},{32,40},{40,48},{48,56},{56,64},{64,7... | collective-permute-start | bytes 393224 | tf_op jit(solution)/shard_map/ppermute | solution.py:147
  11.6 1.9 %collective-permute-done.1.kv2 = bf16[128,512]{1,0:T(8,128)(2,1)S(1)} collective-permute-done((bf16[128,512]{1,0:T(8,128)(2,1)S(1)}, bf16[128,512]{1,0:T(8,128)(2,1)S(1)}, u32[]{:S(2)}, u32[]{:S(2)}) %collective-permute-start.1) | collective-permute-done | bytes 131104 | tf_op jit(solution)/shard_map/ppermute | solution.py:147
  13.5 4.1 %collective-permute-start.2 = (bf16[128,512]{1,0:T(8,128)(2,1)S(1)}, bf16[128,512]{1,0:T(8,128)(2,1)S(1)}, u32[]{:S(2)}, u32[]{:S(2)}) collective-permute-start(bf16[128,512]{1,0:T(8,128)(2,1)S(1)} %collective-permute-done.1.kv2), channel_id=1, source_target_pairs={{0,8},{8,16},{16,24},{24,32},{32,40},{40,48},{48,56},{56,64},{64,7... | collective-permute-start | bytes 393224 | tf_op jit(solution)/shard_map/ppermute | solution.py:147
  17.6 2.4 %collective-permute-done.2.kv3 = bf16[128,512]{1,0:T(8,128)(2,1)S(1)} collective-permute-done((bf16[128,512]{1,0:T(8,128)(2,1)S(1)}, bf16[128,512]{1,0:T(8,128)(2,1)S(1)}, u32[]{:S(2)}, u32[]{:S(2)}) %collective-permute-start.2) | collective-permute-done | bytes 131104 | tf_op jit(solution)/shard_map/ppermute | solution.py:147
  20.0 3.8 %collective-permute-start.3 = (bf16[128,512]{1,0:T(8,128)(2,1)S(1)}, bf16[128,512]{1,0:T(8,128)(2,1)S(1)}, u32[]{:S(2)}, u32[]{:S(2)}) collective-permute-start(bf16[128,512]{1,0:T(8,128)(2,1)S(1)} %collective-permute-done.2.kv3), channel_id=1, source_target_pairs={{0,8},{8,16},{16,24},{24,32},{32,40},{40,48},{48,56},{56,64},{64,7... | collective-permute-start | bytes 393224 | tf_op jit(solution)/shard_map/ppermute | solution.py:147
  23.8 1.1 %shard_map.84 = (bf16[2,256,128]{2,1,0:T(8,128)(2,1)S(1)}, bf16[2,256,128]{2,1,0:T(8,128)(2,1)S(1)}, bf16[128,512]{1,0:T(8,128)(2,1)S(1)}) custom-call(bf16[128,256]{1,0:T(8,128)(2,1)} %q.1, bf16[128,256]{1,0:T(8,128)(2,1)} %do.1, bf16[64,512]{1,0:T(8,128)(2,1)} %bitcast.10), custom_call_target="tpu_custom_call" | custom-call | tf_op jit(solution)/shard_map/pallas_call | solution.py:29
  24.9 1.9 %collective-permute-done.3.kv4 = bf16[128,512]{1,0:T(8,128)(2,1)S(1)} collective-permute-done((bf16[128,512]{1,0:T(8,128)(2,1)S(1)}, bf16[128,512]{1,0:T(8,128)(2,1)S(1)}, u32[]{:S(2)}, u32[]{:S(2)}) %collective-permute-start.3) | collective-permute-done | bytes 131104 | tf_op jit(solution)/shard_map/ppermute | solution.py:147
  26.9 4.2 %shard_map.86 = (bf16[128,256]{1,0:T(8,128)(2,1)}, bf16[256,512]{1,0:T(8,128)(2,1)S(1)}, f32[128,512]{1,0:T(8,128)S(1)}, f32[128,512]{1,0:T(8,128)S(1)}, f32[128,512]{1,0:T(8,128)S(1)}, /*index=5*/f32[32,8,128]{2,1,0:T(8,128)}) custom-call(s32[1]{0:T(128)} %bitcast.first, bf16[2,256,128]{2,1,0:T(8,128)(2,1)S(1)} %get-tuple-element.17.qs, ...), custom_call_target="tpu_custom_call" | custom-call | tf_op jit(solution)/shard_map/pallas_call | solution.py:29
  31.1 25.0 %all-to-all-start = ((f32[32,8,128]{2,1,0:T(8,128)}), f32[32,8,128]{2,1,0:T(8,128)S(1)}, u32[]{:S(2)}, u32[]{:S(2)}) async-start(f32[32,8,128]{2,1,0:T(8,128)} %get-tuple-element.29), calls=%async_computation | async-start | bytes 262144 | tf_op jit(solution)/shard_map/all_to_all | solution.py:151
  56.1 1.3 %collective-permute-start.4 = (bf16[256,512]{1,0:T(8,128)(2,1)S(1)}, bf16[256,512]{1,0:T(8,128)(2,1)S(1)}, u32[]{:S(2)}, u32[]{:S(2)}) collective-permute-start(bf16[256,512]{1,0:T(8,128)(2,1)S(1)} %get-tuple-element.22), channel_id=1, source_target_pairs={{16,0},{24,8},{32,16},{40,24},{48,32},{56,40},{64,48},{72,56},{80,... | collective-permute-start | bytes 786440 | tf_op jit(solution)/shard_map/ppermute | solution.py:147
  57.4 6.3 %all-to-all-done = f32[32,8,128]{2,1,0:T(8,128)S(1)} async-done(((f32[32,8,128]{2,1,0:T(8,128)}), f32[32,8,128]{2,1,0:T(8,128)S(1)}, u32[]{:S(2)}, u32[]{:S(2)}) %all-to-all-start) | async-done | bytes 131104 | tf_op jit(solution)/shard_map/all_to_all | solution.py:151
  63.7 0.6 tile.4
  64.3 5.7 %all-to-all-start.1 = ((f32[16,8,128]{2,1,0:T(8,128)}), f32[16,8,128]{2,1,0:T(8,128)S(1)}, u32[]{:S(2)}, u32[]{:S(2)}) async-start(f32[16,8,128]{2,1,0:T(8,128)} %tile.4), calls=%async_computation.1 | async-start | bytes 131072 | tf_op jit(solution)/shard_map/all_to_all | solution.py:151
  70.0 1.6 %collective-permute-done.4.far = bf16[256,512]{1,0:T(8,128)(2,1)S(1)} collective-permute-done((bf16[256,512]{1,0:T(8,128)(2,1)S(1)}, bf16[256,512]{1,0:T(8,128)(2,1)S(1)}, u32[]{:S(2)}, u32[]{:S(2)}) %collective-permute-start.4) | collective-permute-done | bytes 262176 | tf_op jit(solution)/shard_map/ppermute | solution.py:147
  71.7 1.3 %collective-permute-start.5 = (bf16[128,512]{1,0:T(8,128)(2,1)S(1)}, bf16[128,512]{1,0:T(8,128)(2,1)S(1)}, u32[]{:S(2)}, u32[]{:S(2)}) collective-permute-start(bf16[128,512]{1,0:T(8,128)(2,1)S(1)} %get-tuple-element.25), channel_id=1, source_target_pairs={{16,0},{24,8},{32,16},{40,24},{48,32},{56,40},{64,48},{72,56},{80,... | collective-permute-start | bytes 393224 | tf_op jit(solution)/shard_map/ppermute | solution.py:147
  73.0 1.3 %collective-permute-start.6 = (bf16[128,512]{1,0:T(8,128)(2,1)S(1)}, bf16[128,512]{1,0:T(8,128)(2,1)S(1)}, u32[]{:S(2)}, u32[]{:S(2)}) collective-permute-start(bf16[128,512]{1,0:T(8,128)(2,1)S(1)} %get-tuple-element.26), channel_id=1, source_target_pairs={{8,0},{16,8},{24,16},{32,24},{40,32},{48,40},{56,48},{64,56},{72,6... | collective-permute-start | bytes 393224 | tf_op jit(solution)/shard_map/ppermute | solution.py:147
  74.3 7.4 %all-to-all-done.1 = f32[16,8,128]{2,1,0:T(8,128)S(1)} async-done(((f32[16,8,128]{2,1,0:T(8,128)}), f32[16,8,128]{2,1,0:T(8,128)S(1)}, u32[]{:S(2)}, u32[]{:S(2)}) %all-to-all-start.1) | async-done | bytes 65568 | tf_op jit(solution)/shard_map/all_to_all | solution.py:151
  81.6 0.7 tile.5
  82.3 5.8 %all-to-all-start.2 = ((f32[32,8,128]{2,1,0:T(8,128)}), f32[32,8,128]{2,1,0:T(8,128)S(1)}, u32[]{:S(2)}, u32[]{:S(2)}) async-start(f32[32,8,128]{2,1,0:T(8,128)} %tile.5), calls=%async_computation.2 | async-start | bytes 262144 | tf_op jit(solution)/shard_map/all_to_all | solution.py:151
  88.1 0.0 collective-permute-done.5.r2
  88.1 0.0 collective-permute-done.6.r1
  88.2 0.7 shard_map.88
  88.8 6.9 %all-to-all-done.2 = f32[32,8,128]{2,1,0:T(8,128)S(1)} async-done(((f32[32,8,128]{2,1,0:T(8,128)}), f32[32,8,128]{2,1,0:T(8,128)S(1)}, u32[]{:S(2)}, u32[]{:S(2)}) %all-to-all-start.2) | async-done | bytes 131104 | tf_op jit(solution)/shard_map/all_to_all | solution.py:151
  95.7 0.7 copy.10
  (3 shorter events, 0.1 us)
Async XLA Ops:
  1.5 6.3 %collective-permute-start = (bf16[128,512]{1,0:T(8,128)(2,1)S(1)}, bf16[128,512]{1,0:T(8,128)(2,1)S(1)}, u32[]{:S(2)}, u32[]{:S(2)}) collective-permute-start(bf16[128,512]{1,0:T(8,128)(2,1)S(1)} %shard_map.85.kv0), channel_id=1, source_target_pairs={{0,8},{8,16},{16,24},{24,32},{32,40},{40,48},{48,56},{56,64},{64,7... | collective-permute-start | bytes 393224 | tf_op jit(solution)/shard_map/ppermute | solution.py:147
  7.8 5.7 %collective-permute-start.1 = (bf16[128,512]{1,0:T(8,128)(2,1)S(1)}, bf16[128,512]{1,0:T(8,128)(2,1)S(1)}, u32[]{:S(2)}, u32[]{:S(2)}) collective-permute-start(bf16[128,512]{1,0:T(8,128)(2,1)S(1)} %collective-permute-done.kv1), channel_id=1, source_target_pairs={{0,8},{8,16},{16,24},{24,32},{32,40},{40,48},{48,56},{56,64},{64,7... | collective-permute-start | bytes 393224 | tf_op jit(solution)/shard_map/ppermute | solution.py:147
  13.5 6.5 %collective-permute-start.2 = (bf16[128,512]{1,0:T(8,128)(2,1)S(1)}, bf16[128,512]{1,0:T(8,128)(2,1)S(1)}, u32[]{:S(2)}, u32[]{:S(2)}) collective-permute-start(bf16[128,512]{1,0:T(8,128)(2,1)S(1)} %collective-permute-done.1.kv2), channel_id=1, source_target_pairs={{0,8},{8,16},{16,24},{24,32},{32,40},{40,48},{48,56},{56,64},{64,7... | collective-permute-start | bytes 393224 | tf_op jit(solution)/shard_map/ppermute | solution.py:147
  20.0 6.9 %collective-permute-start.3 = (bf16[128,512]{1,0:T(8,128)(2,1)S(1)}, bf16[128,512]{1,0:T(8,128)(2,1)S(1)}, u32[]{:S(2)}, u32[]{:S(2)}) collective-permute-start(bf16[128,512]{1,0:T(8,128)(2,1)S(1)} %collective-permute-done.2.kv3), channel_id=1, source_target_pairs={{0,8},{8,16},{16,24},{24,32},{32,40},{40,48},{48,56},{56,64},{64,7... | collective-permute-start | bytes 393224 | tf_op jit(solution)/shard_map/ppermute | solution.py:147
  31.1 32.6 %all-to-all-start = ((f32[32,8,128]{2,1,0:T(8,128)}), f32[32,8,128]{2,1,0:T(8,128)S(1)}, u32[]{:S(2)}, u32[]{:S(2)}) async-start(f32[32,8,128]{2,1,0:T(8,128)} %get-tuple-element.29), calls=%async_computation | async-start | bytes 262144 | tf_op jit(solution)/shard_map/all_to_all | solution.py:151
  56.1 15.5 %collective-permute-start.4 = (bf16[256,512]{1,0:T(8,128)(2,1)S(1)}, bf16[256,512]{1,0:T(8,128)(2,1)S(1)}, u32[]{:S(2)}, u32[]{:S(2)}) collective-permute-start(bf16[256,512]{1,0:T(8,128)(2,1)S(1)} %get-tuple-element.22), channel_id=1, source_target_pairs={{16,0},{24,8},{32,16},{40,24},{48,32},{56,40},{64,48},{72,56},{80,... | collective-permute-start | bytes 786440 | tf_op jit(solution)/shard_map/ppermute | solution.py:147
  64.3 17.3 %all-to-all-start.1 = ((f32[16,8,128]{2,1,0:T(8,128)}), f32[16,8,128]{2,1,0:T(8,128)S(1)}, u32[]{:S(2)}, u32[]{:S(2)}) async-start(f32[16,8,128]{2,1,0:T(8,128)} %tile.4), calls=%async_computation.1 | async-start | bytes 131072 | tf_op jit(solution)/shard_map/all_to_all | solution.py:151
  71.7 16.5 %collective-permute-start.5 = (bf16[128,512]{1,0:T(8,128)(2,1)S(1)}, bf16[128,512]{1,0:T(8,128)(2,1)S(1)}, u32[]{:S(2)}, u32[]{:S(2)}) collective-permute-start(bf16[128,512]{1,0:T(8,128)(2,1)S(1)} %get-tuple-element.25), channel_id=1, source_target_pairs={{16,0},{24,8},{32,16},{40,24},{48,32},{56,40},{64,48},{72,56},{80,... | collective-permute-start | bytes 393224 | tf_op jit(solution)/shard_map/ppermute | solution.py:147
  73.0 15.2 %collective-permute-start.6 = (bf16[128,512]{1,0:T(8,128)(2,1)S(1)}, bf16[128,512]{1,0:T(8,128)(2,1)S(1)}, u32[]{:S(2)}, u32[]{:S(2)}) collective-permute-start(bf16[128,512]{1,0:T(8,128)(2,1)S(1)} %get-tuple-element.26), channel_id=1, source_target_pairs={{8,0},{16,8},{24,16},{32,24},{40,32},{48,40},{56,48},{64,56},{72,6... | collective-permute-start | bytes 393224 | tf_op jit(solution)/shard_map/ppermute | solution.py:147
  82.3 13.4 %all-to-all-start.2 = ((f32[32,8,128]{2,1,0:T(8,128)}), f32[32,8,128]{2,1,0:T(8,128)S(1)}, u32[]{:S(2)}, u32[]{:S(2)}) async-start(f32[32,8,128]{2,1,0:T(8,128)} %tile.5), calls=%async_computation.2 | async-start | bytes 262144 | tf_op jit(solution)/shard_map/all_to_all | solution.py:151

commit v5 on v4

v5 whole, which is shorter than its diff:
```python
import jax
import jax.numpy as jnp
from jax import lax
from jax.experimental import pallas as pl
from jax.experimental.pallas import tpu as pltpu
from jax.sharding import PartitionSpec as P


HEAD_DIM = 64
BAND = 512
TOK = 128
REACH = BAND // TOK
HEADS = 2
PAIR = HEADS * HEAD_DIM
ROWS = 2 * TOK
SPAN = BAND + ROWS
DIMS = (4, 4, 4, 4, 2)
SCALE = HEAD_DIM ** (-0.5)
F32 = jnp.float32
BF16 = jnp.bfloat16
NN = ((1,), (0,))
NT = ((1,), (1,))
TN = ((0,), (0,))


def call(body, outs, *args, **kw):
    shapes = [pltpu.VMEM(s, d) if v else jax.ShapeDtypeStruct(s, d) for s, d, v in outs]
    return list(pl.pallas_call(body, out_shape=shapes, **kw)(*args))


def near(x):
    return pltpu.with_memory_space_constraint(x, pltpu.VMEM)


def mm(a, b, dims):
    return lax.dot_general(a, b, (dims, ((), ())), preferred_element_type=F32)


def span(block):
    return slice(block * TOK, (block + 1) * TOK)


def flip_matrix(count):
    row = lax.broadcasted_iota(jnp.int32, (count, count), 0)
    col = lax.broadcasted_iota(jnp.int32, (count, count), 1)
    return jnp.where(row + col == count - 1, 1.0, 0.0).astype(BF16)


def low_lanes(shape):
    return lax.broadcasted_iota(jnp.int32, shape, len(shape) - 1) < HEAD_DIM


def half(b):
    return pl.ds(pl.multiple_of(b * TOK, TOK), TOK)


def pack_body(odd, x, y, keep, send):
    take = odd[0] > 0
    for i, a in enumerate((x, y)):
        lanes = slice(i * PAIR, (i + 1) * PAIR)
        keep[:, lanes] = jnp.where(take, a[:, PAIR:], a[:, :PAIR])
        send[:, lanes] = jnp.where(take, a[:, :PAIR], a[:, PAIR:])


def pack_q_body(odd, x, y, emb_t, keep, send, erev):
    pack_body(odd, x, y, keep, send)
    flip = flip_matrix(TOK)
    for b in range(REACH):
        back = mm(emb_t[:, span(REACH - 1 - b)], flip, NN).astype(BF16)
        erev[:HEAD_DIM, span(b)] = back
        erev[HEAD_DIM:, span(b)] = back


def unite_body(odd, keep, got, out):
    out[half(odd[0])] = keep[...]
    out[half(1 - odd[0])] = got[...]


def unite_q_body(odd, keep, got, qs, dos):
    low = low_lanes((TOK, PAIR))
    zero = jnp.zeros((TOK, PAIR), BF16)
    for rows, part in ((half(odd[0]), keep), (half(1 - odd[0]), got)):
        for i, out in enumerate((qs, dos)):
            x = part[:, i * PAIR : (i + 1) * PAIR]
            out[0, rows] = jnp.where(low, x, zero)
            out[1, rows] = jnp.where(low, zero, x)


def main_body(first, qs, dos, erev, kv2, kv1, kv0, gq, far, d1, d0, gemb):
    flip = flip_matrix(ROWS)
    row = lax.broadcasted_iota(jnp.int32, (ROWS, SPAN), 0)
    col = lax.broadcasted_iota(jnp.int32, (ROWS, SPAN), 1)
    ahead = col - row - 1
    valid = (ahead >= 0) & (ahead < BAND) & (col >= first[0])
    k = jnp.concatenate([x[:, :PAIR] for x in (kv2, kv1, kv0)], axis=0)
    v = jnp.concatenate([x[:, PAIR:] for x in (kv2, kv1, kv0)], axis=0)
    total = jnp.zeros((PAIR, BAND), F32)
    gk = jnp.zeros((SPAN, PAIR), F32)
    gv = jnp.zeros((SPAN, PAIR), F32)
    gqs = []
    for h in range(HEADS):
        q, do = qs[h], dos[h]
        along = jnp.concatenate([mm(q, erev[...], NN), jnp.zeros((ROWS, ROWS), F32)], axis=1)
        s = (pltpu.roll(along, 1, 1, stride=1, stride_axis=0) + mm(q, k, NT)) * SCALE
        s = jnp.where(valid, s, -jnp.inf)
        dp = mm(do, v, NT)
        prob = jnp.exp(s - jnp.max(s, axis=1, keepdims=True))
        prob = prob * (1.0 / jnp.sum(prob, axis=1, keepdims=True))
        prob_b = prob.astype(BF16)
        delta = jnp.sum(prob_b.astype(F32) * dp, axis=1, keepdims=True)
        ds = (prob * (dp - delta) * SCALE).astype(BF16)
        dalong = pltpu.roll(mm(flip, ds, NN), BAND, 1, stride=1, stride_axis=0)[:, :BAND].astype(BF16)
        total = total + mm(mm(flip, q, NN).astype(BF16), dalong, TN)
        gk = gk + mm(ds, q, TN)
        gv = gv + mm(prob_b, do, TN)
        gqe = mm(dalong, erev[...], NT)
        hi = gqe.astype(BF16)
        lo = (gqe - hi.astype(F32)).astype(BF16)
        gqs.append(mm(ds, k, NN) + mm(flip, hi, NN) + mm(flip, lo, NN))
    gq[...] = jnp.where(low_lanes((ROWS, PAIR)), *gqs).astype(BF16)
    for part, lanes in ((gk, slice(0, PAIR)), (gv, slice(PAIR, 2 * PAIR))):
        far[:, lanes] = part[:ROWS].astype(BF16)
        d1[:, lanes] = part[ROWS : 2 * ROWS]
        d0[:, lanes] = part[2 * ROWS :]
    total = total[:HEAD_DIM] + total[HEAD_DIM:]
    flip = flip_matrix(TOK)
    for b in range(REACH):
        block = total[:, span(REACH - 1 - b)]
        hi = block.astype(BF16)
        lo = (block - hi.astype(F32)).astype(BF16)
        block = mm(hi, flip, NN) + mm(lo, flip, NN)
        for d in range(HEAD_DIM // 8):
            gemb[d * REACH + b] = block[d * 8 : (d + 1) * 8]


def add_body(far, d1, out):
    out[...] = (d1[...] + far[...].astype(F32)).astype(BF16)


def final_body(odd, got, d0, gq, keep, send):
    for rows, out in ((half(odd[0]), keep), (half(1 - odd[0]), send)):
        out[:, :PAIR] = gq[rows]
        out[:, PAIR:] = (d0[rows] + got[rows].astype(F32)).astype(BF16)


def unpack_body(odd, keep, got, *outs):
    swap = odd[0] > 0
    for i, out in enumerate(outs):
        lanes = slice(i * PAIR, (i + 1) * PAIR)
        a, b = keep[:, lanes], got[:, lanes]
        out[:, :PAIR] = jnp.where(swap, b, a)
        out[:, PAIR:] = jnp.where(swap, a, b)


SEQ = ("y", "zg", "zi")


def shift(x, steps):
    n = lax.axis_size(SEQ)
    return lax.ppermute(x, SEQ, [(s, s + steps) for s in range(max(0, -steps), min(n, n - steps))])


def exchange(x, axes):
    return lax.all_to_all(x, axes, 0, 0, tiled=True)


def spread(x, axes):
    return exchange(jnp.tile(x, (lax.axis_size(axes), 1, 1)), axes)


def swap(x):
    return lax.ppermute(x, SEQ, [(s, s ^ 1) for s in range(lax.axis_size(SEQ))])


def local(query, key_rows, value_matrix_rows, grad_out, rel_embed):
    line, plane = ("zg", "zi"), ("y", "x", "core")
    here = lax.axis_index(SEQ)
    odd = (here % 2).reshape(1)
    sm, vm = pl.BlockSpec(memory_space=pltpu.SMEM), pl.BlockSpec(memory_space=pltpu.VMEM)

    def staged_call(body, outs, *args):
        return call(body, outs, *args, in_specs=[sm] + [vm] * (len(args) - 1))

    part = ((TOK, 2 * PAIR), BF16, True)
    keep, send = staged_call(pack_body, [part] * 2, odd, key_rows, value_matrix_rows)
    got = swap(send)
    unit = (ROWS, 2 * PAIR)
    (kv0,) = staged_call(unite_body, [(unit, BF16, True)], odd, near(keep), near(got))
    kv1 = shift(kv0, 2)
    kv2 = shift(kv1, 2)
    keep, send, erev = staged_call(
        pack_q_body, [part, part, ((PAIR, BAND), BF16, True)], odd, query, grad_out, rel_embed.T
    )
    got = swap(send)
    heads = ((HEADS, ROWS, PAIR), BF16, True)
    qs, dos = staged_call(unite_q_body, [heads] * 2, odd, near(keep), near(got))
    first = (ROWS * jnp.maximum(BAND // ROWS - here // 2, 0)).astype(jnp.int32).reshape(1)
    gq, far, d1, d0, gemb = staged_call(
        main_body,
        [((ROWS, PAIR), BF16, True), (unit, BF16, True), (unit, F32, True), (unit, F32, True)]
        + [((lax.axis_size(plane), 8, 128), F32, True)],
        first, near(qs), near(dos), near(erev), near(kv2), near(kv1), near(kv0),
    )
    part = jnp.sum(exchange(gemb, plane), axis=0)
    part = jnp.sum(spread(part, line), axis=0)
    whole = spread(part, plane)
    grad_embed_t = whole.reshape(8, REACH, 8, 128).transpose(0, 2, 1, 3).reshape(HEAD_DIM, BAND)
    far = shift(far, -2)
    (far,) = call(add_body, [(unit, BF16, True)], near(far), near(d1))
    far = shift(far, -2)
    third = ((TOK, 3 * PAIR), BF16, True)
    keep, send = staged_call(final_body, [third] * 2, odd, near(far), near(d0), near(gq))
    got = swap(send)
    grads = staged_call(unpack_body, [((TOK, 2 * PAIR), BF16, False)] * 3, odd, near(keep), near(got))
    return (*grads, grad_embed_t.T)


def solution(mesh):
    fine = jax.sharding.Mesh(mesh.devices.reshape(DIMS), ("y", "zg", "zi", "x", "core"))
    rows = P(SEQ, ("x", "core"))
    return jax.shard_map(
        local,
        mesh=fine,
        in_specs=(rows, rows, rows, rows, P()),
        out_specs=(rows, rows, rows, P()),
        check_vma=False,
    )
```

time: 97 us -> 98.6 us (1.016)
  blocking collectives: 0 us -> 21.7 us
  starting transfers between devices: 56.4 us -> 45.9 us
  waiting for transfers between devices: 30.3 us -> 21.5 us
    all_to_all x0 -> x1, blocking collectives: none -> 21.7 us  [exchange(): return lax.all_to_all(x, axes, 0, 0, tiled=True)]
    all_to_all x3 -> x2, waiting for transfers between devices: 20.6 us -> 0.82 us  [exchange(): return lax.all_to_all(x, axes, 0, 0, tiled=True)]
    all_to_all x3 -> x2, starting transfers between devices: 36.5 us -> 21.3 us  [exchange(): return lax.all_to_all(x, axes, 0, 0, tiled=True)]
    ppermute x0 -> x3, waiting for transfers between devices: none -> 8.79 us  [swap(): return lax.ppermute(x, SEQ, [(s, s ^ 1) for s in range(lax.axis_size(SEQ))])]
    ppermute x0 -> x3, starting transfers between devices: none -> 8.2 us  [swap(): return lax.ppermute(x, SEQ, [(s, s ^ 1) for s in range(lax.axis_size(SEQ))])]
    ppermute x7 -> x4, starting transfers between devices: 19.9 us -> 16.4 us  [shift(): lax.ppermute(x, SEQ, [(s, s + steps) for s in range(max(0, -steps), min(n...]
    ppermute x7 -> x4, waiting for transfers between devices: 9.73 us -> 11.9 us  [shift(): lax.ppermute(x, SEQ, [(s, s + steps) for s in range(max(0, -steps), min(n...]
    pallas_call x5 -> x8, Pallas kernels: 6.91 us -> 6.2 us  [call(): return list(pl.pallas_call(body, out_shape=shapes, **kw)(*args))]
  transfers between devices with their start and end apart: 10 -> 9, of which waited for: 8 -> 6; matrix products, arithmetic and copies ran while one was open for 1% -> 1% of each run, Pallas kernels for 2% -> 2%
where the time goes in v5:
time: 98.6 us; the launch traced here: 98 us
  starting transfers between devices  45.9 us (47%)
  blocking collectives  21.7 us (22%)
  waiting for transfers between devices  21.5 us (22%)
  Pallas kernels  6.2 us (6%)
  local copies, waits for them, and re-layouts  1.96 us (2%)
    all_to_all x1, blocking collectives, exchange(): return lax.all_to_all(x, axes, 0, 0, tiled=True)  21.7 us
    all_to_all x2, starting transfers between devices, exchange(): return lax.all_to_all(x, axes, 0, 0, tiled=True)  21.3 us
    ppermute x4, starting transfers between devices, shift(): lax.ppermute(x, SEQ, [(s, s + steps) for s in range(max(0, -steps), min(n...  16.4 us
    ppermute x4, waiting for transfers between devices, shift(): lax.ppermute(x, SEQ, [(s, s + steps) for s in range(max(0, -steps), min(n...  11.9 us
    ppermute x3, waiting for transfers between devices, swap(): return lax.ppermute(x, SEQ, [(s, s ^ 1) for s in range(lax.axis_size(SEQ))])  8.79 us
    ppermute x3, starting transfers between devices, swap(): return lax.ppermute(x, SEQ, [(s, s ^ 1) for s in range(lax.axis_size(SEQ))])  8.2 us
    pallas_call x8, Pallas kernels, call(): return list(pl.pallas_call(body, out_shape=shapes, **kw)(*args))  6.2 us
  transfers between devices with their start and end apart: 9, of which 6 were waited for; matrix products, arithmetic and copies ran while one was open for 1% of the time, Pallas kernels for 2%

profile of v5, /device:TPU:1, one launch (start us, length us, event | category | flops | bytes accessed | tf_op | source)
XLA Modules:
  0.0 98.0 jit_solution(2674683241495734174)
XLA Ops:
  0.6 0.9 shard_map.86
  1.5 4.4 %collective-permute-start.1 = (bf16[128,256]{1,0:T(8,128)(2,1)S(1)}, bf16[128,256]{1,0:T(8,128)(2,1)S(1)}, u32[]{:S(2)}, u32[]{:S(2)}) collective-permute-start(bf16[128,256]{1,0:T(8,128)(2,1)S(1)} %get-tuple-element.27), channel_id=1, source_target_pairs={{0,8},{8,0},{16,24},{24,16},{32,40},{40,32},{48,56},{56,48},{64,72... | collective-permute-start | bytes 196616 | tf_op jit(solution)/shard_map/ppermute | solution.py:172
  5.9 1.6 %collective-permute-done.1.got = bf16[128,256]{1,0:T(8,128)(2,1)S(1)} collective-permute-done((bf16[128,256]{1,0:T(8,128)(2,1)S(1)}, bf16[128,256]{1,0:T(8,128)(2,1)S(1)}, u32[]{:S(2)}, u32[]{:S(2)}) %collective-permute-start.1) | collective-permute-done | bytes 65568 | tf_op jit(solution)/shard_map/ppermute | solution.py:172
  7.6 4.9 %collective-permute-start.2 = (bf16[256,256]{1,0:T(8,128)(2,1)S(1)}, bf16[256,256]{1,0:T(8,128)(2,1)S(1)}, u32[]{:S(2)}, u32[]{:S(2)}) collective-permute-start(bf16[256,256]{1,0:T(8,128)(2,1)S(1)} %shard_map.87.kv0), channel_id=1, source_target_pairs={{0,16},{8,24},{16,32},{24,40},{32,48},{40,56},{48,64},{56,72},{64,... | collective-permute-start | bytes 393224 | tf_op jit(solution)/shard_map/ppermute | solution.py:160
  12.5 1.9 %collective-permute-done.2.kv1 = bf16[256,256]{1,0:T(8,128)(2,1)S(1)} collective-permute-done((bf16[256,256]{1,0:T(8,128)(2,1)S(1)}, bf16[256,256]{1,0:T(8,128)(2,1)S(1)}, u32[]{:S(2)}, u32[]{:S(2)}) %collective-permute-start.2) | collective-permute-done | bytes 131104 | tf_op jit(solution)/shard_map/ppermute | solution.py:160
  14.4 8.9 %collective-permute-start.3 = (bf16[256,256]{1,0:T(8,128)(2,1)S(1)}, bf16[256,256]{1,0:T(8,128)(2,1)S(1)}, u32[]{:S(2)}, u32[]{:S(2)}) collective-permute-start(bf16[256,256]{1,0:T(8,128)(2,1)S(1)} %collective-permute-done.2.kv1), channel_id=1, source_target_pairs={{0,16},{8,24},{16,32},{24,40},{32,48},{40,56},{48,64},{56,72},{64,... | collective-permute-start | bytes 393224 | tf_op jit(solution)/shard_map/ppermute | solution.py:160
  23.3 1.1 %shard_map.84 = (bf16[128,256]{1,0:T(8,128)(2,1)S(1)}, bf16[128,256]{1,0:T(8,128)(2,1)S(1)}, bf16[128,512]{1,0:T(8,128)(2,1)S(1)}) custom-call(s32[1]{0:T(128)} %bitcast.odd, bf16[128,256]{1,0:T(8,128)(2,1)} %x.2, bf16[128,256]{1,0:T(8,128)(2,1)} %y.2, bf16[64,512]{1,0:T(8,128)(2,1)} %bitcast.11), custom_call_target="tpu_custom_call" | custom-call | tf_op jit(solution)/shard_map/pallas_call | solution.py:28
  24.4 1.9 %collective-permute-start = (bf16[128,256]{1,0:T(8,128)(2,1)S(1)}, bf16[128,256]{1,0:T(8,128)(2,1)S(1)}, u32[]{:S(2)}, u32[]{:S(2)}) collective-permute-start(bf16[128,256]{1,0:T(8,128)(2,1)S(1)} %get-tuple-element.22), channel_id=1, source_target_pairs={{0,8},{8,0},{16,24},{24,16},{32,40},{40,32},{48,56},{56,48},{64,72... | collective-permute-start | bytes 196616 | tf_op jit(solution)/shard_map/ppermute | solution.py:172
  26.4 3.1 %collective-permute-done.got = bf16[128,256]{1,0:T(8,128)(2,1)S(1)} collective-permute-done((bf16[128,256]{1,0:T(8,128)(2,1)S(1)}, bf16[128,256]{1,0:T(8,128)(2,1)S(1)}, u32[]{:S(2)}, u32[]{:S(2)}) %collective-permute-start) | collective-permute-done | bytes 65568 | tf_op jit(solution)/shard_map/ppermute | solution.py:172
  29.5 0.0 collective-permute-done.3.kv2
  29.5 3.4 %shard_map.88 = (bf16[256,128]{1,0:T(8,128)(2,1)S(1)}, bf16[256,256]{1,0:T(8,128)(2,1)S(1)}, f32[256,256]{1,0:T(8,128)S(1)}, f32[256,256]{1,0:T(8,128)S(1)}, f32[32,8,128]{2,1,0:T(8,128)S(1)}) custom-call(s32[1]{0:T(128)} %bitcast.1.first, bf16[2,256,128]{2,1,0:T(8,128)(2,1)S(1)} %get-tuple-element.23.qs, bf16[2,256,128]{2,1,0:T(8,128)(2,1)S(1)} %get-tuple-element.24.dos, ...), custom_call_target="tpu_custom_call" | custom-call | tf_op jit(solution)/shard_map/pallas_call | solution.py:28
  32.9 21.7 %all_to_all.15 = f32[32,8,128]{2,1,0:T(8,128)S(1)} all-to-all(f32[32,8,128]{2,1,0:T(8,128)S(1)} %get-tuple-element.37), channel_id=1, replica_groups=mesh['y'=4,'zg'=4,'zi'=4,'x'=4,'core'=2] {'y','x','core'}, dimensions={0} | all-to-all | bytes 262144 | tf_op jit(solution)/shard_map/all_to_all | solution.py:164
  54.6 0.6 tile.4
  55.2 9.8 %all-to-all-start.1 = ((f32[16,8,128]{2,1,0:T(8,128)}), f32[16,8,128]{2,1,0:T(8,128)S(1)}, u32[]{:S(2)}, u32[]{:S(2)}) async-start(f32[16,8,128]{2,1,0:T(8,128)} %tile.4), calls=%async_computation.1 | async-start | bytes 131072 | tf_op jit(solution)/shard_map/all_to_all | solution.py:164
  65.0 1.3 %collective-permute-start.4 = (bf16[256,256]{1,0:T(8,128)(2,1)S(1)}, bf16[256,256]{1,0:T(8,128)(2,1)S(1)}, u32[]{:S(2)}, u32[]{:S(2)}) collective-permute-start(bf16[256,256]{1,0:T(8,128)(2,1)S(1)} %get-tuple-element.28), channel_id=1, source_target_pairs={{16,0},{24,8},{32,16},{40,24},{48,32},{56,40},{64,48},{72,56},{80,... | collective-permute-start | bytes 393224 | tf_op jit(solution)/shard_map/ppermute | solution.py:160
  66.3 9.9 %collective-permute-done.4.far = bf16[256,256]{1,0:T(8,128)(2,1)S(1)} collective-permute-done((bf16[256,256]{1,0:T(8,128)(2,1)S(1)}, bf16[256,256]{1,0:T(8,128)(2,1)S(1)}, u32[]{:S(2)}, u32[]{:S(2)}) %collective-permute-start.4) | collective-permute-done | bytes 131104 | tf_op jit(solution)/shard_map/ppermute | solution.py:160
  76.3 1.3 %collective-permute-start.5 = (bf16[256,256]{1,0:T(8,128)(2,1)S(1)}, bf16[256,256]{1,0:T(8,128)(2,1)S(1)}, u32[]{:S(2)}, u32[]{:S(2)}) collective-permute-start(bf16[256,256]{1,0:T(8,128)(2,1)S(1)} %shard_map.89), channel_id=1, source_target_pairs={{16,0},{24,8},{32,16},{40,24},{48,32},{56,40},{64,48},{72,56},{80,... | collective-permute-start | bytes 393224 | tf_op jit(solution)/shard_map/ppermute | solution.py:160
  77.6 0.0 all-to-all-done.1
  77.6 0.7 tile.5
  78.3 11.5 %all-to-all-start.2 = ((f32[32,8,128]{2,1,0:T(8,128)}), f32[32,8,128]{2,1,0:T(8,128)S(1)}, u32[]{:S(2)}, u32[]{:S(2)}) async-start(f32[32,8,128]{2,1,0:T(8,128)} %tile.5), calls=%async_computation.2 | async-start | bytes 262144 | tf_op jit(solution)/shard_map/all_to_all | solution.py:164
  89.8 0.0 collective-permute-done.5.got
  89.8 1.9 %collective-permute-start.6 = (bf16[128,384]{1,0:T(8,128)(2,1)S(1)}, bf16[128,384]{1,0:T(8,128)(2,1)S(1)}, u32[]{:S(2)}, u32[]{:S(2)}) collective-permute-start(bf16[128,384]{1,0:T(8,128)(2,1)S(1)} %get-tuple-element.33), channel_id=1, source_target_pairs={{0,8},{8,0},{16,24},{24,16},{32,40},{40,32},{48,56},{56,48},{64,72... | collective-permute-start | bytes 294920 | tf_op jit(solution)/shard_map/ppermute | solution.py:172
  91.8 4.1 %collective-permute-done.6.got = bf16[128,384]{1,0:T(8,128)(2,1)S(1)} collective-permute-done((bf16[128,384]{1,0:T(8,128)(2,1)S(1)}, bf16[128,384]{1,0:T(8,128)(2,1)S(1)}, u32[]{:S(2)}, u32[]{:S(2)}) %collective-permute-start.6) | collective-permute-done | bytes 98336 | tf_op jit(solution)/shard_map/ppermute | solution.py:172
  95.8 0.7 shard_map.91
  96.6 0.8 all-to-all-done.2
  97.4 0.7 copy.10
  (6 shorter events, 0.2 us)
Async XLA Ops:
  1.5 6.0 %collective-permute-start.1 = (bf16[128,256]{1,0:T(8,128)(2,1)S(1)}, bf16[128,256]{1,0:T(8,128)(2,1)S(1)}, u32[]{:S(2)}, u32[]{:S(2)}) collective-permute-start(bf16[128,256]{1,0:T(8,128)(2,1)S(1)} %get-tuple-element.27), channel_id=1, source_target_pairs={{0,8},{8,0},{16,24},{24,16},{32,40},{40,32},{48,56},{56,48},{64,72... | collective-permute-start | bytes 196616 | tf_op jit(solution)/shard_map/ppermute | solution.py:172
  7.6 6.8 %collective-permute-start.2 = (bf16[256,256]{1,0:T(8,128)(2,1)S(1)}, bf16[256,256]{1,0:T(8,128)(2,1)S(1)}, u32[]{:S(2)}, u32[]{:S(2)}) collective-permute-start(bf16[256,256]{1,0:T(8,128)(2,1)S(1)} %shard_map.87.kv0), channel_id=1, source_target_pairs={{0,16},{8,24},{16,32},{24,40},{32,48},{40,56},{48,64},{56,72},{64,... | collective-permute-start | bytes 393224 | tf_op jit(solution)/shard_map/ppermute | solution.py:160
  14.4 15.1 %collective-permute-start.3 = (bf16[256,256]{1,0:T(8,128)(2,1)S(1)}, bf16[256,256]{1,0:T(8,128)(2,1)S(1)}, u32[]{:S(2)}, u32[]{:S(2)}) collective-permute-start(bf16[256,256]{1,0:T(8,128)(2,1)S(1)} %collective-permute-done.2.kv1), channel_id=1, source_target_pairs={{0,16},{8,24},{16,32},{24,40},{32,48},{40,56},{48,64},{56,72},{64,... | collective-permute-start | bytes 393224 | tf_op jit(solution)/shard_map/ppermute | solution.py:160
  24.4 5.0 %collective-permute-start = (bf16[128,256]{1,0:T(8,128)(2,1)S(1)}, bf16[128,256]{1,0:T(8,128)(2,1)S(1)}, u32[]{:S(2)}, u32[]{:S(2)}) collective-permute-start(bf16[128,256]{1,0:T(8,128)(2,1)S(1)} %get-tuple-element.22), channel_id=1, source_target_pairs={{0,8},{8,0},{16,24},{24,16},{32,40},{40,32},{48,56},{56,48},{64,72... | collective-permute-start | bytes 196616 | tf_op jit(solution)/shard_map/ppermute | solution.py:172
  55.2 22.4 %all-to-all-start.1 = ((f32[16,8,128]{2,1,0:T(8,128)}), f32[16,8,128]{2,1,0:T(8,128)S(1)}, u32[]{:S(2)}, u32[]{:S(2)}) async-start(f32[16,8,128]{2,1,0:T(8,128)} %tile.4), calls=%async_computation.1 | async-start | bytes 131072 | tf_op jit(solution)/shard_map/all_to_all | solution.py:164
  65.0 11.2 %collective-permute-start.4 = (bf16[256,256]{1,0:T(8,128)(2,1)S(1)}, bf16[256,256]{1,0:T(8,128)(2,1)S(1)}, u32[]{:S(2)}, u32[]{:S(2)}) collective-permute-start(bf16[256,256]{1,0:T(8,128)(2,1)S(1)} %get-tuple-element.28), channel_id=1, source_target_pairs={{16,0},{24,8},{32,16},{40,24},{48,32},{56,40},{64,48},{72,56},{80,... | collective-permute-start | bytes 393224 | tf_op jit(solution)/shard_map/ppermute | solution.py:160
  76.3 13.5 %collective-permute-start.5 = (bf16[256,256]{1,0:T(8,128)(2,1)S(1)}, bf16[256,256]{1,0:T(8,128)(2,1)S(1)}, u32[]{:S(2)}, u32[]{:S(2)}) collective-permute-start(bf16[256,256]{1,0:T(8,128)(2,1)S(1)} %shard_map.89), channel_id=1, source_target_pairs={{16,0},{24,8},{32,16},{40,24},{48,32},{56,40},{64,48},{72,56},{80,... | collective-permute-start | bytes 393224 | tf_op jit(solution)/shard_map/ppermute | solution.py:160
  78.3 19.1 %all-to-all-start.2 = ((f32[32,8,128]{2,1,0:T(8,128)}), f32[32,8,128]{2,1,0:T(8,128)S(1)}, u32[]{:S(2)}, u32[]{:S(2)}) async-start(f32[32,8,128]{2,1,0:T(8,128)} %tile.5), calls=%async_computation.2 | async-start | bytes 262144 | tf_op jit(solution)/shard_map/all_to_all | solution.py:164
  89.8 6.0 %collective-permute-start.6 = (bf16[128,384]{1,0:T(8,128)(2,1)S(1)}, bf16[128,384]{1,0:T(8,128)(2,1)S(1)}, u32[]{:S(2)}, u32[]{:S(2)}) collective-permute-start(bf16[128,384]{1,0:T(8,128)(2,1)S(1)} %get-tuple-element.33), channel_id=1, source_target_pairs={{0,8},{8,0},{16,24},{24,16},{32,40},{40,32},{48,56},{56,48},{64,72... | collective-permute-start | bytes 294920 | tf_op jit(solution)/shard_map/ppermute | solution.py:172

commit v6 on v5

--- a/solution.py
+++ b/solution.py
@@ -133,6 +133,10 @@
             gemb[d * REACH + b] = block[d * 8 : (d + 1) * 8]
 
 
+def sum_body(x, out):
+    out[...] = jnp.broadcast_to(jnp.sum(x[...], axis=0, keepdims=True), out.shape)
+
+
 def add_body(far, d1, out):
     out[...] = (d1[...] + far[...].astype(F32)).astype(BF16)
 
@@ -162,10 +166,6 @@
 
 def exchange(x, axes):
     return lax.all_to_all(x, axes, 0, 0, tiled=True)
-
-
-def spread(x, axes):
-    return exchange(jnp.tile(x, (lax.axis_size(axes), 1, 1)), axes)
 
 
 def swap(x):
@@ -201,9 +201,11 @@
         + [((lax.axis_size(plane), 8, 128), F32, True)],
         first, near(qs), near(dos), near(erev), near(kv2), near(kv1), near(kv0),
     )
-    part = jnp.sum(exchange(gemb, plane), axis=0)
-    part = jnp.sum(spread(part, line), axis=0)
-    whole = spread(part, plane)
+    whole = exchange(gemb, plane)
+    for axes in (line, plane):
+        tiles = ((lax.axis_size(axes), 8, 128), F32, True)
+        (whole,) = call(sum_body, [tiles], near(whole))
+        whole = exchange(whole, axes)
     grad_embed_t = whole.reshape(8, REACH, 8, 128).transpose(0, 2, 1, 3).reshape(HEAD_DIM, BAND)
     far = shift(far, -2)
     (far,) = call(add_body, [(unit, BF16, True)], near(far), near(d1))

time: 98.6 us -> 98.6 us (level)
  Pallas kernels: 6.2 us -> 7.55 us
  local copies, waits for them, and re-layouts: 1.96 us -> 0.66 us
    pallas_call x8 -> x10, Pallas kernels: 6.2 us -> 7.55 us  [call(): return list(pl.pallas_call(body, out_shape=shapes, **kw)(*args))]
    another operation x2 -> x0, local copies, waits for them, and re-layouts: 1.3 us -> none  [spread(): return exchange(jnp.tile(x, (lax.axis_size(axes), 1, 1)), axes)]
  transfers between devices with their start and end apart: 9 -> 9, of which waited for: 6 -> 6; matrix products, arithmetic and copies ran while one was open for 1% -> 0% of each run, Pallas kernels for 2% -> 3%
where the time goes in v6:
time: 98.6 us; the launch traced here: 98 us
  starting transfers between devices  45.9 us (47%)
  blocking collectives  21.7 us (22%)
  waiting for transfers between devices  21.5 us (22%)
  Pallas kernels  7.55 us (8%)
    all_to_all x1, blocking collectives, exchange(): return lax.all_to_all(x, axes, 0, 0, tiled=True)  21.7 us
    all_to_all x2, starting transfers between devices, exchange(): return lax.all_to_all(x, axes, 0, 0, tiled=True)  21.3 us
    ppermute x4, starting transfers between devices, shift(): lax.ppermute(x, SEQ, [(s, s + steps) for s in range(max(0, -steps), min(n...  16.4 us
    ppermute x4, waiting for transfers between devices, shift(): lax.ppermute(x, SEQ, [(s, s + steps) for s in range(max(0, -steps), min(n...  11.9 us
    ppermute x3, waiting for transfers between devices, swap(): return lax.ppermute(x, SEQ, [(s, s ^ 1) for s in range(lax.axis_size(SEQ))])  8.79 us
    ppermute x3, starting transfers between devices, swap(): return lax.ppermute(x, SEQ, [(s, s ^ 1) for s in range(lax.axis_size(SEQ))])  8.2 us
    pallas_call x10, Pallas kernels, call(): return list(pl.pallas_call(body, out_shape=shapes, **kw)(*args))  7.55 us
  transfers between devices with their start and end apart: 9, of which 6 were waited for; matrix products, arithmetic and copies ran while one was open for 0% of the time, Pallas kernels for 3%

profile of v6, /device:TPU:1, one launch (start us, length us, event | category | flops | bytes accessed | tf_op | source)
XLA Modules:
  0.0 98.0 jit_solution(17723097332529125749)
XLA Ops:
  0.6 0.9 shard_map.86
  1.5 4.4 %collective-permute-start.1 = (bf16[128,256]{1,0:T(8,128)(2,1)S(1)}, bf16[128,256]{1,0:T(8,128)(2,1)S(1)}, u32[]{:S(2)}, u32[]{:S(2)}) collective-permute-start(bf16[128,256]{1,0:T(8,128)(2,1)S(1)} %get-tuple-element.27), channel_id=1, source_target_pairs={{0,8},{8,0},{16,24},{24,16},{32,40},{40,32},{48,56},{56,48},{64,72... | collective-permute-start | bytes 196616 | tf_op jit(solution)/shard_map/ppermute | solution.py:172
  5.9 1.6 %collective-permute-done.1.got = bf16[128,256]{1,0:T(8,128)(2,1)S(1)} collective-permute-done((bf16[128,256]{1,0:T(8,128)(2,1)S(1)}, bf16[128,256]{1,0:T(8,128)(2,1)S(1)}, u32[]{:S(2)}, u32[]{:S(2)}) %collective-permute-start.1) | collective-permute-done | bytes 65568 | tf_op jit(solution)/shard_map/ppermute | solution.py:172
  7.6 4.9 %collective-permute-start.2 = (bf16[256,256]{1,0:T(8,128)(2,1)S(1)}, bf16[256,256]{1,0:T(8,128)(2,1)S(1)}, u32[]{:S(2)}, u32[]{:S(2)}) collective-permute-start(bf16[256,256]{1,0:T(8,128)(2,1)S(1)} %shard_map.87.kv0), channel_id=1, source_target_pairs={{0,16},{8,24},{16,32},{24,40},{32,48},{40,56},{48,64},{56,72},{64,... | collective-permute-start | bytes 393224 | tf_op jit(solution)/shard_map/ppermute | solution.py:164
  12.5 1.9 %collective-permute-done.2.kv1 = bf16[256,256]{1,0:T(8,128)(2,1)S(1)} collective-permute-done((bf16[256,256]{1,0:T(8,128)(2,1)S(1)}, bf16[256,256]{1,0:T(8,128)(2,1)S(1)}, u32[]{:S(2)}, u32[]{:S(2)}) %collective-permute-start.2) | collective-permute-done | bytes 131104 | tf_op jit(solution)/shard_map/ppermute | solution.py:164
  14.4 8.9 %collective-permute-start.3 = (bf16[256,256]{1,0:T(8,128)(2,1)S(1)}, bf16[256,256]{1,0:T(8,128)(2,1)S(1)}, u32[]{:S(2)}, u32[]{:S(2)}) collective-permute-start(bf16[256,256]{1,0:T(8,128)(2,1)S(1)} %collective-permute-done.2.kv1), channel_id=1, source_target_pairs={{0,16},{8,24},{16,32},{24,40},{32,48},{40,56},{48,64},{56,72},{64,... | collective-permute-start | bytes 393224 | tf_op jit(solution)/shard_map/ppermute | solution.py:164
  23.3 1.1 %shard_map.84 = (bf16[128,256]{1,0:T(8,128)(2,1)S(1)}, bf16[128,256]{1,0:T(8,128)(2,1)S(1)}, bf16[128,512]{1,0:T(8,128)(2,1)S(1)}) custom-call(s32[1]{0:T(128)} %bitcast.odd, bf16[128,256]{1,0:T(8,128)(2,1)} %x.2, bf16[128,256]{1,0:T(8,128)(2,1)} %y.2, bf16[64,512]{1,0:T(8,128)(2,1)} %bitcast.11), custom_call_target="tpu_custom_call" | custom-call | tf_op jit(solution)/shard_map/pallas_call | solution.py:28
  24.4 1.9 %collective-permute-start = (bf16[128,256]{1,0:T(8,128)(2,1)S(1)}, bf16[128,256]{1,0:T(8,128)(2,1)S(1)}, u32[]{:S(2)}, u32[]{:S(2)}) collective-permute-start(bf16[128,256]{1,0:T(8,128)(2,1)S(1)} %get-tuple-element.22), channel_id=1, source_target_pairs={{0,8},{8,0},{16,24},{24,16},{32,40},{40,32},{48,56},{56,48},{64,72... | collective-permute-start | bytes 196616 | tf_op jit(solution)/shard_map/ppermute | solution.py:172
  26.4 3.1 %collective-permute-done.got = bf16[128,256]{1,0:T(8,128)(2,1)S(1)} collective-permute-done((bf16[128,256]{1,0:T(8,128)(2,1)S(1)}, bf16[128,256]{1,0:T(8,128)(2,1)S(1)}, u32[]{:S(2)}, u32[]{:S(2)}) %collective-permute-start) | collective-permute-done | bytes 65568 | tf_op jit(solution)/shard_map/ppermute | solution.py:172
  29.5 0.0 collective-permute-done.3.kv2
  29.5 3.4 %shard_map.88 = (bf16[256,128]{1,0:T(8,128)(2,1)S(1)}, bf16[256,256]{1,0:T(8,128)(2,1)S(1)}, f32[256,256]{1,0:T(8,128)S(1)}, f32[256,256]{1,0:T(8,128)S(1)}, f32[32,8,128]{2,1,0:T(8,128)S(1)}) custom-call(s32[1]{0:T(128)} %bitcast.1.first, bf16[2,256,128]{2,1,0:T(8,128)(2,1)S(1)} %get-tuple-element.23.qs, bf16[2,256,128]{2,1,0:T(8,128)(2,1)S(1)} %get-tuple-element.24.dos, ...), custom_call_target="tpu_custom_call" | custom-call | tf_op jit(solution)/shard_map/pallas_call | solution.py:28
  32.9 21.7 %all_to_all.15.x = f32[32,8,128]{2,1,0:T(8,128)S(1)} all-to-all(f32[32,8,128]{2,1,0:T(8,128)S(1)} %get-tuple-element.37), channel_id=1, replica_groups=mesh['y'=4,'zg'=4,'zi'=4,'x'=4,'core'=2] {'y','x','core'}, dimensions={0} | all-to-all | bytes 262144 | tf_op jit(solution)/shard_map/all_to_all | solution.py:168
  54.6 0.7 shard_map.92
  55.2 9.8 %all-to-all-start.1 = ((f32[16,8,128]{2,1,0:T(8,128)}), f32[16,8,128]{2,1,0:T(8,128)S(1)}, u32[]{:S(2)}, u32[]{:S(2)}) async-start(f32[16,8,128]{2,1,0:T(8,128)} %shard_map.92), calls=%async_computation.1 | async-start | bytes 131072 | tf_op jit(solution)/shard_map/all_to_all | solution.py:168
  65.0 1.3 %collective-permute-start.4 = (bf16[256,256]{1,0:T(8,128)(2,1)S(1)}, bf16[256,256]{1,0:T(8,128)(2,1)S(1)}, u32[]{:S(2)}, u32[]{:S(2)}) collective-permute-start(bf16[256,256]{1,0:T(8,128)(2,1)S(1)} %get-tuple-element.28), channel_id=1, source_target_pairs={{16,0},{24,8},{32,16},{40,24},{48,32},{56,40},{64,48},{72,56},{80,... | collective-permute-start | bytes 393224 | tf_op jit(solution)/shard_map/ppermute | solution.py:164
  66.3 9.9 %collective-permute-done.4.far = bf16[256,256]{1,0:T(8,128)(2,1)S(1)} collective-permute-done((bf16[256,256]{1,0:T(8,128)(2,1)S(1)}, bf16[256,256]{1,0:T(8,128)(2,1)S(1)}, u32[]{:S(2)}, u32[]{:S(2)}) %collective-permute-start.4) | collective-permute-done | bytes 131104 | tf_op jit(solution)/shard_map/ppermute | solution.py:164
  76.3 1.3 %collective-permute-start.5 = (bf16[256,256]{1,0:T(8,128)(2,1)S(1)}, bf16[256,256]{1,0:T(8,128)(2,1)S(1)}, u32[]{:S(2)}, u32[]{:S(2)}) collective-permute-start(bf16[256,256]{1,0:T(8,128)(2,1)S(1)} %shard_map.89), channel_id=1, source_target_pairs={{16,0},{24,8},{32,16},{40,24},{48,32},{56,40},{64,48},{72,56},{80,... | collective-permute-start | bytes 393224 | tf_op jit(solution)/shard_map/ppermute | solution.py:164
  77.6 0.0 all-to-all-done.1.x
  77.6 0.7 shard_map.93
  78.3 11.5 %all-to-all-start.2 = ((f32[32,8,128]{2,1,0:T(8,128)}), f32[32,8,128]{2,1,0:T(8,128)S(1)}, u32[]{:S(2)}, u32[]{:S(2)}) async-start(f32[32,8,128]{2,1,0:T(8,128)} %shard_map.93), calls=%async_computation.2 | async-start | bytes 262144 | tf_op jit(solution)/shard_map/all_to_all | solution.py:168
  89.8 0.0 collective-permute-done.5.got
  89.8 1.9 %collective-permute-start.6 = (bf16[128,384]{1,0:T(8,128)(2,1)S(1)}, bf16[128,384]{1,0:T(8,128)(2,1)S(1)}, u32[]{:S(2)}, u32[]{:S(2)}) collective-permute-start(bf16[128,384]{1,0:T(8,128)(2,1)S(1)} %get-tuple-element.33), channel_id=1, source_target_pairs={{0,8},{8,0},{16,24},{24,16},{32,40},{40,32},{48,56},{56,48},{64,72... | collective-permute-start | bytes 294920 | tf_op jit(solution)/shard_map/ppermute | solution.py:172
  91.7 4.1 %collective-permute-done.6.got = bf16[128,384]{1,0:T(8,128)(2,1)S(1)} collective-permute-done((bf16[128,384]{1,0:T(8,128)(2,1)S(1)}, bf16[128,384]{1,0:T(8,128)(2,1)S(1)}, u32[]{:S(2)}, u32[]{:S(2)}) %collective-permute-start.6) | collective-permute-done | bytes 98336 | tf_op jit(solution)/shard_map/ppermute | solution.py:172
  95.8 0.7 shard_map.91
  96.5 0.8 all-to-all-done.2
  97.4 0.7 copy.10
  (4 shorter events, 0.1 us)
Async XLA Ops:
  1.5 6.0 %collective-permute-start.1 = (bf16[128,256]{1,0:T(8,128)(2,1)S(1)}, bf16[128,256]{1,0:T(8,128)(2,1)S(1)}, u32[]{:S(2)}, u32[]{:S(2)}) collective-permute-start(bf16[128,256]{1,0:T(8,128)(2,1)S(1)} %get-tuple-element.27), channel_id=1, source_target_pairs={{0,8},{8,0},{16,24},{24,16},{32,40},{40,32},{48,56},{56,48},{64,72... | collective-permute-start | bytes 196616 | tf_op jit(solution)/shard_map/ppermute | solution.py:172
  7.6 6.8 %collective-permute-start.2 = (bf16[256,256]{1,0:T(8,128)(2,1)S(1)}, bf16[256,256]{1,0:T(8,128)(2,1)S(1)}, u32[]{:S(2)}, u32[]{:S(2)}) collective-permute-start(bf16[256,256]{1,0:T(8,128)(2,1)S(1)} %shard_map.87.kv0), channel_id=1, source_target_pairs={{0,16},{8,24},{16,32},{24,40},{32,48},{40,56},{48,64},{56,72},{64,... | collective-permute-start | bytes 393224 | tf_op jit(solution)/shard_map/ppermute | solution.py:164
  14.4 15.1 %collective-permute-start.3 = (bf16[256,256]{1,0:T(8,128)(2,1)S(1)}, bf16[256,256]{1,0:T(8,128)(2,1)S(1)}, u32[]{:S(2)}, u32[]{:S(2)}) collective-permute-start(bf16[256,256]{1,0:T(8,128)(2,1)S(1)} %collective-permute-done.2.kv1), channel_id=1, source_target_pairs={{0,16},{8,24},{16,32},{24,40},{32,48},{40,56},{48,64},{56,72},{64,... | collective-permute-start | bytes 393224 | tf_op jit(solution)/shard_map/ppermute | solution.py:164
  24.4 5.0 %collective-permute-start = (bf16[128,256]{1,0:T(8,128)(2,1)S(1)}, bf16[128,256]{1,0:T(8,128)(2,1)S(1)}, u32[]{:S(2)}, u32[]{:S(2)}) collective-permute-start(bf16[128,256]{1,0:T(8,128)(2,1)S(1)} %get-tuple-element.22), channel_id=1, source_target_pairs={{0,8},{8,0},{16,24},{24,16},{32,40},{40,32},{48,56},{56,48},{64,72... | collective-permute-start | bytes 196616 | tf_op jit(solution)/shard_map/ppermute | solution.py:172
  55.2 22.4 %all-to-all-start.1 = ((f32[16,8,128]{2,1,0:T(8,128)}), f32[16,8,128]{2,1,0:T(8,128)S(1)}, u32[]{:S(2)}, u32[]{:S(2)}) async-start(f32[16,8,128]{2,1,0:T(8,128)} %shard_map.92), calls=%async_computation.1 | async-start | bytes 131072 | tf_op jit(solution)/shard_map/all_to_all | solution.py:168
  65.0 11.2 %collective-permute-start.4 = (bf16[256,256]{1,0:T(8,128)(2,1)S(1)}, bf16[256,256]{1,0:T(8,128)(2,1)S(1)}, u32[]{:S(2)}, u32[]{:S(2)}) collective-permute-start(bf16[256,256]{1,0:T(8,128)(2,1)S(1)} %get-tuple-element.28), channel_id=1, source_target_pairs={{16,0},{24,8},{32,16},{40,24},{48,32},{56,40},{64,48},{72,56},{80,... | collective-permute-start | bytes 393224 | tf_op jit(solution)/shard_map/ppermute | solution.py:164
  76.3 13.5 %collective-permute-start.5 = (bf16[256,256]{1,0:T(8,128)(2,1)S(1)}, bf16[256,256]{1,0:T(8,128)(2,1)S(1)}, u32[]{:S(2)}, u32[]{:S(2)}) collective-permute-start(bf16[256,256]{1,0:T(8,128)(2,1)S(1)} %shard_map.89), channel_id=1, source_target_pairs={{16,0},{24,8},{32,16},{40,24},{48,32},{56,40},{64,48},{72,56},{80,... | collective-permute-start | bytes 393224 | tf_op jit(solution)/shard_map/ppermute | solution.py:164
  78.3 19.1 %all-to-all-start.2 = ((f32[32,8,128]{2,1,0:T(8,128)}), f32[32,8,128]{2,1,0:T(8,128)S(1)}, u32[]{:S(2)}, u32[]{:S(2)}) async-start(f32[32,8,128]{2,1,0:T(8,128)} %shard_map.93), calls=%async_computation.2 | async-start | bytes 262144 | tf_op jit(solution)/shard_map/all_to_all | solution.py:168
  89.8 6.0 %collective-permute-start.6 = (bf16[128,384]{1,0:T(8,128)(2,1)S(1)}, bf16[128,384]{1,0:T(8,128)(2,1)S(1)}, u32[]{:S(2)}, u32[]{:S(2)}) collective-permute-start(bf16[128,384]{1,0:T(8,128)(2,1)S(1)} %get-tuple-element.33), channel_id=1, source_target_pairs={{0,8},{8,0},{16,24},{24,16},{32,40},{40,32},{48,56},{56,48},{64,72... | collective-permute-start | bytes 294920 | tf_op jit(solution)/shard_map/ppermute | solution.py:172

commit v7 on v6

v7 whole, which is shorter than its diff:
```python
import jax
import jax.numpy as jnp
from jax import lax
from jax.experimental import pallas as pl
from jax.experimental.pallas import tpu as pltpu
from jax.sharding import PartitionSpec as P


HEAD_DIM = 64
BAND = 512
TOK = 128
REACH = BAND // TOK
HEADS = 2
PAIR = HEADS * HEAD_DIM
ROWS = 2 * TOK
SPAN = BAND + ROWS
DIMS = (4, 4, 4, 4, 2)
SCALE = HEAD_DIM ** (-0.5)
F32 = jnp.float32
BF16 = jnp.bfloat16
NN = ((1,), (0,))
NT = ((1,), (1,))
TN = ((0,), (0,))


def call(body, outs, *args, **kw):
    shapes = [pltpu.VMEM(s, d) if v else jax.ShapeDtypeStruct(s, d) for s, d, v in outs]
    return list(pl.pallas_call(body, out_shape=shapes, **kw)(*args))


def near(x):
    return pltpu.with_memory_space_constraint(x, pltpu.VMEM)


def mm(a, b, dims):
    return lax.dot_general(a, b, (dims, ((), ())), preferred_element_type=F32)


def span(block):
    return slice(block * TOK, (block + 1) * TOK)


def flip_matrix(count):
    row = lax.broadcasted_iota(jnp.int32, (count, count), 0)
    col = lax.broadcasted_iota(jnp.int32, (count, count), 1)
    return jnp.where(row + col == count - 1, 1.0, 0.0).astype(BF16)


def low_lanes(shape):
    return lax.broadcasted_iota(jnp.int32, shape, len(shape) - 1) < HEAD_DIM


def half(b):
    return pl.ds(pl.multiple_of(b * TOK, TOK), TOK)


def pick(take, x):
    low, high = x[:, :PAIR], x[:, PAIR:]
    return jnp.where(take, high, low), jnp.where(take, low, high)


def pack_body(odd, k, v, mine, other):
    for i, x in enumerate((k, v)):
        lanes = slice(i * PAIR, (i + 1) * PAIR)
        mine[:, lanes], other[:, lanes] = pick(odd[0] > 0, x)


def pack_q_body(odd, q, do, emb_t, kv_other, mine, other, erev):
    other[:, : 2 * PAIR] = kv_other[...]
    for i, x in enumerate((q, do)):
        a, b = pick(odd[0] > 0, x)
        mine[:, i * PAIR : (i + 1) * PAIR] = a
        other[:, (i + 2) * PAIR : (i + 3) * PAIR] = b
    flip = flip_matrix(TOK)
    for b in range(REACH):
        back = mm(emb_t[:, span(REACH - 1 - b)], flip, NN).astype(BF16)
        erev[:HEAD_DIM, span(b)] = back
        erev[HEAD_DIM:, span(b)] = back


def unite_body(odd, kv_mine, q_mine, got, near_a, near_b, kv, qs, dos):
    here, there = half(odd[0]), half(1 - odd[0])
    kv[0, here] = near_a[...]
    kv[0, there] = near_b[...]
    kv[1, here] = kv_mine[...]
    kv[1, there] = got[:, : 2 * PAIR]
    low = low_lanes((TOK, PAIR))
    zero = jnp.zeros((TOK, PAIR), BF16)
    for rows, part, first in ((here, q_mine, 0), (there, got, 2)):
        for i, out in enumerate((qs, dos)):
            x = part[:, (first + i) * PAIR : (first + i + 1) * PAIR]
            out[0, rows] = jnp.where(low, x, zero)
            out[1, rows] = jnp.where(low, zero, x)


def main_body(place, qs, dos, erev, kv, far_a, far_b, far, d1, d0, gq, send, gemb, kv2, gqs, d0s):
    here, there = half(place[0]), half(1 - place[0])
    kv2[here] = far_a[...]
    kv2[there] = far_b[...]
    flip = flip_matrix(ROWS)
    row = lax.broadcasted_iota(jnp.int32, (ROWS, SPAN), 0)
    col = lax.broadcasted_iota(jnp.int32, (ROWS, SPAN), 1)
    ahead = col - row - 1
    valid = (ahead >= 0) & (ahead < BAND) & (col >= place[1])
    k = jnp.concatenate([x[:, :PAIR] for x in (kv2, kv.at[0], kv.at[1])], axis=0)
    v = jnp.concatenate([x[:, PAIR:] for x in (kv2, kv.at[0], kv.at[1])], axis=0)
    total = jnp.zeros((PAIR, BAND), F32)
    gk = jnp.zeros((SPAN, PAIR), F32)
    gv = jnp.zeros((SPAN, PAIR), F32)
    gq_parts = []
    for h in range(HEADS):
        q, do = qs[h], dos[h]
        along = jnp.concatenate([mm(q, erev[...], NN), jnp.zeros((ROWS, ROWS), F32)], axis=1)
        s = (pltpu.roll(along, 1, 1, stride=1, stride_axis=0) + mm(q, k, NT)) * SCALE
        s = jnp.where(valid, s, -jnp.inf)
        dp = mm(do, v, NT)
        prob = jnp.exp(s - jnp.max(s, axis=1, keepdims=True))
        prob = prob * (1.0 / jnp.sum(prob, axis=1, keepdims=True))
        prob_b = prob.astype(BF16)
        delta = jnp.sum(prob_b.astype(F32) * dp, axis=1, keepdims=True)
        ds = (prob * (dp - delta) * SCALE).astype(BF16)
        dalong = pltpu.roll(mm(flip, ds, NN), BAND, 1, stride=1, stride_axis=0)[:, :BAND].astype(BF16)
        total = total + mm(mm(flip, q, NN).astype(BF16), dalong, TN)
        gk = gk + mm(ds, q, TN)
        gv = gv + mm(prob_b, do, TN)
        gqe = mm(dalong, erev[...], NT)
        hi = gqe.astype(BF16)
        lo = (gqe - hi.astype(F32)).astype(BF16)
        gq_parts.append(mm(ds, k, NN) + mm(flip, hi, NN) + mm(flip, lo, NN))
    gqs[...] = jnp.where(low_lanes((ROWS, PAIR)), *gq_parts).astype(BF16)
    gq[...] = gqs[here]
    send[:, :PAIR] = gqs[there]
    for part, lanes in ((gk, slice(0, PAIR)), (gv, slice(PAIR, 2 * PAIR))):
        far[:, lanes] = part[:ROWS].astype(BF16)
        d1[:, lanes] = part[ROWS : 2 * ROWS]
        d0s[:, lanes] = part[2 * ROWS :]
    d0[...] = d0s[here]
    send[:, PAIR:] = d0s[there].astype(BF16)
    total = total[:HEAD_DIM] + total[HEAD_DIM:]
    flip = flip_matrix(TOK)
    for b in range(REACH):
        block = total[:, span(REACH - 1 - b)]
        hi = block.astype(BF16)
        lo = (block - hi.astype(F32)).astype(BF16)
        block = mm(hi, flip, NN) + mm(lo, flip, NN)
        for d in range(HEAD_DIM // 8):
            gemb[d * REACH + b] = block[d * 8 : (d + 1) * 8]


def sum_body(x, out):
    out[...] = jnp.broadcast_to(jnp.sum(x[...], axis=0, keepdims=True), out.shape)


def add_body(odd, got, d1, out_a, out_b):
    for rows, out in ((half(odd[0]), out_a), (half(1 - odd[0]), out_b)):
        out[...] = (d1[rows] + got[rows].astype(F32)).astype(BF16)


def final_body(odd, gq, d0, got, got_a, got_b, grad_q, grad_k, grad_v):
    swap = odd[0] > 0
    mine = (d0[...] + got_a[...].astype(F32)).astype(BF16)
    other = (got[:, PAIR:].astype(F32) + got_b[...].astype(F32)).astype(BF16)
    pairs = (gq[...], got[:, :PAIR]), (mine[:, :PAIR], other[:, :PAIR]), (mine[:, PAIR:], other[:, PAIR:])
    for out, (a, b) in zip((grad_q, grad_k, grad_v), pairs):
        out[:, :PAIR] = jnp.where(swap, b, a)
        out[:, PAIR:] = jnp.where(swap, a, b)


SEQ = ("y", "zg", "zi")


def shift(x, steps, cross=False):
    n = lax.axis_size(SEQ)
    pairs = [(s, (s ^ 1 if cross else s) + steps) for s in range(n)]
    return near(lax.ppermute(x, SEQ, [(s, t) for s, t in pairs if 0 <= t < n]))


def exchange(x, axes):
    return lax.all_to_all(x, axes, 0, 0, tiled=True)


def local(query, key_rows, value_matrix_rows, grad_out, rel_embed):
    line, plane = ("zg", "zi"), ("y", "x", "core")
    here = lax.axis_index(SEQ)
    odd = (here & 1).reshape(1)
    sm, vm = pl.BlockSpec(memory_space=pltpu.SMEM), pl.BlockSpec(memory_space=pltpu.VMEM)

    def run(name, body, outs, *args, **kw):
        outs = call(body, outs, *args, in_specs=[sm] + [vm] * (len(args) - 1), **kw)
        return [near(x) for x in outs] if name not in ("main", "final") else outs

    half_unit, unit = ((TOK, 2 * PAIR), BF16, True), (ROWS, 2 * PAIR)
    kv_mine, kv_other = run("pack", pack_body, [half_unit] * 2, odd, key_rows, value_matrix_rows)
    near_a = shift(kv_mine, 2)
    near_b = shift(kv_other, 2, True)
    q_mine, other, erev = run(
        "qpack",
        pack_q_body,
        [half_unit, ((TOK, 4 * PAIR), BF16, True), ((PAIR, BAND), BF16, True)],
        odd, query, grad_out, rel_embed.T, kv_other,
    )
    got = shift(other, 0, True)
    far_a = shift(near_a, 2)
    far_b = shift(near_b, 2)
    heads = ((HEADS, ROWS, PAIR), BF16, True)
    kv, qs, dos = run(
        "unite",
        unite_body,
        [((2, ROWS, 2 * PAIR), BF16, True), heads, heads],
        odd, kv_mine, q_mine, got, near_a, near_b,
    )
    first = ROWS * jnp.maximum(BAND // ROWS - (here >> 1), 0)
    far, d1, d0, gq, send, gemb = run(
        "main",
        main_body,
        [
            (unit, BF16, True),
            (unit, F32, True),
            ((TOK, 2 * PAIR), F32, True),
            ((TOK, PAIR), BF16, True),
            ((TOK, 3 * PAIR), BF16, True),
            ((lax.axis_size(plane), 8, 128), F32, True),
        ],
        jnp.stack([here & 1, first]), qs, dos, erev, kv, far_a, far_b,
        scratch_shapes=[pltpu.VMEM(unit, BF16), pltpu.VMEM((ROWS, PAIR), BF16), pltpu.VMEM(unit, F32)],
    )
    whole = exchange(gemb, plane)
    for axes in (line, plane):
        tiles = ((lax.axis_size(axes), 8, 128), F32, True)
        (whole,) = call(sum_body, [tiles], near(whole))
        whole = exchange(whole, axes)
    grad_embed_t = whole.reshape(8, REACH, 8, 128).transpose(0, 2, 1, 3).reshape(HEAD_DIM, BAND)
    back = shift(far, -2)
    swapped = shift(send, 0, True)
    out_a, out_b = run("add", add_body, [half_unit] * 2, odd, back, near(d1))
    out_a = shift(out_a, -2)
    out_b = shift(out_b, -2, True)
    grads = run("final", final_body, [((TOK, 2 * PAIR), BF16, False)] * 3, odd, near(gq), near(d0), swapped, out_a, out_b)
    return (*grads, grad_embed_t.T)


def solution(mesh):
    fine = jax.sharding.Mesh(mesh.devices.reshape(DIMS), ("y", "zg", "zi", "x", "core"))
    rows = P(SEQ, ("x", "core"))
    return jax.shard_map(
        local,
        mesh=fine,
        in_specs=(rows, rows, rows, rows, P()),
        out_specs=(rows, rows, rows, P()),
        check_vma=False,
    )
```

time: 98.6 us -> 94.3 us (0.956)
  waiting for transfers between devices: 21.5 us -> 18.5 us
  blocking collectives: 21.7 us -> 19.2 us
    ppermute x7 -> x9, waiting for transfers between devices: 20.6 us -> 8.18 us  [shift(): return near(lax.ppermute(x, SEQ, [(s, t) for s, t in pairs if 0 <= t < n]))]
    all_to_all x2, waiting for transfers between devices: 0.82 us -> 10.3 us  [exchange(): return lax.all_to_all(x, axes, 0, 0, tiled=True)]
    all_to_all x2, starting transfers between devices: 21.3 us -> 12.7 us  [exchange(): return lax.all_to_all(x, axes, 0, 0, tiled=True)]
    ppermute x7 -> x9, starting transfers between devices: 24.6 us -> 32.5 us  [shift(): return near(lax.ppermute(x, SEQ, [(s, t) for s, t in pairs if 0 <= t < n]))]
    all_to_all x1, blocking collectives: 21.7 us -> 19.2 us  [exchange(): return lax.all_to_all(x, axes, 0, 0, tiled=True)]
    pallas_call x10 -> x8, Pallas kernels: 7.55 us -> 8.19 us  [call(): return list(pl.pallas_call(body, out_shape=shapes, **kw)(*args))]
  transfers between devices with their start and end apart: 9 -> 11, of which waited for: 6 -> 4; matrix products, arithmetic and copies ran while one was open for 0% -> 1% of each run, Pallas kernels for 3% -> 3%
where the time goes in v7:
time: 94.3 us; the launch traced here: 93.1 us
  starting transfers between devices  45.2 us (48%)
  blocking collectives  19.2 us (20%)
  waiting for transfers between devices  18.5 us (20%)
  Pallas kernels  8.19 us (9%)
    ppermute x9, starting transfers between devices, shift(): return near(lax.ppermute(x, SEQ, [(s, t) for s, t in pairs if 0 <= t < n]))  32.5 us
    all_to_all x1, blocking collectives, exchange(): return lax.all_to_all(x, axes, 0, 0, tiled=True)  19.2 us
    all_to_all x2, starting transfers between devices, exchange(): return lax.all_to_all(x, axes, 0, 0, tiled=True)  12.7 us
    all_to_all x2, waiting for transfers between devices, exchange(): return lax.all_to_all(x, axes, 0, 0, tiled=True)  10.3 us
    pallas_call x8, Pallas kernels, call(): return list(pl.pallas_call(body, out_shape=shapes, **kw)(*args))  8.19 us
    ppermute x9, waiting for transfers between devices, shift(): return near(lax.ppermute(x, SEQ, [(s, t) for s, t in pairs if 0 <= t < n]))  8.18 us
  transfers between devices with their start and end apart: 11, of which 4 were waited for; matrix products, arithmetic and copies ran while one was open for 1% of the time, Pallas kernels for 3%

profile of v7, /device:TPU:1, one launch (start us, length us, event | category | flops | bytes accessed | tf_op | source)
XLA Modules:
  0.0 93.1 jit_solution(5298038046864565050)
XLA Ops:
  0.6 0.9 shard_map.84
  1.5 5.7 %collective-permute-start.1 = (bf16[128,256]{1,0:T(8,128)(2,1)S(1)}, bf16[128,256]{1,0:T(8,128)(2,1)S(1)}, u32[]{:S(2)}, u32[]{:S(2)}) collective-permute-start(bf16[128,256]{1,0:T(8,128)(2,1)S(1)} %get-tuple-element.23.kv_mine), channel_id=1, source_target_pairs={{0,16},{8,24},{16,32},{24,40},{32,48},{40,56},{48,64},{56,72},{64,... | collective-permute-start | bytes 196616 | tf_op jit(solution)/shard_map/ppermute | solution.py:175
  7.3 7.5 %collective-permute-start.2 = (bf16[128,256]{1,0:T(8,128)(2,1)S(1)}, bf16[128,256]{1,0:T(8,128)(2,1)S(1)}, u32[]{:S(2)}, u32[]{:S(2)}) collective-permute-start(bf16[128,256]{1,0:T(8,128)(2,1)S(1)} %get-tuple-element.24.kv_other), channel_id=1, source_target_pairs={{0,24},{8,16},{16,40},{24,32},{32,56},{40,48},{48,72},{56,64},{64,... | collective-permute-start | bytes 196616 | tf_op jit(solution)/shard_map/ppermute | solution.py:175
  14.7 1.1 %shard_map.85 = (bf16[128,256]{1,0:T(8,128)(2,1)S(1)}, bf16[128,512]{1,0:T(8,128)(2,1)S(1)}, bf16[128,512]{1,0:T(8,128)(2,1)S(1)}) custom-call(s32[1]{0:T(128)} %bitcast.odd, bf16[128,256]{1,0:T(8,128)(2,1)} %q.1, bf16[128,256]{1,0:T(8,128)(2,1)} %do.1, bf16[64,512]{1,0:T(8,128)(2,1)} %bitcast.11, bf16[128,256]{1,0:T(8,128)(2,1)S(1)} %get-tuple-element.24.kv_other), custom_call_target="tpu_custom_call" | custom-call | tf_op jit(solution)/shard_map/pallas_call | solution.py:28
  15.8 1.9 %collective-permute-start = (bf16[128,512]{1,0:T(8,128)(2,1)S(1)}, bf16[128,512]{1,0:T(8,128)(2,1)S(1)}, u32[]{:S(2)}, u32[]{:S(2)}) collective-permute-start(bf16[128,512]{1,0:T(8,128)(2,1)S(1)} %get-tuple-element.26), channel_id=1, source_target_pairs={{0,8},{8,0},{16,24},{24,16},{32,40},{40,32},{48,56},{56,48},{64,72... | collective-permute-start | bytes 393224 | tf_op jit(solution)/shard_map/ppermute | solution.py:175
  17.8 0.0 collective-permute-done.1.near_a
  17.8 4.9 %collective-permute-start.3 = (bf16[128,256]{1,0:T(8,128)(2,1)S(1)}, bf16[128,256]{1,0:T(8,128)(2,1)S(1)}, u32[]{:S(2)}, u32[]{:S(2)}) collective-permute-start(bf16[128,256]{1,0:T(8,128)(2,1)S(1)} %collective-permute-done.1.near_a), channel_id=1, source_target_pairs={{0,16},{8,24},{16,32},{24,40},{32,48},{40,56},{48,64},{56,72},{64,... | collective-permute-start | bytes 196616 | tf_op jit(solution)/shard_map/ppermute | solution.py:175
  22.7 0.0 collective-permute-done.2.near_b
  22.7 5.2 %collective-permute-start.4 = (bf16[128,256]{1,0:T(8,128)(2,1)S(1)}, bf16[128,256]{1,0:T(8,128)(2,1)S(1)}, u32[]{:S(2)}, u32[]{:S(2)}) collective-permute-start(bf16[128,256]{1,0:T(8,128)(2,1)S(1)} %collective-permute-done.2.near_b), channel_id=1, source_target_pairs={{0,16},{8,24},{16,32},{24,40},{32,48},{40,56},{48,64},{56,72},{64,... | collective-permute-start | bytes 196616 | tf_op jit(solution)/shard_map/ppermute | solution.py:175
  27.9 0.6 pad_add_fusion.place
  28.5 0.0 collective-permute-done.got
  28.5 0.1 shard_map.86
  28.6 0.0 collective-permute-done.3.far_a
  28.6 0.6 collective-permute-done.4.far_b
  29.2 4.1 %shard_map.87 = (bf16[256,256]{1,0:T(8,128)(2,1)S(1)}, f32[256,256]{1,0:T(8,128)S(1)}, f32[128,256]{1,0:T(8,128)S(1)}, bf16[128,128]{1,0:T(8,128)(2,1)S(1)}, bf1...) custom-call(s32[2]{0:T(128)} %pad_add_fusion.place, bf16[2,256,128]{2,1,0:T(8,128)(2,1)S(1)} %get-tuple-element.27.qs, ...), custom_call_target="tpu_custom_call" | custom-call | tf_op jit(solution)/shard_map/pallas_call | solution.py:28
  33.3 19.2 %all_to_all.15.x = f32[32,8,128]{2,1,0:T(8,128)S(1)} all-to-all(f32[32,8,128]{2,1,0:T(8,128)S(1)} %get-tuple-element.41), channel_id=1, replica_groups=mesh['y'=4,'zg'=4,'zi'=4,'x'=4,'core'=2] {'y','x','core'}, dimensions={0} | all-to-all | bytes 262144 | tf_op jit(solution)/shard_map/all_to_all | solution.py:179
  52.5 0.7 shard_map.90
  53.1 7.0 %all-to-all-start.1 = ((f32[16,8,128]{2,1,0:T(8,128)}), f32[16,8,128]{2,1,0:T(8,128)S(1)}, u32[]{:S(2)}, u32[]{:S(2)}) async-start(f32[16,8,128]{2,1,0:T(8,128)} %shard_map.90), calls=%async_computation.1 | async-start | bytes 131072 | tf_op jit(solution)/shard_map/all_to_all | solution.py:179
  60.1 1.3 %collective-permute-start.6 = (bf16[256,256]{1,0:T(8,128)(2,1)S(1)}, bf16[256,256]{1,0:T(8,128)(2,1)S(1)}, u32[]{:S(2)}, u32[]{:S(2)}) collective-permute-start(bf16[256,256]{1,0:T(8,128)(2,1)S(1)} %get-tuple-element.34), channel_id=1, source_target_pairs={{16,0},{24,8},{32,16},{40,24},{48,32},{56,40},{64,48},{72,56},{80,... | collective-permute-start | bytes 393224 | tf_op jit(solution)/shard_map/ppermute | solution.py:175
  61.4 10.3 %all-to-all-done.1.x = f32[16,8,128]{2,1,0:T(8,128)S(1)} async-done(((f32[16,8,128]{2,1,0:T(8,128)}), f32[16,8,128]{2,1,0:T(8,128)S(1)}, u32[]{:S(2)}, u32[]{:S(2)}) %all-to-all-start.1) | async-done | bytes 65568 | tf_op jit(solution)/shard_map/all_to_all | solution.py:179
  71.7 0.7 shard_map.91
  72.4 5.7 %all-to-all-start.2 = ((f32[32,8,128]{2,1,0:T(8,128)}), f32[32,8,128]{2,1,0:T(8,128)S(1)}, u32[]{:S(2)}, u32[]{:S(2)}) async-start(f32[32,8,128]{2,1,0:T(8,128)} %shard_map.91), calls=%async_computation.2 | async-start | bytes 262144 | tf_op jit(solution)/shard_map/all_to_all | solution.py:179
  78.1 3.5 %collective-permute-start.5 = (bf16[128,384]{1,0:T(8,128)(2,1)S(1)}, bf16[128,384]{1,0:T(8,128)(2,1)S(1)}, u32[]{:S(2)}, u32[]{:S(2)}) collective-permute-start(bf16[128,384]{1,0:T(8,128)(2,1)S(1)} %get-tuple-element.33), channel_id=1, source_target_pairs={{0,8},{8,0},{16,24},{24,16},{32,40},{40,32},{48,56},{56,48},{64,72... | collective-permute-start | bytes 294920 | tf_op jit(solution)/shard_map/ppermute | solution.py:175
  81.5 0.0 collective-permute-done.6.got
  81.6 1.3 %collective-permute-start.7 = (bf16[128,256]{1,0:T(8,128)(2,1)S(1)}, bf16[128,256]{1,0:T(8,128)(2,1)S(1)}, u32[]{:S(2)}, u32[]{:S(2)}) collective-permute-start(bf16[128,256]{1,0:T(8,128)(2,1)S(1)} %get-tuple-element.36), channel_id=1, source_target_pairs={{16,0},{24,8},{32,16},{40,24},{48,32},{56,40},{64,48},{72,56},{80,... | collective-permute-start | bytes 196616 | tf_op jit(solution)/shard_map/ppermute | solution.py:175
  82.9 1.3 %collective-permute-start.8 = (bf16[128,256]{1,0:T(8,128)(2,1)S(1)}, bf16[128,256]{1,0:T(8,128)(2,1)S(1)}, u32[]{:S(2)}, u32[]{:S(2)}) collective-permute-start(bf16[128,256]{1,0:T(8,128)(2,1)S(1)} %get-tuple-element.37), channel_id=1, source_target_pairs={{16,8},{24,0},{32,24},{40,16},{48,40},{56,32},{64,56},{72,48},{80,... | collective-permute-start | bytes 196616 | tf_op jit(solution)/shard_map/ppermute | solution.py:175
  84.2 0.0 collective-permute-done.5.got
  84.2 5.1 %collective-permute-done.7.got_a = bf16[128,256]{1,0:T(8,128)(2,1)S(1)} collective-permute-done((bf16[128,256]{1,0:T(8,128)(2,1)S(1)}, bf16[128,256]{1,0:T(8,128)(2,1)S(1)}, u32[]{:S(2)}, u32[]{:S(2)}) %collective-permute-start.7) | collective-permute-done | bytes 65568 | tf_op jit(solution)/shard_map/ppermute | solution.py:175
  89.3 2.4 %collective-permute-done.8.got_b = bf16[128,256]{1,0:T(8,128)(2,1)S(1)} collective-permute-done((bf16[128,256]{1,0:T(8,128)(2,1)S(1)}, bf16[128,256]{1,0:T(8,128)(2,1)S(1)}, u32[]{:S(2)}, u32[]{:S(2)}) %collective-permute-start.8) | collective-permute-done | bytes 65568 | tf_op jit(solution)/shard_map/ppermute | solution.py:175
  91.7 0.7 shard_map.89
  92.4 0.0 all-to-all-done.2
  92.4 0.7 copy.10
  (1 shorter events, 0.0 us)
Async XLA Ops:
  1.5 16.2 %collective-permute-start.1 = (bf16[128,256]{1,0:T(8,128)(2,1)S(1)}, bf16[128,256]{1,0:T(8,128)(2,1)S(1)}, u32[]{:S(2)}, u32[]{:S(2)}) collective-permute-start(bf16[128,256]{1,0:T(8,128)(2,1)S(1)} %get-tuple-element.23.kv_mine), channel_id=1, source_target_pairs={{0,16},{8,24},{16,32},{24,40},{32,48},{40,56},{48,64},{56,72},{64,... | collective-permute-start | bytes 196616 | tf_op jit(solution)/shard_map/ppermute | solution.py:175
  7.3 15.4 %collective-permute-start.2 = (bf16[128,256]{1,0:T(8,128)(2,1)S(1)}, bf16[128,256]{1,0:T(8,128)(2,1)S(1)}, u32[]{:S(2)}, u32[]{:S(2)}) collective-permute-start(bf16[128,256]{1,0:T(8,128)(2,1)S(1)} %get-tuple-element.24.kv_other), channel_id=1, source_target_pairs={{0,24},{8,16},{16,40},{24,32},{32,56},{40,48},{48,72},{56,64},{64,... | collective-permute-start | bytes 196616 | tf_op jit(solution)/shard_map/ppermute | solution.py:175
  15.8 12.7 %collective-permute-start = (bf16[128,512]{1,0:T(8,128)(2,1)S(1)}, bf16[128,512]{1,0:T(8,128)(2,1)S(1)}, u32[]{:S(2)}, u32[]{:S(2)}) collective-permute-start(bf16[128,512]{1,0:T(8,128)(2,1)S(1)} %get-tuple-element.26), channel_id=1, source_target_pairs={{0,8},{8,0},{16,24},{24,16},{32,40},{40,32},{48,56},{56,48},{64,72... | collective-permute-start | bytes 393224 | tf_op jit(solution)/shard_map/ppermute | solution.py:175
  17.8 10.8 %collective-permute-start.3 = (bf16[128,256]{1,0:T(8,128)(2,1)S(1)}, bf16[128,256]{1,0:T(8,128)(2,1)S(1)}, u32[]{:S(2)}, u32[]{:S(2)}) collective-permute-start(bf16[128,256]{1,0:T(8,128)(2,1)S(1)} %collective-permute-done.1.near_a), channel_id=1, source_target_pairs={{0,16},{8,24},{16,32},{24,40},{32,48},{40,56},{48,64},{56,72},{64,... | collective-permute-start | bytes 196616 | tf_op jit(solution)/shard_map/ppermute | solution.py:175
  22.7 6.5 %collective-permute-start.4 = (bf16[128,256]{1,0:T(8,128)(2,1)S(1)}, bf16[128,256]{1,0:T(8,128)(2,1)S(1)}, u32[]{:S(2)}, u32[]{:S(2)}) collective-permute-start(bf16[128,256]{1,0:T(8,128)(2,1)S(1)} %collective-permute-done.2.near_b), channel_id=1, source_target_pairs={{0,16},{8,24},{16,32},{24,40},{32,48},{40,56},{48,64},{56,72},{64,... | collective-permute-start | bytes 196616 | tf_op jit(solution)/shard_map/ppermute | solution.py:175
  53.1 18.6 %all-to-all-start.1 = ((f32[16,8,128]{2,1,0:T(8,128)}), f32[16,8,128]{2,1,0:T(8,128)S(1)}, u32[]{:S(2)}, u32[]{:S(2)}) async-start(f32[16,8,128]{2,1,0:T(8,128)} %shard_map.90), calls=%async_computation.1 | async-start | bytes 131072 | tf_op jit(solution)/shard_map/all_to_all | solution.py:179
  60.1 21.4 %collective-permute-start.6 = (bf16[256,256]{1,0:T(8,128)(2,1)S(1)}, bf16[256,256]{1,0:T(8,128)(2,1)S(1)}, u32[]{:S(2)}, u32[]{:S(2)}) collective-permute-start(bf16[256,256]{1,0:T(8,128)(2,1)S(1)} %get-tuple-element.34), channel_id=1, source_target_pairs={{16,0},{24,8},{32,16},{40,24},{48,32},{56,40},{64,48},{72,56},{80,... | collective-permute-start | bytes 393224 | tf_op jit(solution)/shard_map/ppermute | solution.py:175
  72.4 20.0 %all-to-all-start.2 = ((f32[32,8,128]{2,1,0:T(8,128)}), f32[32,8,128]{2,1,0:T(8,128)S(1)}, u32[]{:S(2)}, u32[]{:S(2)}) async-start(f32[32,8,128]{2,1,0:T(8,128)} %shard_map.91), calls=%async_computation.2 | async-start | bytes 262144 | tf_op jit(solution)/shard_map/all_to_all | solution.py:179
  78.1 6.1 %collective-permute-start.5 = (bf16[128,384]{1,0:T(8,128)(2,1)S(1)}, bf16[128,384]{1,0:T(8,128)(2,1)S(1)}, u32[]{:S(2)}, u32[]{:S(2)}) collective-permute-start(bf16[128,384]{1,0:T(8,128)(2,1)S(1)} %get-tuple-element.33), channel_id=1, source_target_pairs={{0,8},{8,0},{16,24},{24,16},{32,40},{40,32},{48,56},{56,48},{64,72... | collective-permute-start | bytes 294920 | tf_op jit(solution)/shard_map/ppermute | solution.py:175
  81.6 7.7 %collective-permute-start.7 = (bf16[128,256]{1,0:T(8,128)(2,1)S(1)}, bf16[128,256]{1,0:T(8,128)(2,1)S(1)}, u32[]{:S(2)}, u32[]{:S(2)}) collective-permute-start(bf16[128,256]{1,0:T(8,128)(2,1)S(1)} %get-tuple-element.36), channel_id=1, source_target_pairs={{16,0},{24,8},{32,16},{40,24},{48,32},{56,40},{64,48},{72,56},{80,... | collective-permute-start | bytes 196616 | tf_op jit(solution)/shard_map/ppermute | solution.py:175
  82.9 8.8 %collective-permute-start.8 = (bf16[128,256]{1,0:T(8,128)(2,1)S(1)}, bf16[128,256]{1,0:T(8,128)(2,1)S(1)}, u32[]{:S(2)}, u32[]{:S(2)}) collective-permute-start(bf16[128,256]{1,0:T(8,128)(2,1)S(1)} %get-tuple-element.37), channel_id=1, source_target_pairs={{16,8},{24,0},{32,24},{40,16},{48,40},{56,32},{64,56},{72,48},{80,... | collective-permute-start | bytes 196616 | tf_op jit(solution)/shard_map/ppermute | solution.py:175

commit v8 on v7

--- a/solution.py
+++ b/solution.py
@@ -59,18 +59,14 @@
     return jnp.where(take, high, low), jnp.where(take, low, high)
 
 
-def pack_body(odd, k, v, mine, other):
-    for i, x in enumerate((k, v)):
-        lanes = slice(i * PAIR, (i + 1) * PAIR)
-        mine[:, lanes], other[:, lanes] = pick(odd[0] > 0, x)
-
-
-def pack_q_body(odd, q, do, emb_t, kv_other, mine, other, erev):
-    other[:, : 2 * PAIR] = kv_other[...]
-    for i, x in enumerate((q, do)):
+def pack_body(odd, k, v, q, do, emb_t, kv_mine, kv_other, q_mine, other, erev):
+    for i, x in enumerate((k, v, q, do)):
         a, b = pick(odd[0] > 0, x)
-        mine[:, i * PAIR : (i + 1) * PAIR] = a
-        other[:, (i + 2) * PAIR : (i + 3) * PAIR] = b
+        other[:, i * PAIR : (i + 1) * PAIR] = b
+        lanes = slice(i % 2 * PAIR, (i % 2 + 1) * PAIR)
+        (kv_mine if i < 2 else q_mine)[:, lanes] = a
+        if i < 2:
+            kv_other[:, lanes] = b
     flip = flip_matrix(TOK)
     for b in range(REACH):
         back = mm(emb_t[:, span(REACH - 1 - b)], flip, NN).astype(BF16)
@@ -78,7 +74,7 @@
         erev[HEAD_DIM:, span(b)] = back
 
 
-def unite_body(odd, kv_mine, q_mine, got, near_a, near_b, kv, qs, dos):
+def early_body(odd, kv_mine, q_mine, got, near_a, near_b, kv, qs, dos):
     here, there = half(odd[0]), half(1 - odd[0])
     kv[0, here] = near_a[...]
     kv[0, there] = near_b[...]
@@ -93,15 +89,15 @@
             out[1, rows] = jnp.where(low, zero, x)
 
 
-def main_body(place, qs, dos, erev, kv, far_a, far_b, far, d1, d0, gq, send, gemb, kv2, gqs, d0s):
-    here, there = half(place[0]), half(1 - place[0])
+def main_body(odd, first, qs, dos, erev, kv, far_a, far_b, far, d1, d0, gq, gemb, kv2):
+    here, there = half(odd[0]), half(1 - odd[0])
     kv2[here] = far_a[...]
     kv2[there] = far_b[...]
     flip = flip_matrix(ROWS)
     row = lax.broadcasted_iota(jnp.int32, (ROWS, SPAN), 0)
     col = lax.broadcasted_iota(jnp.int32, (ROWS, SPAN), 1)
     ahead = col - row - 1
-    valid = (ahead >= 0) & (ahead < BAND) & (col >= place[1])
+    valid = (ahead >= 0) & (ahead < BAND) & (col >= first[0])
     k = jnp.concatenate([x[:, :PAIR] for x in (kv2, kv.at[0], kv.at[1])], axis=0)
     v = jnp.concatenate([x[:, PAIR:] for x in (kv2, kv.at[0], kv.at[1])], axis=0)
     total = jnp.zeros((PAIR, BAND), F32)
@@ -127,15 +123,11 @@
         hi = gqe.astype(BF16)
         lo = (gqe - hi.astype(F32)).astype(BF16)
         gq_parts.append(mm(ds, k, NN) + mm(flip, hi, NN) + mm(flip, lo, NN))
-    gqs[...] = jnp.where(low_lanes((ROWS, PAIR)), *gq_parts).astype(BF16)
-    gq[...] = gqs[here]
-    send[:, :PAIR] = gqs[there]
+    gq[...] = jnp.where(low_lanes((ROWS, PAIR)), *gq_parts).astype(BF16)
     for part, lanes in ((gk, slice(0, PAIR)), (gv, slice(PAIR, 2 * PAIR))):
         far[:, lanes] = part[:ROWS].astype(BF16)
         d1[:, lanes] = part[ROWS : 2 * ROWS]
-        d0s[:, lanes] = part[2 * ROWS :]
-    d0[...] = d0s[here]
-    send[:, PAIR:] = d0s[there].astype(BF16)
+        d0[:, lanes] = part[2 * ROWS :]
     total = total[:HEAD_DIM] + total[HEAD_DIM:]
     flip = flip_matrix(TOK)
     for b in range(REACH):
@@ -151,17 +143,21 @@
     out[...] = jnp.broadcast_to(jnp.sum(x[...], axis=0, keepdims=True), out.shape)
 
 
-def add_body(odd, got, d1, out_a, out_b):
-    for rows, out in ((half(odd[0]), out_a), (half(1 - odd[0]), out_b)):
-        out[...] = (d1[rows] + got[rows].astype(F32)).astype(BF16)
-
-
-def final_body(odd, gq, d0, got, got_a, got_b, grad_q, grad_k, grad_v):
+def add_body(got, d1, out):
+    out[...] = (d1[...] + got[...].astype(F32)).astype(BF16)
+
+
+def final_body(odd, got, d0, gq, keep, send):
+    for rows, out in ((half(odd[0]), keep), (half(1 - odd[0]), send)):
+        out[:, :PAIR] = gq[rows]
+        out[:, PAIR:] = (d0[rows] + got[rows].astype(F32)).astype(BF16)
+
+
+def unpack_body(odd, keep, got, *outs):
     swap = odd[0] > 0
-    mine = (d0[...] + got_a[...].astype(F32)).astype(BF16)
-    other = (got[:, PAIR:].astype(F32) + got_b[...].astype(F32)).astype(BF16)
-    pairs = (gq[...], got[:, :PAIR]), (mine[:, :PAIR], other[:, :PAIR]), (mine[:, PAIR:], other[:, PAIR:])
-    for out, (a, b) in zip((grad_q, grad_k, grad_v), pairs):
+    for i, out in enumerate(outs):
+        lanes = slice(i * PAIR, (i + 1) * PAIR)
+        a, b = keep[:, lanes], got[:, lanes]
         out[:, :PAIR] = jnp.where(swap, b, a)
         out[:, PAIR:] = jnp.where(swap, a, b)
 
@@ -183,46 +179,40 @@
     line, plane = ("zg", "zi"), ("y", "x", "core")
     here = lax.axis_index(SEQ)
     odd = (here & 1).reshape(1)
+    first = (ROWS * jnp.maximum(BAND // ROWS - (here >> 1), 0)).reshape(1)
     sm, vm = pl.BlockSpec(memory_space=pltpu.SMEM), pl.BlockSpec(memory_space=pltpu.VMEM)
 
-    def run(name, body, outs, *args, **kw):
-        outs = call(body, outs, *args, in_specs=[sm] + [vm] * (len(args) - 1), **kw)
-        return [near(x) for x in outs] if name not in ("main", "final") else outs
+    def run(name, body, outs, scalars, *args, **kw):
+        specs = [sm] * len(scalars) + [vm] * len(args)
+        outs = call(body, outs, *scalars, *args, in_specs=specs, **kw)
+        return [near(x) for x in outs] if name != "unpack" else outs
 
     half_unit, unit = ((TOK, 2 * PAIR), BF16, True), (ROWS, 2 * PAIR)
-    kv_mine, kv_other = run("pack", pack_body, [half_unit] * 2, odd, key_rows, value_matrix_rows)
+    kv_mine, kv_other, q_mine, other, erev = run(
+        "pack",
+        pack_body,
+        [half_unit] * 3 + [((TOK, 4 * PAIR), BF16, True), ((PAIR, BAND), BF16, True)],
+        [odd], key_rows, value_matrix_rows, query, grad_out, rel_embed.T,
+    )
+    got = shift(other, 0, True)
     near_a = shift(kv_mine, 2)
     near_b = shift(kv_other, 2, True)
-    q_mine, other, erev = run(
-        "qpack",
-        pack_q_body,
-        [half_unit, ((TOK, 4 * PAIR), BF16, True), ((PAIR, BAND), BF16, True)],
-        odd, query, grad_out, rel_embed.T, kv_other,
-    )
-    got = shift(other, 0, True)
     far_a = shift(near_a, 2)
     far_b = shift(near_b, 2)
     heads = ((HEADS, ROWS, PAIR), BF16, True)
     kv, qs, dos = run(
-        "unite",
-        unite_body,
+        "early",
+        early_body,
         [((2, ROWS, 2 * PAIR), BF16, True), heads, heads],
-        odd, kv_mine, q_mine, got, near_a, near_b,
-    )
-    first = ROWS * jnp.maximum(BAND // ROWS - (here >> 1), 0)
-    far, d1, d0, gq, send, gemb = run(
+        [odd], kv_mine, q_mine, got, near_a, near_b,
+    )
+    far, d1, d0, gq, gemb = run(
         "main",
         main_body,
-        [
-            (unit, BF16, True),
-            (unit, F32, True),
-            ((TOK, 2 * PAIR), F32, True),
-            ((TOK, PAIR), BF16, True),
-            ((TOK, 3 * PAIR), BF16, True),
-            ((lax.axis_size(plane), 8, 128), F32, True),
-        ],
-        jnp.stack([here & 1, first]), qs, dos, erev, kv, far_a, far_b,
-        scratch_shapes=[pltpu.VMEM(unit, BF16), pltpu.VMEM((ROWS, PAIR), BF16), pltpu.VMEM(unit, F32)],
+        [(unit, BF16, True), (unit, F32, True), (unit, F32, True), ((ROWS, PAIR), BF16, True)]
+        + [((lax.axis_size(plane), 8, 128), F32, True)],
+        [odd, first], qs, dos, erev, kv, far_a, far_b,
+        scratch_shapes=[pltpu.VMEM(unit, BF16)],
     )
     whole = exchange(gemb, plane)
     for axes in (line, plane):
@@ -231,11 +221,12 @@
         whole = exchange(whole, axes)
     grad_embed_t = whole.reshape(8, REACH, 8, 128).transpose(0, 2, 1, 3).reshape(HEAD_DIM, BAND)
     back = shift(far, -2)
-    swapped = shift(send, 0, True)
-    out_a, out_b = run("add", add_body, [half_unit] * 2, odd, back, near(d1))
-    out_a = shift(out_a, -2)
-    out_b = shift(out_b, -2, True)
-    grads = run("final", final_body, [((TOK, 2 * PAIR), BF16, False)] * 3, odd, near(gq), near(d0), swapped, out_a, out_b)
+    (back,) = run("add", add_body, [(unit, BF16, True)], [], back, d1)
+    back = shift(back, -2)
+    third = ((TOK, 3 * PAIR), BF16, True)
+    keep, send = run("final", final_body, [third] * 2, [odd], back, d0, gq)
+    got = shift(send, 0, True)
+    grads = run("unpack", unpack_body, [((TOK, 2 * PAIR), BF16, False)] * 3, [odd], keep, got)
     return (*grads, grad_embed_t.T)
 
 

time: 94.3 us -> 95.1 us (level)
  starting transfers between devices: 45.2 us -> 51.4 us
  waiting for transfers between devices: 18.5 us -> 16.1 us
  Pallas kernels: 8.19 us -> 6.76 us
    all_to_all x2, waiting for transfers between devices: 10.3 us -> 0.82 us  [exchange(): return lax.all_to_all(x, axes, 0, 0, tiled=True)]
    all_to_all x2, starting transfers between devices: 12.7 us -> 20.9 us  [exchange(): return lax.all_to_all(x, axes, 0, 0, tiled=True)]
    ppermute x9 -> x8, waiting for transfers between devices: 8.18 us -> 15.2 us  [shift(): return near(lax.ppermute(x, SEQ, [(s, t) for s, t in pairs if 0 <= t < n]))]
    ppermute x9 -> x8, starting transfers between devices: 32.5 us -> 30.4 us  [shift(): return near(lax.ppermute(x, SEQ, [(s, t) for s, t in pairs if 0 <= t < n]))]
    pallas_call x8, Pallas kernels: 8.19 us -> 6.76 us  [call(): return list(pl.pallas_call(body, out_shape=shapes, **kw)(*args))]
  transfers between devices with their start and end apart: 11 -> 10, of which waited for: 4 -> 4; matrix products, arithmetic and copies ran while one was open for 1% -> 0% of each run, Pallas kernels for 3% -> 2%
where the time goes in v8:
time: 95.1 us; the launch traced here: 94.6 us
  starting transfers between devices  51.4 us (54%)
  blocking collectives  18.9 us (20%)
  waiting for transfers between devices  16.1 us (17%)
  Pallas kernels  6.76 us (7%)
    ppermute x8, starting transfers between devices, shift(): return near(lax.ppermute(x, SEQ, [(s, t) for s, t in pairs if 0 <= t < n]))  30.4 us
    all_to_all x2, starting transfers between devices, exchange(): return lax.all_to_all(x, axes, 0, 0, tiled=True)  20.9 us
    all_to_all x1, blocking collectives, exchange(): return lax.all_to_all(x, axes, 0, 0, tiled=True)  18.9 us
    ppermute x8, waiting for transfers between devices, shift(): return near(lax.ppermute(x, SEQ, [(s, t) for s, t in pairs if 0 <= t < n]))  15.2 us
    pallas_call x8, Pallas kernels, call(): return list(pl.pallas_call(body, out_shape=shapes, **kw)(*args))  6.76 us
  transfers between devices with their start and end apart: 10, of which 4 were waited for; matrix products, arithmetic and copies ran while one was open for 0% of the time, Pallas kernels for 2%

profile of v8, /device:TPU:1, one launch (start us, length us, event | category | flops | bytes accessed | tf_op | source)
XLA Modules:
  0.0 94.6 jit_solution(547302371546215084)
XLA Ops:
  0.6 1.2 %shard_map.84 = (bf16[128,256]{1,0:T(8,128)(2,1)S(1)}, bf16[128,256]{1,0:T(8,128)(2,1)S(1)}, bf16[128,256]{1,0:T(8,128)(2,1)S(1)}, bf16[128,512]{1,0:T(8,128)(2,1)S(1)}, bf16[128,512]{1,0:T(8,128)(2,1)S(1)}) custom-call(s32[1]{0:T(128)} %bitcast.odd, bf16[128,256]{1,0:T(8,128)(2,1)} %k.1, bf16[128,256]{1,0:T(8,128)(2,1)} %v.1, bf16[128,256]{1,0:T(8,128)(2,1)} %q.1, ...), custom_call_target="tpu_custom_call" | custom-call | tf_op jit(solution)/shard_map/pallas_call | solution.py:28
  1.8 4.4 %collective-permute-start = (bf16[128,512]{1,0:T(8,128)(2,1)S(1)}, bf16[128,512]{1,0:T(8,128)(2,1)S(1)}, u32[]{:S(2)}, u32[]{:S(2)}) collective-permute-start(bf16[128,512]{1,0:T(8,128)(2,1)S(1)} %get-tuple-element.24), channel_id=1, source_target_pairs={{0,8},{8,0},{16,24},{24,16},{32,40},{40,32},{48,56},{56,48},{64,72... | collective-permute-start | bytes 393224 | tf_op jit(solution)/shard_map/ppermute | solution.py:171
  6.2 4.6 %collective-permute-start.2 = (bf16[128,256]{1,0:T(8,128)(2,1)S(1)}, bf16[128,256]{1,0:T(8,128)(2,1)S(1)}, u32[]{:S(2)}, u32[]{:S(2)}) collective-permute-start(bf16[128,256]{1,0:T(8,128)(2,1)S(1)} %get-tuple-element.25), channel_id=1, source_target_pairs={{0,24},{8,16},{16,40},{24,32},{32,56},{40,48},{48,72},{56,64},{64,... | collective-permute-start | bytes 196616 | tf_op jit(solution)/shard_map/ppermute | solution.py:171
  10.8 6.1 %collective-permute-start.1 = (bf16[128,256]{1,0:T(8,128)(2,1)S(1)}, bf16[128,256]{1,0:T(8,128)(2,1)S(1)}, u32[]{:S(2)}, u32[]{:S(2)}) collective-permute-start(bf16[128,256]{1,0:T(8,128)(2,1)S(1)} %get-tuple-element.22.kv_mine), channel_id=1, source_target_pairs={{0,16},{8,24},{16,32},{24,40},{32,48},{40,56},{48,64},{56,72},{64,... | collective-permute-start | bytes 196616 | tf_op jit(solution)/shard_map/ppermute | solution.py:171
  16.9 0.0 collective-permute-done.2.near_b
  17.0 4.9 %collective-permute-start.4 = (bf16[128,256]{1,0:T(8,128)(2,1)S(1)}, bf16[128,256]{1,0:T(8,128)(2,1)S(1)}, u32[]{:S(2)}, u32[]{:S(2)}) collective-permute-start(bf16[128,256]{1,0:T(8,128)(2,1)S(1)} %collective-permute-done.2.near_b), channel_id=1, source_target_pairs={{0,16},{8,24},{16,32},{24,40},{32,48},{40,56},{48,64},{56,72},{64,... | collective-permute-start | bytes 196616 | tf_op jit(solution)/shard_map/ppermute | solution.py:171
  21.9 0.0 collective-permute-done.1.near_a
  21.9 5.9 %collective-permute-start.3 = (bf16[128,256]{1,0:T(8,128)(2,1)S(1)}, bf16[128,256]{1,0:T(8,128)(2,1)S(1)}, u32[]{:S(2)}, u32[]{:S(2)}) collective-permute-start(bf16[128,256]{1,0:T(8,128)(2,1)S(1)} %collective-permute-done.1.near_a), channel_id=1, source_target_pairs={{0,16},{8,24},{16,32},{24,40},{32,48},{40,56},{48,64},{56,72},{64,... | collective-permute-start | bytes 196616 | tf_op jit(solution)/shard_map/ppermute | solution.py:171
  27.8 0.0 collective-permute-done.got
  27.8 0.1 shard_map.85
  27.9 0.0 collective-permute-done.4.far_b
  27.9 1.2 %collective-permute-done.3.far_a = bf16[128,256]{1,0:T(8,128)(2,1)S(1)} collective-permute-done((bf16[128,256]{1,0:T(8,128)(2,1)S(1)}, bf16[128,256]{1,0:T(8,128)(2,1)S(1)}, u32[]{:S(2)}, u32[]{:S(2)}) %collective-permute-start.3) | collective-permute-done | bytes 65568 | tf_op jit(solution)/shard_map/ppermute | solution.py:171
  29.1 3.4 %shard_map.86 = (bf16[256,256]{1,0:T(8,128)(2,1)S(1)}, f32[256,256]{1,0:T(8,128)S(1)}, f32[256,256]{1,0:T(8,128)S(1)}, bf16[256,128]{1,0:T(8,128)(2,1)S(1)}, f32[32,8,128]{2,1,0:T(8,128)S(1)}) custom-call(s32[1]{0:T(128)} %bitcast.odd, s32[1]{0:T(128)} %bitcast.1.first, bf16[2,256,128]{2,1,0:T(8,128)(2,1)S(1)} %get-tuple-element.26.qs, ...), custom_call_target="tpu_custom_call" | custom-call | tf_op jit(solution)/shard_map/pallas_call | solution.py:28
  32.5 18.9 %all_to_all.15.x = f32[32,8,128]{2,1,0:T(8,128)S(1)} all-to-all(f32[32,8,128]{2,1,0:T(8,128)S(1)} %get-tuple-element.39), channel_id=1, replica_groups=mesh['y'=4,'zg'=4,'zi'=4,'x'=4,'core'=2] {'y','x','core'}, dimensions={0} | all-to-all | bytes 262144 | tf_op jit(solution)/shard_map/all_to_all | solution.py:175
  51.5 0.7 shard_map.90
  52.1 9.5 %all-to-all-start.1 = ((f32[16,8,128]{2,1,0:T(8,128)}), f32[16,8,128]{2,1,0:T(8,128)S(1)}, u32[]{:S(2)}, u32[]{:S(2)}) async-start(f32[16,8,128]{2,1,0:T(8,128)} %shard_map.90), calls=%async_computation.1 | async-start | bytes 131072 | tf_op jit(solution)/shard_map/all_to_all | solution.py:175
  61.6 1.3 %collective-permute-start.5 = (bf16[256,256]{1,0:T(8,128)(2,1)S(1)}, bf16[256,256]{1,0:T(8,128)(2,1)S(1)}, u32[]{:S(2)}, u32[]{:S(2)}) collective-permute-start(bf16[256,256]{1,0:T(8,128)(2,1)S(1)} %get-tuple-element.30), channel_id=1, source_target_pairs={{16,0},{24,8},{32,16},{40,24},{48,32},{56,40},{64,48},{72,56},{80,... | collective-permute-start | bytes 393224 | tf_op jit(solution)/shard_map/ppermute | solution.py:171
  62.9 9.9 %collective-permute-done.5.got = bf16[256,256]{1,0:T(8,128)(2,1)S(1)} collective-permute-done((bf16[256,256]{1,0:T(8,128)(2,1)S(1)}, bf16[256,256]{1,0:T(8,128)(2,1)S(1)}, u32[]{:S(2)}, u32[]{:S(2)}) %collective-permute-start.5) | collective-permute-done | bytes 131104 | tf_op jit(solution)/shard_map/ppermute | solution.py:171
  72.8 1.3 %collective-permute-start.6 = (bf16[256,256]{1,0:T(8,128)(2,1)S(1)}, bf16[256,256]{1,0:T(8,128)(2,1)S(1)}, u32[]{:S(2)}, u32[]{:S(2)}) collective-permute-start(bf16[256,256]{1,0:T(8,128)(2,1)S(1)} %shard_map.87), channel_id=1, source_target_pairs={{16,0},{24,8},{32,16},{40,24},{48,32},{56,40},{64,48},{72,56},{80,... | collective-permute-start | bytes 393224 | tf_op jit(solution)/shard_map/ppermute | solution.py:171
  74.1 0.0 all-to-all-done.1.x
  74.2 0.7 shard_map.91
  74.8 11.5 %all-to-all-start.2 = ((f32[32,8,128]{2,1,0:T(8,128)}), f32[32,8,128]{2,1,0:T(8,128)S(1)}, u32[]{:S(2)}, u32[]{:S(2)}) async-start(f32[32,8,128]{2,1,0:T(8,128)} %shard_map.91), calls=%async_computation.2 | async-start | bytes 262144 | tf_op jit(solution)/shard_map/all_to_all | solution.py:175
  86.3 0.0 collective-permute-done.6.got
  86.4 1.9 %collective-permute-start.7 = (bf16[128,384]{1,0:T(8,128)(2,1)S(1)}, bf16[128,384]{1,0:T(8,128)(2,1)S(1)}, u32[]{:S(2)}, u32[]{:S(2)}) collective-permute-start(bf16[128,384]{1,0:T(8,128)(2,1)S(1)} %get-tuple-element.35), channel_id=1, source_target_pairs={{0,8},{8,0},{16,24},{24,16},{32,40},{40,32},{48,56},{56,48},{64,72... | collective-permute-start | bytes 294920 | tf_op jit(solution)/shard_map/ppermute | solution.py:171
  88.3 4.1 %collective-permute-done.7.got = bf16[128,384]{1,0:T(8,128)(2,1)S(1)} collective-permute-done((bf16[128,384]{1,0:T(8,128)(2,1)S(1)}, bf16[128,384]{1,0:T(8,128)(2,1)S(1)}, u32[]{:S(2)}, u32[]{:S(2)}) %collective-permute-start.7) | collective-permute-done | bytes 98336 | tf_op jit(solution)/shard_map/ppermute | solution.py:171
  92.4 0.7 shard_map.89
  93.1 0.8 all-to-all-done.2
  93.9 0.7 copy.10
  (2 shorter events, 0.1 us)
Async XLA Ops:
  1.8 26.0 %collective-permute-start = (bf16[128,512]{1,0:T(8,128)(2,1)S(1)}, bf16[128,512]{1,0:T(8,128)(2,1)S(1)}, u32[]{:S(2)}, u32[]{:S(2)}) collective-permute-start(bf16[128,512]{1,0:T(8,128)(2,1)S(1)} %get-tuple-element.24), channel_id=1, source_target_pairs={{0,8},{8,0},{16,24},{24,16},{32,40},{40,32},{48,56},{56,48},{64,72... | collective-permute-start | bytes 393224 | tf_op jit(solution)/shard_map/ppermute | solution.py:171
  6.2 10.8 %collective-permute-start.2 = (bf16[128,256]{1,0:T(8,128)(2,1)S(1)}, bf16[128,256]{1,0:T(8,128)(2,1)S(1)}, u32[]{:S(2)}, u32[]{:S(2)}) collective-permute-start(bf16[128,256]{1,0:T(8,128)(2,1)S(1)} %get-tuple-element.25), channel_id=1, source_target_pairs={{0,24},{8,16},{16,40},{24,32},{32,56},{40,48},{48,72},{56,64},{64,... | collective-permute-start | bytes 196616 | tf_op jit(solution)/shard_map/ppermute | solution.py:171
  10.8 11.0 %collective-permute-start.1 = (bf16[128,256]{1,0:T(8,128)(2,1)S(1)}, bf16[128,256]{1,0:T(8,128)(2,1)S(1)}, u32[]{:S(2)}, u32[]{:S(2)}) collective-permute-start(bf16[128,256]{1,0:T(8,128)(2,1)S(1)} %get-tuple-element.22.kv_mine), channel_id=1, source_target_pairs={{0,16},{8,24},{16,32},{24,40},{32,48},{40,56},{48,64},{56,72},{64,... | collective-permute-start | bytes 196616 | tf_op jit(solution)/shard_map/ppermute | solution.py:171
  17.0 10.9 %collective-permute-start.4 = (bf16[128,256]{1,0:T(8,128)(2,1)S(1)}, bf16[128,256]{1,0:T(8,128)(2,1)S(1)}, u32[]{:S(2)}, u32[]{:S(2)}) collective-permute-start(bf16[128,256]{1,0:T(8,128)(2,1)S(1)} %collective-permute-done.2.near_b), channel_id=1, source_target_pairs={{0,16},{8,24},{16,32},{24,40},{32,48},{40,56},{48,64},{56,72},{64,... | collective-permute-start | bytes 196616 | tf_op jit(solution)/shard_map/ppermute | solution.py:171
  21.9 7.2 %collective-permute-start.3 = (bf16[128,256]{1,0:T(8,128)(2,1)S(1)}, bf16[128,256]{1,0:T(8,128)(2,1)S(1)}, u32[]{:S(2)}, u32[]{:S(2)}) collective-permute-start(bf16[128,256]{1,0:T(8,128)(2,1)S(1)} %collective-permute-done.1.near_a), channel_id=1, source_target_pairs={{0,16},{8,24},{16,32},{24,40},{32,48},{40,56},{48,64},{56,72},{64,... | collective-permute-start | bytes 196616 | tf_op jit(solution)/shard_map/ppermute | solution.py:171
  52.1 22.0 %all-to-all-start.1 = ((f32[16,8,128]{2,1,0:T(8,128)}), f32[16,8,128]{2,1,0:T(8,128)S(1)}, u32[]{:S(2)}, u32[]{:S(2)}) async-start(f32[16,8,128]{2,1,0:T(8,128)} %shard_map.90), calls=%async_computation.1 | async-start | bytes 131072 | tf_op jit(solution)/shard_map/all_to_all | solution.py:175
  61.6 11.2 %collective-permute-start.5 = (bf16[256,256]{1,0:T(8,128)(2,1)S(1)}, bf16[256,256]{1,0:T(8,128)(2,1)S(1)}, u32[]{:S(2)}, u32[]{:S(2)}) collective-permute-start(bf16[256,256]{1,0:T(8,128)(2,1)S(1)} %get-tuple-element.30), channel_id=1, source_target_pairs={{16,0},{24,8},{32,16},{40,24},{48,32},{56,40},{64,48},{72,56},{80,... | collective-permute-start | bytes 393224 | tf_op jit(solution)/shard_map/ppermute | solution.py:171
  72.8 13.5 %collective-permute-start.6 = (bf16[256,256]{1,0:T(8,128)(2,1)S(1)}, bf16[256,256]{1,0:T(8,128)(2,1)S(1)}, u32[]{:S(2)}, u32[]{:S(2)}) collective-permute-start(bf16[256,256]{1,0:T(8,128)(2,1)S(1)} %shard_map.87), channel_id=1, source_target_pairs={{16,0},{24,8},{32,16},{40,24},{48,32},{56,40},{64,48},{72,56},{80,... | collective-permute-start | bytes 393224 | tf_op jit(solution)/shard_map/ppermute | solution.py:171
  74.8 19.1 %all-to-all-start.2 = ((f32[32,8,128]{2,1,0:T(8,128)}), f32[32,8,128]{2,1,0:T(8,128)S(1)}, u32[]{:S(2)}, u32[]{:S(2)}) async-start(f32[32,8,128]{2,1,0:T(8,128)} %shard_map.91), calls=%async_computation.2 | async-start | bytes 262144 | tf_op jit(solution)/shard_map/all_to_all | solution.py:175
  86.4 6.0 %collective-permute-start.7 = (bf16[128,384]{1,0:T(8,128)(2,1)S(1)}, bf16[128,384]{1,0:T(8,128)(2,1)S(1)}, u32[]{:S(2)}, u32[]{:S(2)}) collective-permute-start(bf16[128,384]{1,0:T(8,128)(2,1)S(1)} %get-tuple-element.35), channel_id=1, source_target_pairs={{0,8},{8,0},{16,24},{24,16},{32,40},{40,32},{48,56},{56,48},{64,72... | collective-permute-start | bytes 294920 | tf_op jit(solution)/shard_map/ppermute | solution.py:171

commit v9 on v8

--- a/solution.py
+++ b/solution.py
@@ -74,7 +74,7 @@
         erev[HEAD_DIM:, span(b)] = back
 
 
-def early_body(odd, kv_mine, q_mine, got, near_a, near_b, kv, qs, dos):
+def early_body(odd, kv_mine, q_mine, got, near_a, near_b, kv, qs, dos, qf):
     here, there = half(odd[0]), half(1 - odd[0])
     kv[0, here] = near_a[...]
     kv[0, there] = near_b[...]
@@ -87,9 +87,12 @@
             x = part[:, (first + i) * PAIR : (first + i + 1) * PAIR]
             out[0, rows] = jnp.where(low, x, zero)
             out[1, rows] = jnp.where(low, zero, x)
-
-
-def main_body(odd, first, qs, dos, erev, kv, far_a, far_b, far, d1, d0, gq, gemb, kv2):
+    flip = flip_matrix(ROWS)
+    for h in range(HEADS):
+        qf[h] = mm(flip, qs[h], NN).astype(BF16)
+
+
+def main_body(odd, first, qs, dos, qf, erev, kv, far_a, far_b, far, d1, d0, gq, gemb, kv2):
     here, there = half(odd[0]), half(1 - odd[0])
     kv2[here] = far_a[...]
     kv2[there] = far_b[...]
@@ -101,9 +104,9 @@
     k = jnp.concatenate([x[:, :PAIR] for x in (kv2, kv.at[0], kv.at[1])], axis=0)
     v = jnp.concatenate([x[:, PAIR:] for x in (kv2, kv.at[0], kv.at[1])], axis=0)
     total = jnp.zeros((PAIR, BAND), F32)
-    gk = jnp.zeros((SPAN, PAIR), F32)
-    gv = jnp.zeros((SPAN, PAIR), F32)
-    gq_parts = []
+    gk = jnp.zeros((PAIR, SPAN), F32)
+    gv = jnp.zeros((PAIR, SPAN), F32)
+    gq_parts, gqe_parts = [], []
     for h in range(HEADS):
         q, do = qs[h], dos[h]
         along = jnp.concatenate([mm(q, erev[...], NN), jnp.zeros((ROWS, ROWS), F32)], axis=1)
@@ -116,15 +119,17 @@
         delta = jnp.sum(prob_b.astype(F32) * dp, axis=1, keepdims=True)
         ds = (prob * (dp - delta) * SCALE).astype(BF16)
         dalong = pltpu.roll(mm(flip, ds, NN), BAND, 1, stride=1, stride_axis=0)[:, :BAND].astype(BF16)
-        total = total + mm(mm(flip, q, NN).astype(BF16), dalong, TN)
-        gk = gk + mm(ds, q, TN)
-        gv = gv + mm(prob_b, do, TN)
-        gqe = mm(dalong, erev[...], NT)
-        hi = gqe.astype(BF16)
-        lo = (gqe - hi.astype(F32)).astype(BF16)
-        gq_parts.append(mm(ds, k, NN) + mm(flip, hi, NN) + mm(flip, lo, NN))
-    gq[...] = jnp.where(low_lanes((ROWS, PAIR)), *gq_parts).astype(BF16)
-    for part, lanes in ((gk, slice(0, PAIR)), (gv, slice(PAIR, 2 * PAIR))):
+        total = total + mm(qf[h], dalong, TN)
+        gk = gk + mm(q, ds, TN)
+        gv = gv + mm(do, prob_b, TN)
+        gq_parts.append(mm(ds, k, NN))
+        gqe_parts.append(mm(dalong, erev[...], NT))
+    low = low_lanes((ROWS, PAIR))
+    gqe = jnp.where(low, *gqe_parts)
+    hi = gqe.astype(BF16)
+    lo = (gqe - hi.astype(F32)).astype(BF16)
+    gq[...] = (jnp.where(low, *gq_parts) + mm(flip, hi, NN) + mm(flip, lo, NN)).astype(BF16)
+    for part, lanes in ((gk.T, slice(0, PAIR)), (gv.T, slice(PAIR, 2 * PAIR))):
         far[:, lanes] = part[:ROWS].astype(BF16)
         d1[:, lanes] = part[ROWS : 2 * ROWS]
         d0[:, lanes] = part[2 * ROWS :]
@@ -200,10 +205,10 @@
     far_a = shift(near_a, 2)
     far_b = shift(near_b, 2)
     heads = ((HEADS, ROWS, PAIR), BF16, True)
-    kv, qs, dos = run(
+    kv, qs, dos, qf = run(
         "early",
         early_body,
-        [((2, ROWS, 2 * PAIR), BF16, True), heads, heads],
+        [((2, ROWS, 2 * PAIR), BF16, True), heads, heads, heads],
         [odd], kv_mine, q_mine, got, near_a, near_b,
     )
     far, d1, d0, gq, gemb = run(
@@ -211,7 +216,7 @@
         main_body,
         [(unit, BF16, True), (unit, F32, True), (unit, F32, True), ((ROWS, PAIR), BF16, True)]
         + [((lax.axis_size(plane), 8, 128), F32, True)],
-        [odd, first], qs, dos, erev, kv, far_a, far_b,
+        [odd, first], qs, dos, qf, erev, kv, far_a, far_b,
         scratch_shapes=[pltpu.VMEM(unit, BF16)],
     )
     whole = exchange(gemb, plane)

time: 95.1 us -> 94.5 us (level)
  no operation moved by 1% of the time
where the time goes in v9:
time: 94.5 us; the launch traced here: 94 us
  starting transfers between devices  51.4 us (54%)
  blocking collectives  18.9 us (20%)
  waiting for transfers between devices  15.9 us (17%)
  Pallas kernels  6.37 us (7%)
    ppermute x8, starting transfers between devices, shift(): return near(lax.ppermute(x, SEQ, [(s, t) for s, t in pairs if 0 <= t < n]))  30.4 us
    all_to_all x2, starting transfers between devices, exchange(): return lax.all_to_all(x, axes, 0, 0, tiled=True)  20.9 us
    all_to_all x1, blocking collectives, exchange(): return lax.all_to_all(x, axes, 0, 0, tiled=True)  18.9 us
    ppermute x8, waiting for transfers between devices, shift(): return near(lax.ppermute(x, SEQ, [(s, t) for s, t in pairs if 0 <= t < n]))  15 us
    pallas_call x8, Pallas kernels, call(): return list(pl.pallas_call(body, out_shape=shapes, **kw)(*args))  6.37 us
  transfers between devices with their start and end apart: 10, of which 4 were waited for; matrix products, arithmetic and copies ran while one was open for 0% of the time, Pallas kernels for 2%

profile of v9, /device:TPU:1, one launch (start us, length us, event | category | flops | bytes accessed | tf_op | source)
XLA Modules:
  0.0 94.0 jit_solution(11705295554790840682)
XLA Ops:
  0.6 1.2 %shard_map.84 = (bf16[128,256]{1,0:T(8,128)(2,1)S(1)}, bf16[128,256]{1,0:T(8,128)(2,1)S(1)}, bf16[128,256]{1,0:T(8,128)(2,1)S(1)}, bf16[128,512]{1,0:T(8,128)(2,1)S(1)}, bf16[128,512]{1,0:T(8,128)(2,1)S(1)}) custom-call(s32[1]{0:T(128)} %bitcast.odd, bf16[128,256]{1,0:T(8,128)(2,1)} %k.1, bf16[128,256]{1,0:T(8,128)(2,1)} %v.1, bf16[128,256]{1,0:T(8,128)(2,1)} %q.1, ...), custom_call_target="tpu_custom_call" | custom-call | tf_op jit(solution)/shard_map/pallas_call | solution.py:28
  1.8 4.4 %collective-permute-start = (bf16[128,512]{1,0:T(8,128)(2,1)S(1)}, bf16[128,512]{1,0:T(8,128)(2,1)S(1)}, u32[]{:S(2)}, u32[]{:S(2)}) collective-permute-start(bf16[128,512]{1,0:T(8,128)(2,1)S(1)} %get-tuple-element.25), channel_id=1, source_target_pairs={{0,8},{8,0},{16,24},{24,16},{32,40},{40,32},{48,56},{56,48},{64,72... | collective-permute-start | bytes 393224 | tf_op jit(solution)/shard_map/ppermute | solution.py:176
  6.2 4.6 %collective-permute-start.2 = (bf16[128,256]{1,0:T(8,128)(2,1)S(1)}, bf16[128,256]{1,0:T(8,128)(2,1)S(1)}, u32[]{:S(2)}, u32[]{:S(2)}) collective-permute-start(bf16[128,256]{1,0:T(8,128)(2,1)S(1)} %get-tuple-element.26), channel_id=1, source_target_pairs={{0,24},{8,16},{16,40},{24,32},{32,56},{40,48},{48,72},{56,64},{64,... | collective-permute-start | bytes 196616 | tf_op jit(solution)/shard_map/ppermute | solution.py:176
  10.8 6.1 %collective-permute-start.1 = (bf16[128,256]{1,0:T(8,128)(2,1)S(1)}, bf16[128,256]{1,0:T(8,128)(2,1)S(1)}, u32[]{:S(2)}, u32[]{:S(2)}) collective-permute-start(bf16[128,256]{1,0:T(8,128)(2,1)S(1)} %get-tuple-element.23.kv_mine), channel_id=1, source_target_pairs={{0,16},{8,24},{16,32},{24,40},{32,48},{40,56},{48,64},{56,72},{64,... | collective-permute-start | bytes 196616 | tf_op jit(solution)/shard_map/ppermute | solution.py:176
  16.9 0.0 collective-permute-done.2.near_b
  17.0 4.9 %collective-permute-start.4 = (bf16[128,256]{1,0:T(8,128)(2,1)S(1)}, bf16[128,256]{1,0:T(8,128)(2,1)S(1)}, u32[]{:S(2)}, u32[]{:S(2)}) collective-permute-start(bf16[128,256]{1,0:T(8,128)(2,1)S(1)} %collective-permute-done.2.near_b), channel_id=1, source_target_pairs={{0,16},{8,24},{16,32},{24,40},{32,48},{40,56},{48,64},{56,72},{64,... | collective-permute-start | bytes 196616 | tf_op jit(solution)/shard_map/ppermute | solution.py:176
  21.9 0.0 collective-permute-done.1.near_a
  21.9 5.9 %collective-permute-start.3 = (bf16[128,256]{1,0:T(8,128)(2,1)S(1)}, bf16[128,256]{1,0:T(8,128)(2,1)S(1)}, u32[]{:S(2)}, u32[]{:S(2)}) collective-permute-start(bf16[128,256]{1,0:T(8,128)(2,1)S(1)} %collective-permute-done.1.near_a), channel_id=1, source_target_pairs={{0,16},{8,24},{16,32},{24,40},{32,48},{40,56},{48,64},{56,72},{64,... | collective-permute-start | bytes 196616 | tf_op jit(solution)/shard_map/ppermute | solution.py:176
  27.8 0.0 collective-permute-done.got
  27.8 0.3 shard_map.85
  28.1 0.0 collective-permute-done.4.far_b
  28.1 1.0 %collective-permute-done.3.far_a = bf16[128,256]{1,0:T(8,128)(2,1)S(1)} collective-permute-done((bf16[128,256]{1,0:T(8,128)(2,1)S(1)}, bf16[128,256]{1,0:T(8,128)(2,1)S(1)}, u32[]{:S(2)}, u32[]{:S(2)}) %collective-permute-start.3) | collective-permute-done | bytes 65568 | tf_op jit(solution)/shard_map/ppermute | solution.py:176
  29.1 2.8 %shard_map.86 = (bf16[256,256]{1,0:T(8,128)(2,1)S(1)}, f32[256,256]{1,0:T(8,128)S(1)}, f32[256,256]{1,0:T(8,128)S(1)}, bf16[256,128]{1,0:T(8,128)(2,1)S(1)}, f32[32,8,128]{2,1,0:T(8,128)S(1)}) custom-call(s32[1]{0:T(128)} %bitcast.odd, s32[1]{0:T(128)} %bitcast.1.first, bf16[2,256,128]{2,1,0:T(8,128)(2,1)S(1)} %get-tuple-element.27.qs, ...), custom_call_target="tpu_custom_call" | custom-call | tf_op jit(solution)/shard_map/pallas_call | solution.py:28
  31.9 18.9 %all_to_all.15.x = f32[32,8,128]{2,1,0:T(8,128)S(1)} all-to-all(f32[32,8,128]{2,1,0:T(8,128)S(1)} %get-tuple-element.41), channel_id=1, replica_groups=mesh['y'=4,'zg'=4,'zi'=4,'x'=4,'core'=2] {'y','x','core'}, dimensions={0} | all-to-all | bytes 262144 | tf_op jit(solution)/shard_map/all_to_all | solution.py:180
  50.8 0.7 shard_map.90
  51.5 9.5 %all-to-all-start.1 = ((f32[16,8,128]{2,1,0:T(8,128)}), f32[16,8,128]{2,1,0:T(8,128)S(1)}, u32[]{:S(2)}, u32[]{:S(2)}) async-start(f32[16,8,128]{2,1,0:T(8,128)} %shard_map.90), calls=%async_computation.1 | async-start | bytes 131072 | tf_op jit(solution)/shard_map/all_to_all | solution.py:180
  61.0 1.3 %collective-permute-start.5 = (bf16[256,256]{1,0:T(8,128)(2,1)S(1)}, bf16[256,256]{1,0:T(8,128)(2,1)S(1)}, u32[]{:S(2)}, u32[]{:S(2)}) collective-permute-start(bf16[256,256]{1,0:T(8,128)(2,1)S(1)} %get-tuple-element.32), channel_id=1, source_target_pairs={{16,0},{24,8},{32,16},{40,24},{48,32},{56,40},{64,48},{72,56},{80,... | collective-permute-start | bytes 393224 | tf_op jit(solution)/shard_map/ppermute | solution.py:176
  62.3 9.9 %collective-permute-done.5.got = bf16[256,256]{1,0:T(8,128)(2,1)S(1)} collective-permute-done((bf16[256,256]{1,0:T(8,128)(2,1)S(1)}, bf16[256,256]{1,0:T(8,128)(2,1)S(1)}, u32[]{:S(2)}, u32[]{:S(2)}) %collective-permute-start.5) | collective-permute-done | bytes 131104 | tf_op jit(solution)/shard_map/ppermute | solution.py:176
  72.2 1.3 %collective-permute-start.6 = (bf16[256,256]{1,0:T(8,128)(2,1)S(1)}, bf16[256,256]{1,0:T(8,128)(2,1)S(1)}, u32[]{:S(2)}, u32[]{:S(2)}) collective-permute-start(bf16[256,256]{1,0:T(8,128)(2,1)S(1)} %shard_map.87), channel_id=1, source_target_pairs={{16,0},{24,8},{32,16},{40,24},{48,32},{56,40},{64,48},{72,56},{80,... | collective-permute-start | bytes 393224 | tf_op jit(solution)/shard_map/ppermute | solution.py:176
  73.5 0.0 all-to-all-done.1.x
  73.6 0.7 shard_map.91
  74.2 11.5 %all-to-all-start.2 = ((f32[32,8,128]{2,1,0:T(8,128)}), f32[32,8,128]{2,1,0:T(8,128)S(1)}, u32[]{:S(2)}, u32[]{:S(2)}) async-start(f32[32,8,128]{2,1,0:T(8,128)} %shard_map.91), calls=%async_computation.2 | async-start | bytes 262144 | tf_op jit(solution)/shard_map/all_to_all | solution.py:180
  85.7 0.0 collective-permute-done.6.got
  85.8 1.9 %collective-permute-start.7 = (bf16[128,384]{1,0:T(8,128)(2,1)S(1)}, bf16[128,384]{1,0:T(8,128)(2,1)S(1)}, u32[]{:S(2)}, u32[]{:S(2)}) collective-permute-start(bf16[128,384]{1,0:T(8,128)(2,1)S(1)} %get-tuple-element.37), channel_id=1, source_target_pairs={{0,8},{8,0},{16,24},{24,16},{32,40},{40,32},{48,56},{56,48},{64,72... | collective-permute-start | bytes 294920 | tf_op jit(solution)/shard_map/ppermute | solution.py:176
  87.7 4.1 %collective-permute-done.7.got = bf16[128,384]{1,0:T(8,128)(2,1)S(1)} collective-permute-done((bf16[128,384]{1,0:T(8,128)(2,1)S(1)}, bf16[128,384]{1,0:T(8,128)(2,1)S(1)}, u32[]{:S(2)}, u32[]{:S(2)}) %collective-permute-start.7) | collective-permute-done | bytes 98336 | tf_op jit(solution)/shard_map/ppermute | solution.py:176
  91.8 0.7 shard_map.89
  92.5 0.8 all-to-all-done.2
  93.3 0.7 copy.10
  (2 shorter events, 0.1 us)
Async XLA Ops:
  1.8 26.0 %collective-permute-start = (bf16[128,512]{1,0:T(8,128)(2,1)S(1)}, bf16[128,512]{1,0:T(8,128)(2,1)S(1)}, u32[]{:S(2)}, u32[]{:S(2)}) collective-permute-start(bf16[128,512]{1,0:T(8,128)(2,1)S(1)} %get-tuple-element.25), channel_id=1, source_target_pairs={{0,8},{8,0},{16,24},{24,16},{32,40},{40,32},{48,56},{56,48},{64,72... | collective-permute-start | bytes 393224 | tf_op jit(solution)/shard_map/ppermute | solution.py:176
  6.2 10.8 %collective-permute-start.2 = (bf16[128,256]{1,0:T(8,128)(2,1)S(1)}, bf16[128,256]{1,0:T(8,128)(2,1)S(1)}, u32[]{:S(2)}, u32[]{:S(2)}) collective-permute-start(bf16[128,256]{1,0:T(8,128)(2,1)S(1)} %get-tuple-element.26), channel_id=1, source_target_pairs={{0,24},{8,16},{16,40},{24,32},{32,56},{40,48},{48,72},{56,64},{64,... | collective-permute-start | bytes 196616 | tf_op jit(solution)/shard_map/ppermute | solution.py:176
  10.8 11.0 %collective-permute-start.1 = (bf16[128,256]{1,0:T(8,128)(2,1)S(1)}, bf16[128,256]{1,0:T(8,128)(2,1)S(1)}, u32[]{:S(2)}, u32[]{:S(2)}) collective-permute-start(bf16[128,256]{1,0:T(8,128)(2,1)S(1)} %get-tuple-element.23.kv_mine), channel_id=1, source_target_pairs={{0,16},{8,24},{16,32},{24,40},{32,48},{40,56},{48,64},{56,72},{64,... | collective-permute-start | bytes 196616 | tf_op jit(solution)/shard_map/ppermute | solution.py:176
  17.0 11.2 %collective-permute-start.4 = (bf16[128,256]{1,0:T(8,128)(2,1)S(1)}, bf16[128,256]{1,0:T(8,128)(2,1)S(1)}, u32[]{:S(2)}, u32[]{:S(2)}) collective-permute-start(bf16[128,256]{1,0:T(8,128)(2,1)S(1)} %collective-permute-done.2.near_b), channel_id=1, source_target_pairs={{0,16},{8,24},{16,32},{24,40},{32,48},{40,56},{48,64},{56,72},{64,... | collective-permute-start | bytes 196616 | tf_op jit(solution)/shard_map/ppermute | solution.py:176
  21.9 7.2 %collective-permute-start.3 = (bf16[128,256]{1,0:T(8,128)(2,1)S(1)}, bf16[128,256]{1,0:T(8,128)(2,1)S(1)}, u32[]{:S(2)}, u32[]{:S(2)}) collective-permute-start(bf16[128,256]{1,0:T(8,128)(2,1)S(1)} %collective-permute-done.1.near_a), channel_id=1, source_target_pairs={{0,16},{8,24},{16,32},{24,40},{32,48},{40,56},{48,64},{56,72},{64,... | collective-permute-start | bytes 196616 | tf_op jit(solution)/shard_map/ppermute | solution.py:176
  51.5 22.0 %all-to-all-start.1 = ((f32[16,8,128]{2,1,0:T(8,128)}), f32[16,8,128]{2,1,0:T(8,128)S(1)}, u32[]{:S(2)}, u32[]{:S(2)}) async-start(f32[16,8,128]{2,1,0:T(8,128)} %shard_map.90), calls=%async_computation.1 | async-start | bytes 131072 | tf_op jit(solution)/shard_map/all_to_all | solution.py:180
  61.0 11.2 %collective-permute-start.5 = (bf16[256,256]{1,0:T(8,128)(2,1)S(1)}, bf16[256,256]{1,0:T(8,128)(2,1)S(1)}, u32[]{:S(2)}, u32[]{:S(2)}) collective-permute-start(bf16[256,256]{1,0:T(8,128)(2,1)S(1)} %get-tuple-element.32), channel_id=1, source_target_pairs={{16,0},{24,8},{32,16},{40,24},{48,32},{56,40},{64,48},{72,56},{80,... | collective-permute-start | bytes 393224 | tf_op jit(solution)/shard_map/ppermute | solution.py:176
  72.2 13.5 %collective-permute-start.6 = (bf16[256,256]{1,0:T(8,128)(2,1)S(1)}, bf16[256,256]{1,0:T(8,128)(2,1)S(1)}, u32[]{:S(2)}, u32[]{:S(2)}) collective-permute-start(bf16[256,256]{1,0:T(8,128)(2,1)S(1)} %shard_map.87), channel_id=1, source_target_pairs={{16,0},{24,8},{32,16},{40,24},{48,32},{56,40},{64,48},{72,56},{80,... | collective-permute-start | bytes 393224 | tf_op jit(solution)/shard_map/ppermute | solution.py:176
  74.2 19.1 %all-to-all-start.2 = ((f32[32,8,128]{2,1,0:T(8,128)}), f32[32,8,128]{2,1,0:T(8,128)S(1)}, u32[]{:S(2)}, u32[]{:S(2)}) async-start(f32[32,8,128]{2,1,0:T(8,128)} %shard_map.91), calls=%async_computation.2 | async-start | bytes 262144 | tf_op jit(solution)/shard_map/all_to_all | solution.py:180
  85.8 6.0 %collective-permute-start.7 = (bf16[128,384]{1,0:T(8,128)(2,1)S(1)}, bf16[128,384]{1,0:T(8,128)(2,1)S(1)}, u32[]{:S(2)}, u32[]{:S(2)}) collective-permute-start(bf16[128,384]{1,0:T(8,128)(2,1)S(1)} %get-tuple-element.37), channel_id=1, source_target_pairs={{0,8},{8,0},{16,24},{24,16},{32,40},{40,32},{48,56},{56,48},{64,72... | collective-permute-start | bytes 294920 | tf_op jit(solution)/shard_map/ppermute | solution.py:176

commit v10 on v9

--- a/solution.py
+++ b/solution.py
@@ -59,7 +59,7 @@
     return jnp.where(take, high, low), jnp.where(take, low, high)
 
 
-def pack_body(odd, k, v, q, do, emb_t, kv_mine, kv_other, q_mine, other, erev):
+def pack_body(odd, k, v, q, do, kv_mine, kv_other, q_mine, other):
     for i, x in enumerate((k, v, q, do)):
         a, b = pick(odd[0] > 0, x)
         other[:, i * PAIR : (i + 1) * PAIR] = b
@@ -67,14 +67,9 @@
         (kv_mine if i < 2 else q_mine)[:, lanes] = a
         if i < 2:
             kv_other[:, lanes] = b
-    flip = flip_matrix(TOK)
-    for b in range(REACH):
-        back = mm(emb_t[:, span(REACH - 1 - b)], flip, NN).astype(BF16)
-        erev[:HEAD_DIM, span(b)] = back
-        erev[HEAD_DIM:, span(b)] = back
-
-
-def early_body(odd, kv_mine, q_mine, got, near_a, near_b, kv, qs, dos, qf):
+
+
+def early_body(odd, kv_mine, q_mine, got, near_a, near_b, emb_t, erev, kv, qs, dos, qf):
     here, there = half(odd[0]), half(1 - odd[0])
     kv[0, here] = near_a[...]
     kv[0, there] = near_b[...]
@@ -87,6 +82,11 @@
             x = part[:, (first + i) * PAIR : (first + i + 1) * PAIR]
             out[0, rows] = jnp.where(low, x, zero)
             out[1, rows] = jnp.where(low, zero, x)
+    flip = flip_matrix(TOK)
+    for b in range(REACH):
+        back = mm(emb_t[:, span(REACH - 1 - b)], flip, NN).astype(BF16)
+        erev[:HEAD_DIM, span(b)] = back
+        erev[HEAD_DIM:, span(b)] = back
     flip = flip_matrix(ROWS)
     for h in range(HEADS):
         qf[h] = mm(flip, qs[h], NN).astype(BF16)
@@ -141,11 +141,12 @@
         lo = (block - hi.astype(F32)).astype(BF16)
         block = mm(hi, flip, NN) + mm(lo, flip, NN)
         for d in range(HEAD_DIM // 8):
-            gemb[d * REACH + b] = block[d * 8 : (d + 1) * 8]
+            gemb[d * REACH + b] = block[d * 8 : (d + 1) * 8].astype(BF16)
 
 
 def sum_body(x, out):
-    out[...] = jnp.broadcast_to(jnp.sum(x[...], axis=0, keepdims=True), out.shape)
+    total = jnp.sum(x[...].astype(F32), axis=0, keepdims=True)
+    out[...] = jnp.broadcast_to(total, out.shape).astype(BF16)
 
 
 def add_body(got, d1, out):
@@ -193,11 +194,11 @@
         return [near(x) for x in outs] if name != "unpack" else outs
 
     half_unit, unit = ((TOK, 2 * PAIR), BF16, True), (ROWS, 2 * PAIR)
-    kv_mine, kv_other, q_mine, other, erev = run(
+    kv_mine, kv_other, q_mine, other = run(
         "pack",
         pack_body,
-        [half_unit] * 3 + [((TOK, 4 * PAIR), BF16, True), ((PAIR, BAND), BF16, True)],
-        [odd], key_rows, value_matrix_rows, query, grad_out, rel_embed.T,
+        [half_unit] * 3 + [((TOK, 4 * PAIR), BF16, True)],
+        [odd], key_rows, value_matrix_rows, query, grad_out,
     )
     got = shift(other, 0, True)
     near_a = shift(kv_mine, 2)
@@ -205,26 +206,26 @@
     far_a = shift(near_a, 2)
     far_b = shift(near_b, 2)
     heads = ((HEADS, ROWS, PAIR), BF16, True)
-    kv, qs, dos, qf = run(
+    erev, kv, qs, dos, qf = run(
         "early",
         early_body,
-        [((2, ROWS, 2 * PAIR), BF16, True), heads, heads, heads],
-        [odd], kv_mine, q_mine, got, near_a, near_b,
+        [((PAIR, BAND), BF16, True), ((2, ROWS, 2 * PAIR), BF16, True), heads, heads, heads],
+        [odd], kv_mine, q_mine, got, near_a, near_b, rel_embed.T,
     )
     far, d1, d0, gq, gemb = run(
         "main",
         main_body,
         [(unit, BF16, True), (unit, F32, True), (unit, F32, True), ((ROWS, PAIR), BF16, True)]
-        + [((lax.axis_size(plane), 8, 128), F32, True)],
+        + [((lax.axis_size(plane), 8, 128), BF16, True)],
         [odd, first], qs, dos, qf, erev, kv, far_a, far_b,
         scratch_shapes=[pltpu.VMEM(unit, BF16)],
     )
     whole = exchange(gemb, plane)
     for axes in (line, plane):
-        tiles = ((lax.axis_size(axes), 8, 128), F32, True)
+        tiles = ((lax.axis_size(axes), 8, 128), BF16, True)
         (whole,) = call(sum_body, [tiles], near(whole))
         whole = exchange(whole, axes)
-    grad_embed_t = whole.reshape(8, REACH, 8, 128).transpose(0, 2, 1, 3).reshape(HEAD_DIM, BAND)
+    grad_embed_t = whole.astype(F32).reshape(8, REACH, 8, 128).transpose(0, 2, 1, 3).reshape(HEAD_DIM, BAND)
     back = shift(far, -2)
     (back,) = run("add", add_body, [(unit, BF16, True)], [], back, d1)
     back = shift(back, -2)

time: 94.5 us -> 89.7 us (0.949)
  starting transfers between devices: 51.4 us -> 44.2 us
  blocking collectives: 18.9 us -> 21.4 us
    ppermute x8, waiting for transfers between devices: 15 us -> 0.15 us  [shift(): return near(lax.ppermute(x, SEQ, [(s, t) for s, t in pairs if 0 <= t < n]))]
    all_to_all x2, waiting for transfers between devices: 0.82 us -> 15 us  [exchange(): return lax.all_to_all(x, axes, 0, 0, tiled=True)]
    all_to_all x2, starting transfers between devices: 20.9 us -> 13.2 us  [exchange(): return lax.all_to_all(x, axes, 0, 0, tiled=True)]
    all_to_all x1, blocking collectives: 18.9 us -> 21.4 us  [exchange(): return lax.all_to_all(x, axes, 0, 0, tiled=True)]
  transfers between devices with their start and end apart: 10 -> 10, of which waited for: 4 -> 3; matrix products, arithmetic and copies ran while one was open for 0% -> 1% of each run, Pallas kernels for 2% -> 3%
where the time goes in v10:
time: 89.7 us; the launch traced here: 89.2 us
  starting transfers between devices  44.2 us (49%)
  blocking collectives  21.4 us (24%)
  waiting for transfers between devices  15.2 us (17%)
  Pallas kernels  7.01 us (8%)
    ppermute x8, starting transfers between devices, shift(): return near(lax.ppermute(x, SEQ, [(s, t) for s, t in pairs if 0 <= t < n]))  31 us
    all_to_all x1, blocking collectives, exchange(): return lax.all_to_all(x, axes, 0, 0, tiled=True)  21.4 us
    all_to_all x2, waiting for transfers between devices, exchange(): return lax.all_to_all(x, axes, 0, 0, tiled=True)  15 us
    all_to_all x2, starting transfers between devices, exchange(): return lax.all_to_all(x, axes, 0, 0, tiled=True)  13.2 us
    pallas_call x8, Pallas kernels, call(): return list(pl.pallas_call(body, out_shape=shapes, **kw)(*args))  7.01 us
  transfers between devices with their start and end apart: 10, of which 3 were waited for; matrix products, arithmetic and copies ran while one was open for 1% of the time, Pallas kernels for 3%

profile of v10, /device:TPU:1, one launch (start us, length us, event | category | flops | bytes accessed | tf_op | source)
XLA Modules:
  0.0 89.2 jit_solution(397786159008533884)
XLA Ops:
  0.6 1.0 %shard_map.84 = (bf16[128,256]{1,0:T(8,128)(2,1)S(1)}, bf16[128,256]{1,0:T(8,128)(2,1)S(1)}, bf16[128,256]{1,0:T(8,128)(2,1)S(1)}, bf16[128,512]{1,0:T(8,128)(2,1)S(1)}) custom-call(s32[1]{0:T(128)} %bitcast.odd, bf16[128,256]{1,0:T(8,128)(2,1)} %k.1, bf16[128,256]{1,0:T(8,128)(2,1)} %v.1, bf16[128,256]{1,0:T(8,128)(2,1)} %q.1, bf16[128,256]{1,0:T(8,128)(2,1)} %do.1), custom_call_target="tpu_custom_call" | custom-call | tf_op jit(solution)/shard_map/pallas_call | solution.py:28
  1.6 4.4 %collective-permute-start = (bf16[128,512]{1,0:T(8,128)(2,1)S(1)}, bf16[128,512]{1,0:T(8,128)(2,1)S(1)}, u32[]{:S(2)}, u32[]{:S(2)}) collective-permute-start(bf16[128,512]{1,0:T(8,128)(2,1)S(1)} %get-tuple-element.25), channel_id=1, source_target_pairs={{0,8},{8,0},{16,24},{24,16},{32,40},{40,32},{48,56},{56,48},{64,72... | collective-permute-start | bytes 393224 | tf_op jit(solution)/shard_map/ppermute | solution.py:177
  6.0 4.6 %collective-permute-start.2 = (bf16[128,256]{1,0:T(8,128)(2,1)S(1)}, bf16[128,256]{1,0:T(8,128)(2,1)S(1)}, u32[]{:S(2)}, u32[]{:S(2)}) collective-permute-start(bf16[128,256]{1,0:T(8,128)(2,1)S(1)} %get-tuple-element.26), channel_id=1, source_target_pairs={{0,24},{8,16},{16,40},{24,32},{32,56},{40,48},{48,72},{56,64},{64,... | collective-permute-start | bytes 196616 | tf_op jit(solution)/shard_map/ppermute | solution.py:177
  10.6 6.1 %collective-permute-start.1 = (bf16[128,256]{1,0:T(8,128)(2,1)S(1)}, bf16[128,256]{1,0:T(8,128)(2,1)S(1)}, u32[]{:S(2)}, u32[]{:S(2)}) collective-permute-start(bf16[128,256]{1,0:T(8,128)(2,1)S(1)} %get-tuple-element.23.kv_mine), channel_id=1, source_target_pairs={{0,16},{8,24},{16,32},{24,40},{32,48},{40,56},{48,64},{56,72},{64,... | collective-permute-start | bytes 196616 | tf_op jit(solution)/shard_map/ppermute | solution.py:177
  16.8 0.0 collective-permute-done.2.near_b
  16.8 4.9 %collective-permute-start.4 = (bf16[128,256]{1,0:T(8,128)(2,1)S(1)}, bf16[128,256]{1,0:T(8,128)(2,1)S(1)}, u32[]{:S(2)}, u32[]{:S(2)}) collective-permute-start(bf16[128,256]{1,0:T(8,128)(2,1)S(1)} %collective-permute-done.2.near_b), channel_id=1, source_target_pairs={{0,16},{8,24},{16,32},{24,40},{32,48},{40,56},{48,64},{56,72},{64,... | collective-permute-start | bytes 196616 | tf_op jit(solution)/shard_map/ppermute | solution.py:177
  21.7 0.0 collective-permute-done.1.near_a
  21.7 5.9 %collective-permute-start.3 = (bf16[128,256]{1,0:T(8,128)(2,1)S(1)}, bf16[128,256]{1,0:T(8,128)(2,1)S(1)}, u32[]{:S(2)}, u32[]{:S(2)}) collective-permute-start(bf16[128,256]{1,0:T(8,128)(2,1)S(1)} %collective-permute-done.1.near_a), channel_id=1, source_target_pairs={{0,16},{8,24},{16,32},{24,40},{32,48},{40,56},{48,64},{56,72},{64,... | collective-permute-start | bytes 196616 | tf_op jit(solution)/shard_map/ppermute | solution.py:177
  27.6 0.0 collective-permute-done.got
  27.6 1.1 %shard_map.85 = (bf16[128,512]{1,0:T(8,128)(2,1)S(1)}, bf16[2,256,256]{2,1,0:T(8,128)(2,1)S(1)}, bf16[2,256,128]{2,1,0:T(8,128)(2,1)S(1)}, bf16[2,256,128]{2,1,0:T(8,128)(2,1)S(1)}, bf16[2,256,128]{2,1,0:T(8,128)(2,1)S(1)}) custom-call(s32[1]{0:T(128)} %bitcast.odd, bf16[128,256]{1,0:T(8,128)(2,1)S(1)} %get-tuple-element.23.kv_mine, ...), custom_call_target="tpu_custom_call" | custom-call | tf_op jit(solution)/shard_map/pallas_call | solution.py:28
  28.8 0.0 collective-permute-done.4.far_b
  28.8 0.1 collective-permute-done.3.far_a
  28.9 2.8 %shard_map.86 = (bf16[256,256]{1,0:T(8,128)(2,1)S(1)}, f32[256,256]{1,0:T(8,128)S(1)}, f32[256,256]{1,0:T(8,128)S(1)}, bf16[256,128]{1,0:T(8,128)(2,1)S(1)}, bf16[32,8,128]{2,1,0:T(8,128)(2,1)S(1)}) custom-call(s32[1]{0:T(128)} %bitcast.odd, s32[1]{0:T(128)} %bitcast.1.first, bf16[2,256,128]{2,1,0:T(8,128)(2,1)S(1)} %get-tuple-element.27.qs, ...), custom_call_target="tpu_custom_call" | custom-call | tf_op jit(solution)/shard_map/pallas_call | solution.py:28
  31.7 1.3 %collective-permute-start.5 = (bf16[256,256]{1,0:T(8,128)(2,1)S(1)}, bf16[256,256]{1,0:T(8,128)(2,1)S(1)}, u32[]{:S(2)}, u32[]{:S(2)}) collective-permute-start(bf16[256,256]{1,0:T(8,128)(2,1)S(1)} %get-tuple-element.32), channel_id=1, source_target_pairs={{16,0},{24,8},{32,16},{40,24},{48,32},{56,40},{64,48},{72,56},{80,... | collective-permute-start | bytes 393224 | tf_op jit(solution)/shard_map/ppermute | solution.py:177
  33.0 21.4 %all_to_all.15.x = bf16[32,8,128]{2,1,0:T(8,128)(2,1)S(1)} all-to-all(bf16[32,8,128]{2,1,0:T(8,128)(2,1)S(1)} %get-tuple-element.41), channel_id=1, replica_groups=mesh['y'=4,'zg'=4,'zi'=4,'x'=4,'core'=2] {'y','x','core'}, dimensions={0} | all-to-all | bytes 131072 | tf_op jit(solution)/shard_map/all_to_all | solution.py:181
  54.4 0.7 shard_map.90
  55.1 7.9 %all-to-all-start.1 = ((bf16[16,8,128]{2,1,0:T(8,128)(2,1)}), bf16[16,8,128]{2,1,0:T(8,128)(2,1)S(1)}, u32[]{:S(2)}, u32[]{:S(2)}) async-start(bf16[16,8,128]{2,1,0:T(8,128)(2,1)} %shard_map.90), calls=%async_computation.1 | async-start | bytes 65536 | tf_op jit(solution)/shard_map/all_to_all | solution.py:181
  63.0 0.0 collective-permute-done.5.got
  63.0 1.3 %collective-permute-start.6 = (bf16[256,256]{1,0:T(8,128)(2,1)S(1)}, bf16[256,256]{1,0:T(8,128)(2,1)S(1)}, u32[]{:S(2)}, u32[]{:S(2)}) collective-permute-start(bf16[256,256]{1,0:T(8,128)(2,1)S(1)} %shard_map.87), channel_id=1, source_target_pairs={{16,0},{24,8},{32,16},{40,24},{48,32},{56,40},{64,48},{72,56},{80,... | collective-permute-start | bytes 393224 | tf_op jit(solution)/shard_map/ppermute | solution.py:177
  64.3 10.1 %all-to-all-done.1.x = bf16[16,8,128]{2,1,0:T(8,128)(2,1)S(1)} async-done(((bf16[16,8,128]{2,1,0:T(8,128)(2,1)}), bf16[16,8,128]{2,1,0:T(8,128)(2,1)S(1)}, u32[]{:S(2)}, u32[]{:S(2)}) %all-to-all-start.1) | async-done | bytes 32800 | tf_op jit(solution)/shard_map/all_to_all | solution.py:181
  74.5 0.7 shard_map.91
  75.1 5.3 %all-to-all-start.2 = ((bf16[32,8,128]{2,1,0:T(8,128)(2,1)}), bf16[32,8,128]{2,1,0:T(8,128)(2,1)S(1)}, u32[]{:S(2)}, u32[]{:S(2)}) async-start(bf16[32,8,128]{2,1,0:T(8,128)(2,1)} %shard_map.91), calls=%async_computation.2 | async-start | bytes 131072 | tf_op jit(solution)/shard_map/all_to_all | solution.py:181
  80.4 0.0 collective-permute-done.6.got
  80.4 2.5 %collective-permute-start.7 = (bf16[128,384]{1,0:T(8,128)(2,1)S(1)}, bf16[128,384]{1,0:T(8,128)(2,1)S(1)}, u32[]{:S(2)}, u32[]{:S(2)}) collective-permute-start(bf16[128,384]{1,0:T(8,128)(2,1)S(1)} %get-tuple-element.37), channel_id=1, source_target_pairs={{0,8},{8,0},{16,24},{24,16},{32,40},{40,32},{48,56},{56,48},{64,72... | collective-permute-start | bytes 294920 | tf_op jit(solution)/shard_map/ppermute | solution.py:177
  82.9 4.9 %all-to-all-done.2 = bf16[32,8,128]{2,1,0:T(8,128)(2,1)S(1)} async-done(((bf16[32,8,128]{2,1,0:T(8,128)(2,1)}), bf16[32,8,128]{2,1,0:T(8,128)(2,1)S(1)}, u32[]{:S(2)}, u32[]{:S(2)}) %all-to-all-start.2) | async-done | bytes 65568 | tf_op jit(solution)/shard_map/all_to_all | solution.py:181
  87.8 0.7 convert_bitcast_fusion
  88.5 0.0 collective-permute-done.7.got
  88.5 0.7 shard_map.89
  (2 shorter events, 0.1 us)
Async XLA Ops:
  1.6 26.0 %collective-permute-start = (bf16[128,512]{1,0:T(8,128)(2,1)S(1)}, bf16[128,512]{1,0:T(8,128)(2,1)S(1)}, u32[]{:S(2)}, u32[]{:S(2)}) collective-permute-start(bf16[128,512]{1,0:T(8,128)(2,1)S(1)} %get-tuple-element.25), channel_id=1, source_target_pairs={{0,8},{8,0},{16,24},{24,16},{32,40},{40,32},{48,56},{56,48},{64,72... | collective-permute-start | bytes 393224 | tf_op jit(solution)/shard_map/ppermute | solution.py:177
  6.0 10.8 %collective-permute-start.2 = (bf16[128,256]{1,0:T(8,128)(2,1)S(1)}, bf16[128,256]{1,0:T(8,128)(2,1)S(1)}, u32[]{:S(2)}, u32[]{:S(2)}) collective-permute-start(bf16[128,256]{1,0:T(8,128)(2,1)S(1)} %get-tuple-element.26), channel_id=1, source_target_pairs={{0,24},{8,16},{16,40},{24,32},{32,56},{40,48},{48,72},{56,64},{64,... | collective-permute-start | bytes 196616 | tf_op jit(solution)/shard_map/ppermute | solution.py:177
  10.6 11.0 %collective-permute-start.1 = (bf16[128,256]{1,0:T(8,128)(2,1)S(1)}, bf16[128,256]{1,0:T(8,128)(2,1)S(1)}, u32[]{:S(2)}, u32[]{:S(2)}) collective-permute-start(bf16[128,256]{1,0:T(8,128)(2,1)S(1)} %get-tuple-element.23.kv_mine), channel_id=1, source_target_pairs={{0,16},{8,24},{16,32},{24,40},{32,48},{40,56},{48,64},{56,72},{64,... | collective-permute-start | bytes 196616 | tf_op jit(solution)/shard_map/ppermute | solution.py:177
  16.8 12.0 %collective-permute-start.4 = (bf16[128,256]{1,0:T(8,128)(2,1)S(1)}, bf16[128,256]{1,0:T(8,128)(2,1)S(1)}, u32[]{:S(2)}, u32[]{:S(2)}) collective-permute-start(bf16[128,256]{1,0:T(8,128)(2,1)S(1)} %collective-permute-done.2.near_b), channel_id=1, source_target_pairs={{0,16},{8,24},{16,32},{24,40},{32,48},{40,56},{48,64},{56,72},{64,... | collective-permute-start | bytes 196616 | tf_op jit(solution)/shard_map/ppermute | solution.py:177
  21.7 7.2 %collective-permute-start.3 = (bf16[128,256]{1,0:T(8,128)(2,1)S(1)}, bf16[128,256]{1,0:T(8,128)(2,1)S(1)}, u32[]{:S(2)}, u32[]{:S(2)}) collective-permute-start(bf16[128,256]{1,0:T(8,128)(2,1)S(1)} %collective-permute-done.1.near_a), channel_id=1, source_target_pairs={{0,16},{8,24},{16,32},{24,40},{32,48},{40,56},{48,64},{56,72},{64,... | collective-permute-start | bytes 196616 | tf_op jit(solution)/shard_map/ppermute | solution.py:177
  31.7 31.2 %collective-permute-start.5 = (bf16[256,256]{1,0:T(8,128)(2,1)S(1)}, bf16[256,256]{1,0:T(8,128)(2,1)S(1)}, u32[]{:S(2)}, u32[]{:S(2)}) collective-permute-start(bf16[256,256]{1,0:T(8,128)(2,1)S(1)} %get-tuple-element.32), channel_id=1, source_target_pairs={{16,0},{24,8},{32,16},{40,24},{48,32},{56,40},{64,48},{72,56},{80,... | collective-permute-start | bytes 393224 | tf_op jit(solution)/shard_map/ppermute | solution.py:177
  55.1 19.4 %all-to-all-start.1 = ((bf16[16,8,128]{2,1,0:T(8,128)(2,1)}), bf16[16,8,128]{2,1,0:T(8,128)(2,1)S(1)}, u32[]{:S(2)}, u32[]{:S(2)}) async-start(bf16[16,8,128]{2,1,0:T(8,128)(2,1)} %shard_map.90), calls=%async_computation.1 | async-start | bytes 65536 | tf_op jit(solution)/shard_map/all_to_all | solution.py:181
  63.0 17.4 %collective-permute-start.6 = (bf16[256,256]{1,0:T(8,128)(2,1)S(1)}, bf16[256,256]{1,0:T(8,128)(2,1)S(1)}, u32[]{:S(2)}, u32[]{:S(2)}) collective-permute-start(bf16[256,256]{1,0:T(8,128)(2,1)S(1)} %shard_map.87), channel_id=1, source_target_pairs={{16,0},{24,8},{32,16},{40,24},{48,32},{56,40},{64,48},{72,56},{80,... | collective-permute-start | bytes 393224 | tf_op jit(solution)/shard_map/ppermute | solution.py:177
  75.1 12.7 %all-to-all-start.2 = ((bf16[32,8,128]{2,1,0:T(8,128)(2,1)}), bf16[32,8,128]{2,1,0:T(8,128)(2,1)S(1)}, u32[]{:S(2)}, u32[]{:S(2)}) async-start(bf16[32,8,128]{2,1,0:T(8,128)(2,1)} %shard_map.91), calls=%async_computation.2 | async-start | bytes 131072 | tf_op jit(solution)/shard_map/all_to_all | solution.py:181
  80.4 8.0 %collective-permute-start.7 = (bf16[128,384]{1,0:T(8,128)(2,1)S(1)}, bf16[128,384]{1,0:T(8,128)(2,1)S(1)}, u32[]{:S(2)}, u32[]{:S(2)}) collective-permute-start(bf16[128,384]{1,0:T(8,128)(2,1)S(1)} %get-tuple-element.37), channel_id=1, source_target_pairs={{0,8},{8,0},{16,24},{24,16},{32,40},{40,32},{48,56},{56,48},{64,72... | collective-permute-start | bytes 294920 | tf_op jit(solution)/shard_map/ppermute | solution.py:177

commit v11 on v10

--- a/solution.py
+++ b/solution.py
@@ -136,10 +136,7 @@
     total = total[:HEAD_DIM] + total[HEAD_DIM:]
     flip = flip_matrix(TOK)
     for b in range(REACH):
-        block = total[:, span(REACH - 1 - b)]
-        hi = block.astype(BF16)
-        lo = (block - hi.astype(F32)).astype(BF16)
-        block = mm(hi, flip, NN) + mm(lo, flip, NN)
+        block = mm(total[:, span(REACH - 1 - b)].astype(BF16), flip, NN)
         for d in range(HEAD_DIM // 8):
             gemb[d * REACH + b] = block[d * 8 : (d + 1) * 8].astype(BF16)
 
@@ -147,6 +144,12 @@
 def sum_body(x, out):
     total = jnp.sum(x[...].astype(F32), axis=0, keepdims=True)
     out[...] = jnp.broadcast_to(total, out.shape).astype(BF16)
+
+
+def place_body(x, out):
+    for d in range(HEAD_DIM // 8):
+        for b in range(REACH):
+            out[d * 8 : (d + 1) * 8, span(b)] = x[d * REACH + b].astype(F32)
 
 
 def add_body(got, d1, out):
@@ -225,7 +228,7 @@
         tiles = ((lax.axis_size(axes), 8, 128), BF16, True)
         (whole,) = call(sum_body, [tiles], near(whole))
         whole = exchange(whole, axes)
-    grad_embed_t = whole.astype(F32).reshape(8, REACH, 8, 128).transpose(0, 2, 1, 3).reshape(HEAD_DIM, BAND)
+    (grad_embed_t,) = call(place_body, [((HEAD_DIM, BAND), F32, False)], near(whole), in_specs=[vm])
     back = shift(far, -2)
     (back,) = run("add", add_body, [(unit, BF16, True)], [], back, d1)
     back = shift(back, -2)

time: 89.7 us -> 89.5 us (level)
  starting transfers between devices: 44.2 us -> 54 us
  blocking collectives: 21.4 us -> 12.3 us
  waiting for transfers between devices: 15.2 us -> 14.3 us
    all_to_all x1, blocking collectives: 21.4 us -> 12.3 us  [exchange(): return lax.all_to_all(x, axes, 0, 0, tiled=True)]
    all_to_all x2, starting transfers between devices: 13.2 us -> 22.2 us  [exchange(): return lax.all_to_all(x, axes, 0, 0, tiled=True)]
    all_to_all x2, waiting for transfers between devices: 15 us -> 14.1 us  [exchange(): return lax.all_to_all(x, axes, 0, 0, tiled=True)]
    pallas_call x8 -> x9, Pallas kernels: 7.01 us -> 7.64 us  [call(): return list(pl.pallas_call(body, out_shape=shapes, **kw)(*args))]
  transfers between devices with their start and end apart: 10 -> 10, of which waited for: 3 -> 3; matrix products, arithmetic and copies ran while one was open for 1% -> 0% of each run, Pallas kernels for 3% -> 3%
where the time goes in v11:
time: 89.5 us; the launch traced here: 89 us
  starting transfers between devices  54 us (60%)
  waiting for transfers between devices  14.3 us (16%)
  blocking collectives  12.3 us (14%)
  Pallas kernels  7.64 us (9%)
    ppermute x8, starting transfers between devices, shift(): return near(lax.ppermute(x, SEQ, [(s, t) for s, t in pairs if 0 <= t < n]))  31.8 us
    all_to_all x2, starting transfers between devices, exchange(): return lax.all_to_all(x, axes, 0, 0, tiled=True)  22.2 us
    all_to_all x2, waiting for transfers between devices, exchange(): return lax.all_to_all(x, axes, 0, 0, tiled=True)  14.1 us
    all_to_all x1, blocking collectives, exchange(): return lax.all_to_all(x, axes, 0, 0, tiled=True)  12.3 us
    pallas_call x9, Pallas kernels, call(): return list(pl.pallas_call(body, out_shape=shapes, **kw)(*args))  7.64 us
  transfers between devices with their start and end apart: 10, of which 3 were waited for; matrix products, arithmetic and copies ran while one was open for 0% of the time, Pallas kernels for 3%

profile of v11, /device:TPU:1, one launch (start us, length us, event | category | flops | bytes accessed | tf_op | source)
XLA Modules:
  0.0 89.0 jit_solution(1179933874546957008)
XLA Ops:
  0.6 1.0 %shard_map.84 = (bf16[128,256]{1,0:T(8,128)(2,1)S(1)}, bf16[128,256]{1,0:T(8,128)(2,1)S(1)}, bf16[128,256]{1,0:T(8,128)(2,1)S(1)}, bf16[128,512]{1,0:T(8,128)(2,1)S(1)}) custom-call(s32[1]{0:T(128)} %bitcast.odd, bf16[128,256]{1,0:T(8,128)(2,1)} %k.1, bf16[128,256]{1,0:T(8,128)(2,1)} %v.1, bf16[128,256]{1,0:T(8,128)(2,1)} %q.1, bf16[128,256]{1,0:T(8,128)(2,1)} %do.1), custom_call_target="tpu_custom_call" | custom-call | tf_op jit(solution)/shard_map/pallas_call | solution.py:28
  1.6 4.4 %collective-permute-start = (bf16[128,512]{1,0:T(8,128)(2,1)S(1)}, bf16[128,512]{1,0:T(8,128)(2,1)S(1)}, u32[]{:S(2)}, u32[]{:S(2)}) collective-permute-start(bf16[128,512]{1,0:T(8,128)(2,1)S(1)} %get-tuple-element.25), channel_id=1, source_target_pairs={{0,8},{8,0},{16,24},{24,16},{32,40},{40,32},{48,56},{56,48},{64,72... | collective-permute-start | bytes 393224 | tf_op jit(solution)/shard_map/ppermute | solution.py:180
  6.0 4.6 %collective-permute-start.2 = (bf16[128,256]{1,0:T(8,128)(2,1)S(1)}, bf16[128,256]{1,0:T(8,128)(2,1)S(1)}, u32[]{:S(2)}, u32[]{:S(2)}) collective-permute-start(bf16[128,256]{1,0:T(8,128)(2,1)S(1)} %get-tuple-element.26), channel_id=1, source_target_pairs={{0,24},{8,16},{16,40},{24,32},{32,56},{40,48},{48,72},{56,64},{64,... | collective-permute-start | bytes 196616 | tf_op jit(solution)/shard_map/ppermute | solution.py:180
  10.6 6.1 %collective-permute-start.1 = (bf16[128,256]{1,0:T(8,128)(2,1)S(1)}, bf16[128,256]{1,0:T(8,128)(2,1)S(1)}, u32[]{:S(2)}, u32[]{:S(2)}) collective-permute-start(bf16[128,256]{1,0:T(8,128)(2,1)S(1)} %get-tuple-element.23.kv_mine), channel_id=1, source_target_pairs={{0,16},{8,24},{16,32},{24,40},{32,48},{40,56},{48,64},{56,72},{64,... | collective-permute-start | bytes 196616 | tf_op jit(solution)/shard_map/ppermute | solution.py:180
  16.8 0.0 collective-permute-done.2.near_b
  16.8 4.9 %collective-permute-start.4 = (bf16[128,256]{1,0:T(8,128)(2,1)S(1)}, bf16[128,256]{1,0:T(8,128)(2,1)S(1)}, u32[]{:S(2)}, u32[]{:S(2)}) collective-permute-start(bf16[128,256]{1,0:T(8,128)(2,1)S(1)} %collective-permute-done.2.near_b), channel_id=1, source_target_pairs={{0,16},{8,24},{16,32},{24,40},{32,48},{40,56},{48,64},{56,72},{64,... | collective-permute-start | bytes 196616 | tf_op jit(solution)/shard_map/ppermute | solution.py:180
  21.7 0.0 collective-permute-done.1.near_a
  21.7 5.9 %collective-permute-start.3 = (bf16[128,256]{1,0:T(8,128)(2,1)S(1)}, bf16[128,256]{1,0:T(8,128)(2,1)S(1)}, u32[]{:S(2)}, u32[]{:S(2)}) collective-permute-start(bf16[128,256]{1,0:T(8,128)(2,1)S(1)} %collective-permute-done.1.near_a), channel_id=1, source_target_pairs={{0,16},{8,24},{16,32},{24,40},{32,48},{40,56},{48,64},{56,72},{64,... | collective-permute-start | bytes 196616 | tf_op jit(solution)/shard_map/ppermute | solution.py:180
  27.6 0.0 collective-permute-done.got
  27.6 1.1 %shard_map.85 = (bf16[128,512]{1,0:T(8,128)(2,1)S(1)}, bf16[2,256,256]{2,1,0:T(8,128)(2,1)S(1)}, bf16[2,256,128]{2,1,0:T(8,128)(2,1)S(1)}, bf16[2,256,128]{2,1,0:T(8,128)(2,1)S(1)}, bf16[2,256,128]{2,1,0:T(8,128)(2,1)S(1)}) custom-call(s32[1]{0:T(128)} %bitcast.odd, bf16[128,256]{1,0:T(8,128)(2,1)S(1)} %get-tuple-element.23.kv_mine, ...), custom_call_target="tpu_custom_call" | custom-call | tf_op jit(solution)/shard_map/pallas_call | solution.py:28
  28.8 0.0 collective-permute-done.4.far_b
  28.8 0.1 collective-permute-done.3.far_a
  28.9 3.4 %shard_map.86 = (bf16[256,256]{1,0:T(8,128)(2,1)S(1)}, f32[256,256]{1,0:T(8,128)S(1)}, f32[256,256]{1,0:T(8,128)S(1)}, bf16[256,128]{1,0:T(8,128)(2,1)S(1)}, bf16[32,8,128]{2,1,0:T(8,128)(2,1)}) custom-call(s32[1]{0:T(128)} %bitcast.odd, s32[1]{0:T(128)} %bitcast.1.first, bf16[2,256,128]{2,1,0:T(8,128)(2,1)S(1)} %get-tuple-element.27.qs, ...), custom_call_target="tpu_custom_call" | custom-call | tf_op jit(solution)/shard_map/pallas_call | solution.py:28
  32.3 1.3 %collective-permute-start.5 = (bf16[256,256]{1,0:T(8,128)(2,1)S(1)}, bf16[256,256]{1,0:T(8,128)(2,1)S(1)}, u32[]{:S(2)}, u32[]{:S(2)}) collective-permute-start(bf16[256,256]{1,0:T(8,128)(2,1)S(1)} %get-tuple-element.32), channel_id=1, source_target_pairs={{16,0},{24,8},{32,16},{40,24},{48,32},{56,40},{64,48},{72,56},{80,... | collective-permute-start | bytes 393224 | tf_op jit(solution)/shard_map/ppermute | solution.py:180
  33.6 14.3 %all-to-all-start = ((bf16[32,8,128]{2,1,0:T(8,128)(2,1)}), bf16[32,8,128]{2,1,0:T(8,128)(2,1)S(1)}, u32[]{:S(2)}, u32[]{:S(2)}) async-start(bf16[32,8,128]{2,1,0:T(8,128)(2,1)} %get-tuple-element.41), calls=%async_computation | async-start | bytes 131072 | tf_op jit(solution)/shard_map/all_to_all | solution.py:184
  47.9 0.0 collective-permute-done.5.got
  47.9 1.3 %collective-permute-start.6 = (bf16[256,256]{1,0:T(8,128)(2,1)S(1)}, bf16[256,256]{1,0:T(8,128)(2,1)S(1)}, u32[]{:S(2)}, u32[]{:S(2)}) collective-permute-start(bf16[256,256]{1,0:T(8,128)(2,1)S(1)} %shard_map.87), channel_id=1, source_target_pairs={{16,0},{24,8},{32,16},{40,24},{48,32},{56,40},{64,48},{72,56},{80,... | collective-permute-start | bytes 393224 | tf_op jit(solution)/shard_map/ppermute | solution.py:180
  49.2 6.0 %all-to-all-done.x = bf16[32,8,128]{2,1,0:T(8,128)(2,1)S(1)} async-done(((bf16[32,8,128]{2,1,0:T(8,128)(2,1)}), bf16[32,8,128]{2,1,0:T(8,128)(2,1)S(1)}, u32[]{:S(2)}, u32[]{:S(2)}) %all-to-all-start) | async-done | bytes 65568 | tf_op jit(solution)/shard_map/all_to_all | solution.py:184
  55.2 0.7 shard_map.90
  55.9 7.9 %all-to-all-start.1 = ((bf16[16,8,128]{2,1,0:T(8,128)(2,1)}), bf16[16,8,128]{2,1,0:T(8,128)(2,1)S(1)}, u32[]{:S(2)}, u32[]{:S(2)}) async-start(bf16[16,8,128]{2,1,0:T(8,128)(2,1)} %shard_map.90), calls=%async_computation.1 | async-start | bytes 65536 | tf_op jit(solution)/shard_map/all_to_all | solution.py:184
  63.8 0.0 collective-permute-done.6.got
  63.9 3.3 %collective-permute-start.7 = (bf16[128,384]{1,0:T(8,128)(2,1)S(1)}, bf16[128,384]{1,0:T(8,128)(2,1)S(1)}, u32[]{:S(2)}, u32[]{:S(2)}) collective-permute-start(bf16[128,384]{1,0:T(8,128)(2,1)S(1)} %get-tuple-element.37), channel_id=1, source_target_pairs={{0,8},{8,0},{16,24},{24,16},{32,40},{40,32},{48,56},{56,48},{64,72... | collective-permute-start | bytes 294920 | tf_op jit(solution)/shard_map/ppermute | solution.py:180
  67.1 8.1 %all-to-all-done.1.x = bf16[16,8,128]{2,1,0:T(8,128)(2,1)S(1)} async-done(((bf16[16,8,128]{2,1,0:T(8,128)(2,1)}), bf16[16,8,128]{2,1,0:T(8,128)(2,1)S(1)}, u32[]{:S(2)}, u32[]{:S(2)}) %all-to-all-start.1) | async-done | bytes 32800 | tf_op jit(solution)/shard_map/all_to_all | solution.py:184
  75.3 12.3 %all_to_all.15.x = bf16[32,8,128]{2,1,0:T(8,128)(2,1)S(1)} all-to-all(bf16[32,8,128]{2,1,0:T(8,128)(2,1)S(1)} %shard_map.91), channel_id=1, replica_groups=mesh['y'=4,'zg'=4,'zi'=4,'x'=4,'core'=2] {'y','x','core'}, dimensions={0} | all-to-all | bytes 131072 | tf_op jit(solution)/shard_map/all_to_all | solution.py:184
  87.6 0.7 shard_map.92
  88.2 0.0 collective-permute-done.7.got
  88.2 0.7 shard_map.89
  (3 shorter events, 0.1 us)
Async XLA Ops:
  1.6 26.0 %collective-permute-start = (bf16[128,512]{1,0:T(8,128)(2,1)S(1)}, bf16[128,512]{1,0:T(8,128)(2,1)S(1)}, u32[]{:S(2)}, u32[]{:S(2)}) collective-permute-start(bf16[128,512]{1,0:T(8,128)(2,1)S(1)} %get-tuple-element.25), channel_id=1, source_target_pairs={{0,8},{8,0},{16,24},{24,16},{32,40},{40,32},{48,56},{56,48},{64,72... | collective-permute-start | bytes 393224 | tf_op jit(solution)/shard_map/ppermute | solution.py:180
  6.0 10.8 %collective-permute-start.2 = (bf16[128,256]{1,0:T(8,128)(2,1)S(1)}, bf16[128,256]{1,0:T(8,128)(2,1)S(1)}, u32[]{:S(2)}, u32[]{:S(2)}) collective-permute-start(bf16[128,256]{1,0:T(8,128)(2,1)S(1)} %get-tuple-element.26), channel_id=1, source_target_pairs={{0,24},{8,16},{16,40},{24,32},{32,56},{40,48},{48,72},{56,64},{64,... | collective-permute-start | bytes 196616 | tf_op jit(solution)/shard_map/ppermute | solution.py:180
  10.6 11.0 %collective-permute-start.1 = (bf16[128,256]{1,0:T(8,128)(2,1)S(1)}, bf16[128,256]{1,0:T(8,128)(2,1)S(1)}, u32[]{:S(2)}, u32[]{:S(2)}) collective-permute-start(bf16[128,256]{1,0:T(8,128)(2,1)S(1)} %get-tuple-element.23.kv_mine), channel_id=1, source_target_pairs={{0,16},{8,24},{16,32},{24,40},{32,48},{40,56},{48,64},{56,72},{64,... | collective-permute-start | bytes 196616 | tf_op jit(solution)/shard_map/ppermute | solution.py:180
  16.8 12.0 %collective-permute-start.4 = (bf16[128,256]{1,0:T(8,128)(2,1)S(1)}, bf16[128,256]{1,0:T(8,128)(2,1)S(1)}, u32[]{:S(2)}, u32[]{:S(2)}) collective-permute-start(bf16[128,256]{1,0:T(8,128)(2,1)S(1)} %collective-permute-done.2.near_b), channel_id=1, source_target_pairs={{0,16},{8,24},{16,32},{24,40},{32,48},{40,56},{48,64},{56,72},{64,... | collective-permute-start | bytes 196616 | tf_op jit(solution)/shard_map/ppermute | solution.py:180
  21.7 7.2 %collective-permute-start.3 = (bf16[128,256]{1,0:T(8,128)(2,1)S(1)}, bf16[128,256]{1,0:T(8,128)(2,1)S(1)}, u32[]{:S(2)}, u32[]{:S(2)}) collective-permute-start(bf16[128,256]{1,0:T(8,128)(2,1)S(1)} %collective-permute-done.1.near_a), channel_id=1, source_target_pairs={{0,16},{8,24},{16,32},{24,40},{32,48},{40,56},{48,64},{56,72},{64,... | collective-permute-start | bytes 196616 | tf_op jit(solution)/shard_map/ppermute | solution.py:180
  32.3 15.6 %collective-permute-start.5 = (bf16[256,256]{1,0:T(8,128)(2,1)S(1)}, bf16[256,256]{1,0:T(8,128)(2,1)S(1)}, u32[]{:S(2)}, u32[]{:S(2)}) collective-permute-start(bf16[256,256]{1,0:T(8,128)(2,1)S(1)} %get-tuple-element.32), channel_id=1, source_target_pairs={{16,0},{24,8},{32,16},{40,24},{48,32},{56,40},{64,48},{72,56},{80,... | collective-permute-start | bytes 393224 | tf_op jit(solution)/shard_map/ppermute | solution.py:180
  33.6 21.6 %all-to-all-start = ((bf16[32,8,128]{2,1,0:T(8,128)(2,1)}), bf16[32,8,128]{2,1,0:T(8,128)(2,1)S(1)}, u32[]{:S(2)}, u32[]{:S(2)}) async-start(bf16[32,8,128]{2,1,0:T(8,128)(2,1)} %get-tuple-element.41), calls=%async_computation | async-start | bytes 131072 | tf_op jit(solution)/shard_map/all_to_all | solution.py:184
  47.9 15.9 %collective-permute-start.6 = (bf16[256,256]{1,0:T(8,128)(2,1)S(1)}, bf16[256,256]{1,0:T(8,128)(2,1)S(1)}, u32[]{:S(2)}, u32[]{:S(2)}) collective-permute-start(bf16[256,256]{1,0:T(8,128)(2,1)S(1)} %shard_map.87), channel_id=1, source_target_pairs={{16,0},{24,8},{32,16},{40,24},{48,32},{56,40},{64,48},{72,56},{80,... | collective-permute-start | bytes 393224 | tf_op jit(solution)/shard_map/ppermute | solution.py:180
  55.9 19.4 %all-to-all-start.1 = ((bf16[16,8,128]{2,1,0:T(8,128)(2,1)}), bf16[16,8,128]{2,1,0:T(8,128)(2,1)S(1)}, u32[]{:S(2)}, u32[]{:S(2)}) async-start(bf16[16,8,128]{2,1,0:T(8,128)(2,1)} %shard_map.90), calls=%async_computation.1 | async-start | bytes 65536 | tf_op jit(solution)/shard_map/all_to_all | solution.py:184
  63.9 24.4 %collective-permute-start.7 = (bf16[128,384]{1,0:T(8,128)(2,1)S(1)}, bf16[128,384]{1,0:T(8,128)(2,1)S(1)}, u32[]{:S(2)}, u32[]{:S(2)}) collective-permute-start(bf16[128,384]{1,0:T(8,128)(2,1)S(1)} %get-tuple-element.37), channel_id=1, source_target_pairs={{0,8},{8,0},{16,24},{24,16},{32,40},{40,32},{48,56},{56,48},{64,72... | collective-permute-start | bytes 294920 | tf_op jit(solution)/shard_map/ppermute | solution.py:180

commit v12 on v10

--- a/solution.py
+++ b/solution.py
@@ -136,10 +136,7 @@
     total = total[:HEAD_DIM] + total[HEAD_DIM:]
     flip = flip_matrix(TOK)
     for b in range(REACH):
-        block = total[:, span(REACH - 1 - b)]
-        hi = block.astype(BF16)
-        lo = (block - hi.astype(F32)).astype(BF16)
-        block = mm(hi, flip, NN) + mm(lo, flip, NN)
+        block = mm(total[:, span(REACH - 1 - b)].astype(BF16), flip, NN)
         for d in range(HEAD_DIM // 8):
             gemb[d * REACH + b] = block[d * 8 : (d + 1) * 8].astype(BF16)
 

time: 89.7 us -> 89.7 us (level)
  no operation moved by 1% of the time
where the time goes in v12:
time: 89.7 us; the launch traced here: 89.2 us
  starting transfers between devices  44.2 us (49%)
  blocking collectives  21.4 us (24%)
  waiting for transfers between devices  15.2 us (17%)
  Pallas kernels  6.98 us (8%)
    ppermute x8, starting transfers between devices, shift(): return near(lax.ppermute(x, SEQ, [(s, t) for s, t in pairs if 0 <= t < n]))  31 us
    all_to_all x1, blocking collectives, exchange(): return lax.all_to_all(x, axes, 0, 0, tiled=True)  21.4 us
    all_to_all x2, waiting for transfers between devices, exchange(): return lax.all_to_all(x, axes, 0, 0, tiled=True)  15 us
    all_to_all x2, starting transfers between devices, exchange(): return lax.all_to_all(x, axes, 0, 0, tiled=True)  13.2 us
    pallas_call x8, Pallas kernels, call(): return list(pl.pallas_call(body, out_shape=shapes, **kw)(*args))  6.98 us
  transfers between devices with their start and end apart: 10, of which 3 were waited for; matrix products, arithmetic and copies ran while one was open for 1% of the time, Pallas kernels for 3%

profile of v12, /device:TPU:1, one launch (start us, length us, event | category | flops | bytes accessed | tf_op | source)
XLA Modules:
  0.0 89.2 jit_solution(9358607136925545507)
XLA Ops:
  0.6 1.0 %shard_map.84 = (bf16[128,256]{1,0:T(8,128)(2,1)S(1)}, bf16[128,256]{1,0:T(8,128)(2,1)S(1)}, bf16[128,256]{1,0:T(8,128)(2,1)S(1)}, bf16[128,512]{1,0:T(8,128)(2,1)S(1)}) custom-call(s32[1]{0:T(128)} %bitcast.odd, bf16[128,256]{1,0:T(8,128)(2,1)} %k.1, bf16[128,256]{1,0:T(8,128)(2,1)} %v.1, bf16[128,256]{1,0:T(8,128)(2,1)} %q.1, bf16[128,256]{1,0:T(8,128)(2,1)} %do.1), custom_call_target="tpu_custom_call" | custom-call | tf_op jit(solution)/shard_map/pallas_call | solution.py:28
  1.6 4.4 %collective-permute-start = (bf16[128,512]{1,0:T(8,128)(2,1)S(1)}, bf16[128,512]{1,0:T(8,128)(2,1)S(1)}, u32[]{:S(2)}, u32[]{:S(2)}) collective-permute-start(bf16[128,512]{1,0:T(8,128)(2,1)S(1)} %get-tuple-element.25), channel_id=1, source_target_pairs={{0,8},{8,0},{16,24},{24,16},{32,40},{40,32},{48,56},{56,48},{64,72... | collective-permute-start | bytes 393224 | tf_op jit(solution)/shard_map/ppermute | solution.py:174
  6.0 4.6 %collective-permute-start.2 = (bf16[128,256]{1,0:T(8,128)(2,1)S(1)}, bf16[128,256]{1,0:T(8,128)(2,1)S(1)}, u32[]{:S(2)}, u32[]{:S(2)}) collective-permute-start(bf16[128,256]{1,0:T(8,128)(2,1)S(1)} %get-tuple-element.26), channel_id=1, source_target_pairs={{0,24},{8,16},{16,40},{24,32},{32,56},{40,48},{48,72},{56,64},{64,... | collective-permute-start | bytes 196616 | tf_op jit(solution)/shard_map/ppermute | solution.py:174
  10.6 6.1 %collective-permute-start.1 = (bf16[128,256]{1,0:T(8,128)(2,1)S(1)}, bf16[128,256]{1,0:T(8,128)(2,1)S(1)}, u32[]{:S(2)}, u32[]{:S(2)}) collective-permute-start(bf16[128,256]{1,0:T(8,128)(2,1)S(1)} %get-tuple-element.23.kv_mine), channel_id=1, source_target_pairs={{0,16},{8,24},{16,32},{24,40},{32,48},{40,56},{48,64},{56,72},{64,... | collective-permute-start | bytes 196616 | tf_op jit(solution)/shard_map/ppermute | solution.py:174
  16.8 0.0 collective-permute-done.2.near_b
  16.8 4.9 %collective-permute-start.4 = (bf16[128,256]{1,0:T(8,128)(2,1)S(1)}, bf16[128,256]{1,0:T(8,128)(2,1)S(1)}, u32[]{:S(2)}, u32[]{:S(2)}) collective-permute-start(bf16[128,256]{1,0:T(8,128)(2,1)S(1)} %collective-permute-done.2.near_b), channel_id=1, source_target_pairs={{0,16},{8,24},{16,32},{24,40},{32,48},{40,56},{48,64},{56,72},{64,... | collective-permute-start | bytes 196616 | tf_op jit(solution)/shard_map/ppermute | solution.py:174
  21.7 0.0 collective-permute-done.1.near_a
  21.7 5.9 %collective-permute-start.3 = (bf16[128,256]{1,0:T(8,128)(2,1)S(1)}, bf16[128,256]{1,0:T(8,128)(2,1)S(1)}, u32[]{:S(2)}, u32[]{:S(2)}) collective-permute-start(bf16[128,256]{1,0:T(8,128)(2,1)S(1)} %collective-permute-done.1.near_a), channel_id=1, source_target_pairs={{0,16},{8,24},{16,32},{24,40},{32,48},{40,56},{48,64},{56,72},{64,... | collective-permute-start | bytes 196616 | tf_op jit(solution)/shard_map/ppermute | solution.py:174
  27.6 0.0 collective-permute-done.got
  27.6 1.1 %shard_map.85 = (bf16[128,512]{1,0:T(8,128)(2,1)S(1)}, bf16[2,256,256]{2,1,0:T(8,128)(2,1)S(1)}, bf16[2,256,128]{2,1,0:T(8,128)(2,1)S(1)}, bf16[2,256,128]{2,1,0:T(8,128)(2,1)S(1)}, bf16[2,256,128]{2,1,0:T(8,128)(2,1)S(1)}) custom-call(s32[1]{0:T(128)} %bitcast.odd, bf16[128,256]{1,0:T(8,128)(2,1)S(1)} %get-tuple-element.23.kv_mine, ...), custom_call_target="tpu_custom_call" | custom-call | tf_op jit(solution)/shard_map/pallas_call | solution.py:28
  28.8 0.0 collective-permute-done.4.far_b
  28.8 0.1 collective-permute-done.3.far_a
  28.9 2.8 %shard_map.86 = (bf16[256,256]{1,0:T(8,128)(2,1)S(1)}, f32[256,256]{1,0:T(8,128)S(1)}, f32[256,256]{1,0:T(8,128)S(1)}, bf16[256,128]{1,0:T(8,128)(2,1)S(1)}, bf16[32,8,128]{2,1,0:T(8,128)(2,1)S(1)}) custom-call(s32[1]{0:T(128)} %bitcast.odd, s32[1]{0:T(128)} %bitcast.1.first, bf16[2,256,128]{2,1,0:T(8,128)(2,1)S(1)} %get-tuple-element.27.qs, ...), custom_call_target="tpu_custom_call" | custom-call | tf_op jit(solution)/shard_map/pallas_call | solution.py:28
  31.7 1.3 %collective-permute-start.5 = (bf16[256,256]{1,0:T(8,128)(2,1)S(1)}, bf16[256,256]{1,0:T(8,128)(2,1)S(1)}, u32[]{:S(2)}, u32[]{:S(2)}) collective-permute-start(bf16[256,256]{1,0:T(8,128)(2,1)S(1)} %get-tuple-element.32), channel_id=1, source_target_pairs={{16,0},{24,8},{32,16},{40,24},{48,32},{56,40},{64,48},{72,56},{80,... | collective-permute-start | bytes 393224 | tf_op jit(solution)/shard_map/ppermute | solution.py:174
  33.0 21.4 %all_to_all.15.x = bf16[32,8,128]{2,1,0:T(8,128)(2,1)S(1)} all-to-all(bf16[32,8,128]{2,1,0:T(8,128)(2,1)S(1)} %get-tuple-element.41), channel_id=1, replica_groups=mesh['y'=4,'zg'=4,'zi'=4,'x'=4,'core'=2] {'y','x','core'}, dimensions={0} | all-to-all | bytes 131072 | tf_op jit(solution)/shard_map/all_to_all | solution.py:178
  54.4 0.7 shard_map.90
  55.0 7.9 %all-to-all-start.1 = ((bf16[16,8,128]{2,1,0:T(8,128)(2,1)}), bf16[16,8,128]{2,1,0:T(8,128)(2,1)S(1)}, u32[]{:S(2)}, u32[]{:S(2)}) async-start(bf16[16,8,128]{2,1,0:T(8,128)(2,1)} %shard_map.90), calls=%async_computation.1 | async-start | bytes 65536 | tf_op jit(solution)/shard_map/all_to_all | solution.py:178
  63.0 0.0 collective-permute-done.5.got
  63.0 1.3 %collective-permute-start.6 = (bf16[256,256]{1,0:T(8,128)(2,1)S(1)}, bf16[256,256]{1,0:T(8,128)(2,1)S(1)}, u32[]{:S(2)}, u32[]{:S(2)}) collective-permute-start(bf16[256,256]{1,0:T(8,128)(2,1)S(1)} %shard_map.87), channel_id=1, source_target_pairs={{16,0},{24,8},{32,16},{40,24},{48,32},{56,40},{64,48},{72,56},{80,... | collective-permute-start | bytes 393224 | tf_op jit(solution)/shard_map/ppermute | solution.py:174
  64.3 10.1 %all-to-all-done.1.x = bf16[16,8,128]{2,1,0:T(8,128)(2,1)S(1)} async-done(((bf16[16,8,128]{2,1,0:T(8,128)(2,1)}), bf16[16,8,128]{2,1,0:T(8,128)(2,1)S(1)}, u32[]{:S(2)}, u32[]{:S(2)}) %all-to-all-start.1) | async-done | bytes 32800 | tf_op jit(solution)/shard_map/all_to_all | solution.py:178
  74.4 0.7 shard_map.91
  75.1 5.3 %all-to-all-start.2 = ((bf16[32,8,128]{2,1,0:T(8,128)(2,1)}), bf16[32,8,128]{2,1,0:T(8,128)(2,1)S(1)}, u32[]{:S(2)}, u32[]{:S(2)}) async-start(bf16[32,8,128]{2,1,0:T(8,128)(2,1)} %shard_map.91), calls=%async_computation.2 | async-start | bytes 131072 | tf_op jit(solution)/shard_map/all_to_all | solution.py:178
  80.4 0.0 collective-permute-done.6.got
  80.4 2.5 %collective-permute-start.7 = (bf16[128,384]{1,0:T(8,128)(2,1)S(1)}, bf16[128,384]{1,0:T(8,128)(2,1)S(1)}, u32[]{:S(2)}, u32[]{:S(2)}) collective-permute-start(bf16[128,384]{1,0:T(8,128)(2,1)S(1)} %get-tuple-element.37), channel_id=1, source_target_pairs={{0,8},{8,0},{16,24},{24,16},{32,40},{40,32},{48,56},{56,48},{64,72... | collective-permute-start | bytes 294920 | tf_op jit(solution)/shard_map/ppermute | solution.py:174
  82.9 4.9 %all-to-all-done.2 = bf16[32,8,128]{2,1,0:T(8,128)(2,1)S(1)} async-done(((bf16[32,8,128]{2,1,0:T(8,128)(2,1)}), bf16[32,8,128]{2,1,0:T(8,128)(2,1)S(1)}, u32[]{:S(2)}, u32[]{:S(2)}) %all-to-all-start.2) | async-done | bytes 65568 | tf_op jit(solution)/shard_map/all_to_all | solution.py:178
  87.8 0.7 convert_bitcast_fusion
  88.5 0.0 collective-permute-done.7.got
  88.5 0.7 shard_map.89
  (2 shorter events, 0.1 us)
Async XLA Ops:
  1.6 26.0 %collective-permute-start = (bf16[128,512]{1,0:T(8,128)(2,1)S(1)}, bf16[128,512]{1,0:T(8,128)(2,1)S(1)}, u32[]{:S(2)}, u32[]{:S(2)}) collective-permute-start(bf16[128,512]{1,0:T(8,128)(2,1)S(1)} %get-tuple-element.25), channel_id=1, source_target_pairs={{0,8},{8,0},{16,24},{24,16},{32,40},{40,32},{48,56},{56,48},{64,72... | collective-permute-start | bytes 393224 | tf_op jit(solution)/shard_map/ppermute | solution.py:174
  6.0 10.8 %collective-permute-start.2 = (bf16[128,256]{1,0:T(8,128)(2,1)S(1)}, bf16[128,256]{1,0:T(8,128)(2,1)S(1)}, u32[]{:S(2)}, u32[]{:S(2)}) collective-permute-start(bf16[128,256]{1,0:T(8,128)(2,1)S(1)} %get-tuple-element.26), channel_id=1, source_target_pairs={{0,24},{8,16},{16,40},{24,32},{32,56},{40,48},{48,72},{56,64},{64,... | collective-permute-start | bytes 196616 | tf_op jit(solution)/shard_map/ppermute | solution.py:174
  10.6 11.0 %collective-permute-start.1 = (bf16[128,256]{1,0:T(8,128)(2,1)S(1)}, bf16[128,256]{1,0:T(8,128)(2,1)S(1)}, u32[]{:S(2)}, u32[]{:S(2)}) collective-permute-start(bf16[128,256]{1,0:T(8,128)(2,1)S(1)} %get-tuple-element.23.kv_mine), channel_id=1, source_target_pairs={{0,16},{8,24},{16,32},{24,40},{32,48},{40,56},{48,64},{56,72},{64,... | collective-permute-start | bytes 196616 | tf_op jit(solution)/shard_map/ppermute | solution.py:174
  16.8 12.0 %collective-permute-start.4 = (bf16[128,256]{1,0:T(8,128)(2,1)S(1)}, bf16[128,256]{1,0:T(8,128)(2,1)S(1)}, u32[]{:S(2)}, u32[]{:S(2)}) collective-permute-start(bf16[128,256]{1,0:T(8,128)(2,1)S(1)} %collective-permute-done.2.near_b), channel_id=1, source_target_pairs={{0,16},{8,24},{16,32},{24,40},{32,48},{40,56},{48,64},{56,72},{64,... | collective-permute-start | bytes 196616 | tf_op jit(solution)/shard_map/ppermute | solution.py:174
  21.7 7.2 %collective-permute-start.3 = (bf16[128,256]{1,0:T(8,128)(2,1)S(1)}, bf16[128,256]{1,0:T(8,128)(2,1)S(1)}, u32[]{:S(2)}, u32[]{:S(2)}) collective-permute-start(bf16[128,256]{1,0:T(8,128)(2,1)S(1)} %collective-permute-done.1.near_a), channel_id=1, source_target_pairs={{0,16},{8,24},{16,32},{24,40},{32,48},{40,56},{48,64},{56,72},{64,... | collective-permute-start | bytes 196616 | tf_op jit(solution)/shard_map/ppermute | solution.py:174
  31.7 31.2 %collective-permute-start.5 = (bf16[256,256]{1,0:T(8,128)(2,1)S(1)}, bf16[256,256]{1,0:T(8,128)(2,1)S(1)}, u32[]{:S(2)}, u32[]{:S(2)}) collective-permute-start(bf16[256,256]{1,0:T(8,128)(2,1)S(1)} %get-tuple-element.32), channel_id=1, source_target_pairs={{16,0},{24,8},{32,16},{40,24},{48,32},{56,40},{64,48},{72,56},{80,... | collective-permute-start | bytes 393224 | tf_op jit(solution)/shard_map/ppermute | solution.py:174
  55.0 19.4 %all-to-all-start.1 = ((bf16[16,8,128]{2,1,0:T(8,128)(2,1)}), bf16[16,8,128]{2,1,0:T(8,128)(2,1)S(1)}, u32[]{:S(2)}, u32[]{:S(2)}) async-start(bf16[16,8,128]{2,1,0:T(8,128)(2,1)} %shard_map.90), calls=%async_computation.1 | async-start | bytes 65536 | tf_op jit(solution)/shard_map/all_to_all | solution.py:178
  63.0 17.4 %collective-permute-start.6 = (bf16[256,256]{1,0:T(8,128)(2,1)S(1)}, bf16[256,256]{1,0:T(8,128)(2,1)S(1)}, u32[]{:S(2)}, u32[]{:S(2)}) collective-permute-start(bf16[256,256]{1,0:T(8,128)(2,1)S(1)} %shard_map.87), channel_id=1, source_target_pairs={{16,0},{24,8},{32,16},{40,24},{48,32},{56,40},{64,48},{72,56},{80,... | collective-permute-start | bytes 393224 | tf_op jit(solution)/shard_map/ppermute | solution.py:174
  75.1 12.7 %all-to-all-start.2 = ((bf16[32,8,128]{2,1,0:T(8,128)(2,1)}), bf16[32,8,128]{2,1,0:T(8,128)(2,1)S(1)}, u32[]{:S(2)}, u32[]{:S(2)}) async-start(bf16[32,8,128]{2,1,0:T(8,128)(2,1)} %shard_map.91), calls=%async_computation.2 | async-start | bytes 131072 | tf_op jit(solution)/shard_map/all_to_all | solution.py:178
  80.4 8.0 %collective-permute-start.7 = (bf16[128,384]{1,0:T(8,128)(2,1)S(1)}, bf16[128,384]{1,0:T(8,128)(2,1)S(1)}, u32[]{:S(2)}, u32[]{:S(2)}) collective-permute-start(bf16[128,384]{1,0:T(8,128)(2,1)S(1)} %get-tuple-element.37), channel_id=1, source_target_pairs={{0,8},{8,0},{16,24},{24,16},{32,40},{40,32},{48,56},{56,48},{64,72... | collective-permute-start | bytes 294920 | tf_op jit(solution)/shard_map/ppermute | solution.py:174
